TPU v7x, 32 devices: a whole 2x2x4 slice. The times are simulated.
32 devices in a mesh: dp: 8 (over z, core), seq: 4 (over y, x).
Axes of the slice: x: 2, y: 2, z: 4, core: 2. Of those that a mesh axis runs over, the one named last changes fastest.
Arguments:
- tokens_in: bfloat16 [16384, 1024], P(('dp', 'seq')), may hold values from -6 to 6
- norm_attn: bfloat16 [1024], P('dp'), may hold values from 0.5 to 1.5
- w_query: bfloat16 [1024, 1024], P('dp'), may hold values from -0.1875 to 0.1875
- key_value_weight: bfloat16 [1024, 1024], P('dp'), may hold values from -0.1875 to 0.1875
- gain_query: bfloat16 [64], P('dp'), may hold values from 1 to 2
- gain_key: bfloat16 [64], P('dp'), may hold values from 1 to 2
- w_out: bfloat16 [1024, 1024], P('dp'), may hold values from -0.75 to 0.75
- norm_ffn: bfloat16 [1024], P('dp'), may hold values from 0.5 to 1.5
- w_gate: bfloat16 [1024, 4608], P(None, 'dp'), may hold values from -0.1875 to 0.1875
- w_up: bfloat16 [1024, 4608], P(None, 'dp'), may hold values from -0.1875 to 0.1875
- w_down: bfloat16 [4608, 1024], P('dp'), may hold values from -0.09375 to 0.09375
- cotangent: bfloat16 [16384, 1024], P(('dp', 'seq')), may hold values from -6 to 6
- segments: int32 [8, 2048], P('dp'), may hold values from 0 to 3, never falling along the last dimension, each value on 1 to 1024 neighbouring positions
- blocks: int32 [8, 16], P('dp'), may hold values from 0 to 15, each once within a row
Outputs:
- output: bfloat16 [16384, 1024], P(('dp', 'seq'))
- grad_tokens: float32 [16384, 1024], P(('dp', 'seq'))
- grad_norm_attn: float32 [1024], P('dp')
- grad_w_query: float32 [1024, 1024], P('dp')
- grad_w_keyval: float32 [1024, 1024], P('dp')
- grad_gain_query: float32 [64], P('dp')
- grad_gain_key: float32 [64], P('dp')
- grad_w_out: float32 [1024, 1024], P('dp')
- grad_norm_ffn: float32 [1024], P('dp')
- grad_w_gate: float32 [1024, 4608], P(None, 'dp')
- grad_w_up: float32 [1024, 4608], P(None, 'dp')
- grad_w_down: float32 [4608, 1024], P('dp')
Inputs may be any that keep to these rules, and one draw needn't show every extreme that they name: `segments`: in each row the document numbers never fall, all 4 documents occur, each covers 1 to 1024 places and the longest exactly 1024. `blocks`: each row holds every block number once.
All inputs are finite; a program needn't handle non-finite values.
Results may differ from a plain program's by a relative error of at most 0.025.
Values may be sent and summed in bfloat16 or wider, within the bound.
A program may use at most 192 MiB of HBM per device.

v0:
```python
import math

import jax
import jax.numpy as jnp
from jax import lax
from jax.sharding import PartitionSpec as P

QUERY_HEADS = 16
KEY_VALUE_HEADS = 8
HEAD_SIZE = 64
BLOCK = 128
QUERY_ROWS = 512


EPS = 1e-05
THETA = 1000000.0
MASKED = -1e30


def normed(tensor, gain_vec):
    factor = lax.rsqrt(jnp.mean(tensor * tensor, axis=-1, keepdims=True) + EPS)
    return tensor * factor * gain_vec


def norm_back(tensor, gain_vec, upstream):
    factor = lax.rsqrt(jnp.mean(tensor * tensor, axis=-1, keepdims=True) + EPS)
    unit_value = tensor * factor
    weighted = upstream * gain_vec
    grad_in = factor * (
        weighted - unit_value * jnp.mean(weighted * unit_value, axis=-1, keepdims=True)
    )
    return (grad_in, upstream * unit_value)


def rotate(tensor, angle_cos, angle_sin):
    half_dim = tensor.shape[-1] // 2
    front_half = tensor[..., :half_dim]
    back_half = tensor[..., half_dim:]
    return jnp.concatenate(
        [
            front_half * angle_cos - back_half * angle_sin,
            back_half * angle_cos + front_half * angle_sin,
        ],
        axis=-1,
    )


def angles(offsets, head_dim):
    half_dim = head_dim // 2
    frequency = jnp.exp(
        jnp.arange(half_dim, dtype=jnp.float32) * (-2.0 * math.log(THETA) / head_dim)
    )
    turned = offsets.astype(jnp.float32)[:, None] * frequency[None, :]
    return (jnp.cos(turned)[:, None, :], jnp.sin(turned)[:, None, :])


def layout(segment_row, order_row, block_len):
    length_all = segment_row.shape[0]
    places = jnp.arange(length_all, dtype=jnp.int32)
    seg_start = jnp.concatenate([jnp.ones((1,), dtype=bool), segment_row[1:] != segment_row[:-1]])
    starts = lax.cummax(jnp.where(seg_start, places, 0), axis=0)
    offsets = places - starts
    placed_tokens = (
        order_row[:, None] * block_len + jnp.arange(block_len, dtype=jnp.int32)[None, :]
    ).reshape(length_all)
    return (placed_tokens, segment_row[placed_tokens], offsets[placed_tokens])


def plain_product(left_op, right_op):
    return jnp.dot(left_op, right_op, preferred_element_type=jnp.float32)


def dot_right_t(left_op, right_op):
    return lax.dot_general(
        left_op, right_op, (((1,), (1,)), ((), ())), preferred_element_type=jnp.float32
    )


def dot_left_t(left_op, right_op):
    return lax.dot_general(
        left_op, right_op, (((0,), (0,)), ((), ())), preferred_element_type=jnp.float32
    )


def gate_back(gate_pre, up_pre, upstream):
    gate_sig = jax.nn.sigmoid(gate_pre)
    grad_gate = upstream * up_pre * gate_sig * (1.0 + gate_pre * (1.0 - gate_sig))
    grad_up = upstream * gate_pre * gate_sig
    return (grad_gate.astype(jnp.bfloat16), grad_up.astype(jnp.bfloat16))


def shards(
    tokens_in,
    norm_attn,
    w_query,
    key_value_weight,
    gain_query,
    gain_key,
    w_out,
    norm_ffn,
    w_gate,
    w_up,
    w_down,
    cotangent,
    segments,
    blocks,
):
    sequence_count = lax.axis_size("seq")
    seq_index = lax.axis_index("seq")
    token_rows = tokens_in.shape[0]
    group_rows = token_rows * sequence_count
    local_key_value = KEY_VALUE_HEADS // sequence_count
    repeat_factor = QUERY_HEADS // KEY_VALUE_HEADS
    factor = HEAD_SIZE ** (-0.5)
    count_blocks = group_rows // QUERY_ROWS
    attn_gain, query_w, key_value_matrix, query_gain, key_gain, out_w, ffn_gain = (
        lax.all_gather(norm_attn, "dp", axis=0, tiled=True),
        lax.all_gather(w_query, "dp", axis=0, tiled=True),
        lax.all_gather(key_value_weight, "dp", axis=0, tiled=True),
        lax.all_gather(gain_query, "dp", axis=0, tiled=True),
        lax.all_gather(gain_key, "dp", axis=0, tiled=True),
        lax.all_gather(w_out, "dp", axis=0, tiled=True),
        lax.all_gather(norm_ffn, "dp", axis=0, tiled=True),
    )
    attn_gain = attn_gain.astype(jnp.float32)
    query_gain = query_gain.astype(jnp.float32)
    key_gain = key_gain.astype(jnp.float32)
    ffn_gain = ffn_gain.astype(jnp.float32)
    placed_tokens, documents_for_rows, offsets = layout(segments[0], blocks[0], BLOCK)
    angle_cos, angle_sin = angles(
        lax.dynamic_slice_in_dim(offsets, seq_index * token_rows, token_rows, 0), HEAD_SIZE
    )
    hidden = tokens_in.astype(jnp.float32)
    normalized_input = normed(hidden, attn_gain).astype(jnp.bfloat16)
    query_raw = plain_product(normalized_input, query_w).reshape(token_rows, QUERY_HEADS, HEAD_SIZE)
    key_value_unrotated = plain_product(normalized_input, key_value_matrix).reshape(
        token_rows, KEY_VALUE_HEADS, 2, HEAD_SIZE
    )
    query_low = rotate(normed(query_raw, query_gain), angle_cos, angle_sin).astype(jnp.bfloat16)
    key_low = rotate(normed(key_value_unrotated[:, :, 0], key_gain), angle_cos, angle_sin).astype(
        jnp.bfloat16
    )
    key_value_reduced = jnp.stack(
        [key_low, key_value_unrotated[:, :, 1].astype(jnp.bfloat16)], axis=2
    )
    query_heads, keyval_heads = (
        lax.all_to_all(
            query_low.reshape(token_rows, QUERY_HEADS * HEAD_SIZE),
            "seq",
            split_axis=1,
            concat_axis=0,
            tiled=True,
        ),
        lax.all_to_all(
            key_value_reduced.reshape(token_rows, KEY_VALUE_HEADS * 2 * HEAD_SIZE),
            "seq",
            split_axis=1,
            concat_axis=0,
            tiled=True,
        ),
    )
    query_matrix = query_heads.reshape(group_rows, local_key_value, repeat_factor, HEAD_SIZE)
    keyval_group = keyval_heads.reshape(group_rows, local_key_value, 2, HEAD_SIZE)
    key_rows = keyval_group[:, :, 0]
    value_rows = keyval_group[:, :, 1]

    def scores_of(block_idx):
        row_start = block_idx * QUERY_ROWS
        query_rows = lax.dynamic_slice_in_dim(query_matrix, row_start, QUERY_ROWS, 0)
        placed_rows = lax.dynamic_slice_in_dim(placed_tokens, row_start, QUERY_ROWS, 0)
        docs_rows = lax.dynamic_slice_in_dim(documents_for_rows, row_start, QUERY_ROWS, 0)
        allowed = (docs_rows[:, None] == documents_for_rows[None, :]) & (
            placed_tokens[None, :] <= placed_rows[:, None]
        )
        raw_scores = (
            jnp.einsum("rkad,jkd->karj", query_rows, key_rows, preferred_element_type=jnp.float32)
            * factor
        )
        return (query_rows, jnp.where(allowed, raw_scores, MASKED))

    def forward_block(block_idx):
        query_rows, masked = scores_of(block_idx)
        row_top = jnp.max(masked, axis=-1, keepdims=True)
        row_total = jnp.sum(jnp.exp(masked - row_top), axis=-1, keepdims=True)
        log_total = row_top + jnp.log(row_total)
        weights_low = jnp.exp(masked - log_total).astype(jnp.bfloat16)
        block_result = jnp.einsum(
            "karj,jkd->rkad", weights_low, value_rows, preferred_element_type=jnp.float32
        )
        return (block_result.astype(jnp.bfloat16), log_total)

    head_outs, log_totals = lax.map(forward_block, jnp.arange(count_blocks))
    attended = lax.all_to_all(
        head_outs.reshape(group_rows, local_key_value * repeat_factor * HEAD_SIZE),
        "seq",
        split_axis=0,
        concat_axis=1,
        tiled=True,
    )
    middle = hidden + plain_product(attended, out_w)
    ffn_in = normed(middle, ffn_gain).astype(jnp.bfloat16)
    gate_all, up_all, down_all = (
        lax.all_gather(w_gate, "dp", axis=1, tiled=True),
        lax.all_gather(w_up, "dp", axis=1, tiled=True),
        lax.all_gather(w_down, "dp", axis=0, tiled=True),
    )
    gate_pre = plain_product(ffn_in, gate_all)
    up_pre = plain_product(ffn_in, up_all)
    activated = (jax.nn.silu(gate_pre) * up_pre).astype(jnp.bfloat16)
    ffn_result = plain_product(activated, down_all)
    block_output = (middle + ffn_result).astype(jnp.bfloat16)
    upstream = cotangent.astype(jnp.float32)
    grad_act = dot_right_t(cotangent, down_all)
    grad_down_part = dot_left_t(activated, cotangent)
    grad_gate, grad_up = gate_back(gate_pre, up_pre, grad_act)
    grad_gate_part = dot_left_t(ffn_in, grad_gate)
    grad_up_part = dot_left_t(ffn_in, grad_up)
    grad_ffn_in = dot_right_t(grad_gate, gate_all) + dot_right_t(grad_up, up_all)
    grad_gate_w, grad_up_w, grad_down = (
        lax.psum_scatter(
            grad_gate_part.astype(jnp.bfloat16), "dp", scatter_dimension=1, tiled=True
        ).astype(jnp.float32),
        lax.psum_scatter(
            grad_up_part.astype(jnp.bfloat16), "dp", scatter_dimension=1, tiled=True
        ).astype(jnp.float32),
        lax.psum_scatter(
            grad_down_part.astype(jnp.bfloat16), "dp", scatter_dimension=0, tiled=True
        ).astype(jnp.float32),
    )
    grad_middle_add, ffn_gain_terms = norm_back(middle, ffn_gain, grad_ffn_in)
    grad_ffn_gain = jnp.sum(ffn_gain_terms, axis=0)
    grad_middle = upstream + grad_middle_add
    grad_branch = grad_middle.astype(jnp.bfloat16)
    grad_out_w = dot_left_t(attended, grad_branch)
    grad_attended = dot_right_t(grad_branch, out_w).astype(jnp.bfloat16)
    grad_head_outs = lax.all_to_all(grad_attended, "seq", split_axis=1, concat_axis=0, tiled=True)
    grad_outs_all = grad_head_outs.reshape(group_rows, local_key_value, repeat_factor, HEAD_SIZE)

    def backward_block(carried, group_members):
        grad_keys, grad_values = carried
        block_idx, log_total = group_members
        query_rows, masked = scores_of(block_idx)
        weights_full = jnp.exp(masked - log_total)
        weights_low = weights_full.astype(jnp.bfloat16)
        grad_rows = lax.dynamic_slice_in_dim(grad_outs_all, block_idx * QUERY_ROWS, QUERY_ROWS, 0)
        grad_weights = jnp.einsum(
            "rkad,jkd->karj", grad_rows, value_rows, preferred_element_type=jnp.float32
        )
        row_dot = jnp.sum(weights_full * grad_weights, axis=-1, keepdims=True)
        grad_scores = (weights_full * (grad_weights - row_dot)).astype(jnp.bfloat16)
        grad_query_rows = (
            jnp.einsum("karj,jkd->rkad", grad_scores, key_rows, preferred_element_type=jnp.float32)
            * factor
        )
        grad_keys = (
            grad_keys
            + jnp.einsum(
                "karj,rkad->jkd", grad_scores, query_rows, preferred_element_type=jnp.float32
            )
            * factor
        )
        grad_values = grad_values + jnp.einsum(
            "karj,rkad->jkd", weights_low, grad_rows, preferred_element_type=jnp.float32
        )
        return ((grad_keys, grad_values), grad_query_rows.astype(jnp.bfloat16))

    zero_heads = jnp.zeros((group_rows, local_key_value, HEAD_SIZE), jnp.float32)
    (grad_keys, grad_values), grad_query_blocks = lax.scan(
        backward_block, (zero_heads, zero_heads), (jnp.arange(count_blocks), log_totals)
    )
    grad_query_heads = grad_query_blocks.reshape(
        group_rows, local_key_value * repeat_factor * HEAD_SIZE
    )
    grad_keyval_heads = (
        jnp.stack([grad_keys, grad_values], axis=2)
        .astype(jnp.bfloat16)
        .reshape(group_rows, local_key_value * 2 * HEAD_SIZE)
    )
    grad_query_tok, key_value_gradient_tokens = (
        lax.all_to_all(grad_query_heads, "seq", split_axis=0, concat_axis=1, tiled=True),
        lax.all_to_all(grad_keyval_heads, "seq", split_axis=0, concat_axis=1, tiled=True),
    )
    grad_query_rot = rotate(
        grad_query_tok.reshape(token_rows, QUERY_HEADS, HEAD_SIZE).astype(jnp.float32),
        angle_cos,
        -angle_sin,
    )
    grad_query_raw, query_gain_terms = norm_back(query_raw, query_gain, grad_query_rot)
    grad_query_gain = jnp.sum(query_gain_terms, axis=(0, 1))
    key_value_gradient_split = key_value_gradient_tokens.reshape(
        token_rows, KEY_VALUE_HEADS, 2, HEAD_SIZE
    )
    grad_key_rot = rotate(
        key_value_gradient_split[:, :, 0].astype(jnp.float32), angle_cos, -angle_sin
    )
    grad_key_raw, key_gain_terms = norm_back(key_value_unrotated[:, :, 0], key_gain, grad_key_rot)
    grad_key_gain = jnp.sum(key_gain_terms, axis=(0, 1))
    grad_query_low = grad_query_raw.astype(jnp.bfloat16).reshape(
        token_rows, QUERY_HEADS * HEAD_SIZE
    )
    grad_keyval_low = jnp.stack(
        [grad_key_raw.astype(jnp.bfloat16), key_value_gradient_split[:, :, 1]], axis=2
    ).reshape(token_rows, KEY_VALUE_HEADS * 2 * HEAD_SIZE)
    grad_normed_in = dot_right_t(grad_query_low, query_w) + dot_right_t(
        grad_keyval_low, key_value_matrix
    )
    grad_query_w = dot_left_t(normalized_input, grad_query_low)
    grad_keyval_w = dot_left_t(normalized_input, grad_keyval_low)
    grad_hidden_add, attn_gain_terms = norm_back(hidden, attn_gain, grad_normed_in)
    grad_attn_gain = jnp.sum(attn_gain_terms, axis=0)
    grad_hidden = grad_middle + grad_hidden_add
    (
        owned_attn_gain,
        owned_query_w,
        owned_keyval_w,
        owned_query_gain,
        owned_key_gain,
        owned_out_w,
        owned_ffn_gain,
    ) = (
        lax.psum_scatter(
            grad_attn_gain.astype(jnp.bfloat16), "dp", scatter_dimension=0, tiled=True
        ).astype(jnp.float32),
        lax.psum_scatter(
            grad_query_w.astype(jnp.bfloat16), "dp", scatter_dimension=0, tiled=True
        ).astype(jnp.float32),
        lax.psum_scatter(
            grad_keyval_w.astype(jnp.bfloat16), "dp", scatter_dimension=0, tiled=True
        ).astype(jnp.float32),
        lax.psum_scatter(
            grad_query_gain.astype(jnp.bfloat16), "dp", scatter_dimension=0, tiled=True
        ).astype(jnp.float32),
        lax.psum_scatter(
            grad_key_gain.astype(jnp.bfloat16), "dp", scatter_dimension=0, tiled=True
        ).astype(jnp.float32),
        lax.psum_scatter(
            grad_out_w.astype(jnp.bfloat16), "dp", scatter_dimension=0, tiled=True
        ).astype(jnp.float32),
        lax.psum_scatter(
            grad_ffn_gain.astype(jnp.bfloat16), "dp", scatter_dimension=0, tiled=True
        ).astype(jnp.float32),
    )
    (
        total_attn_gain,
        total_query_w,
        total_keyval_w,
        total_query_gain,
        total_key_gain,
        total_out_w,
        total_ffn_gain,
        total_gate_w,
        total_up_w,
        total_down_w,
    ) = lax.psum(
        (
            owned_attn_gain,
            owned_query_w,
            owned_keyval_w,
            owned_query_gain,
            owned_key_gain,
            owned_out_w,
            owned_ffn_gain,
            grad_gate_w,
            grad_up_w,
            grad_down,
        ),
        "seq",
    )
    return (
        block_output,
        grad_hidden,
        total_attn_gain,
        total_query_w,
        total_keyval_w,
        total_query_gain,
        total_key_gain,
        total_out_w,
        total_ffn_gain,
        total_gate_w,
        total_up_w,
        total_down_w,
    )


def solution(mesh):
    return jax.shard_map(
        shards,
        mesh=mesh,
        in_specs=(
            P(("dp", "seq"), None),
            P("dp"),
            P("dp", None),
            P("dp", None),
            P("dp"),
            P("dp"),
            P("dp", None),
            P("dp"),
            P(None, "dp"),
            P(None, "dp"),
            P("dp", None),
            P(("dp", "seq"), None),
            P("dp", None),
            P("dp", None),
        ),
        out_specs=(
            P(("dp", "seq"), None),
            P(("dp", "seq"), None),
            P("dp"),
            P("dp", None),
            P("dp", None),
            P("dp"),
            P("dp"),
            P("dp", None),
            P("dp"),
            P(None, "dp"),
            P(None, "dp"),
            P("dp", None),
        ),
        check_vma=False,
    )
```

profile of v0, /device:TPU:0, one launch (start us, length us, event | category | flops | bytes accessed | tf_op | source)
XLA Modules:
  0.0 1336.3 jit_solution(3187364560856251971)
XLA Ops:
  11.2 13.5 %all-gather = bf16[8,1,128]{2,1,0:T(2,128)(2,1)S(1)} all-gather(bf16[1,1,128]{2,1,0:T(2,128)(2,1)S(1)} %bitcast.328), channel_id=1, replica_groups=mesh['dp'=8,'seq'=4] {'dp'}, dimensions={0}, use_global_device_ids=true | all-gather | bytes 2304 | tf_op jit(solution)/shard_map/all_gather | solution.py:117
  26.5 14.3 %all-reduce.8 = (bf16[64]{0:T(256)(128)(2,1)S(1)}, bf16[64]{0:T(256)(128)(2,1)S(1)}) all-reduce(bf16[64]{0:T(256)(128)(2,1)S(1)} %dynamic-update-slice, bf16[64]{0:T(256)(128)(2,1)S(1)} %dynamic-update-slice.1), channel_id=1, replica_groups=mesh['dp'=8,'seq'=4] {'dp'}, use_global_device_ids=true, to_apply=%add | all-reduce | flops 128 | bytes 512
  41.5 11.8 gather_fusion.1
  84.8 11.8 gather_fusion
  106.9 61.7 %while.28 = (s32[]{:T(128)}, bf16[4,512,2,2,64]{1,4,3,2,0:T(8,128)(2,1)}, f32[4,2,2,512,1]{3,2,1,4,0:T(2,128)}, s32[4]{0:T(128)S(1)}, s32[2048]{0:T(1024)S(1)}, ...) while((s32[]{:T(128)}, ...), condition=%wide.region_8.9_spmd.clone, body=%wide.region_5.8_spmd.clone.sunk | while | flops 1123155968 | bytes 56201496 | solution.py:192
  204.5 80.3 %all-gather.17.cloned.1.call-done = bf16[1024,4608]{0,1:T(8,128)(2,1)} async-done(((bf16[1024,576]{0,1:T(8,128)(2,1)}), bf16[1024,4608]{0,1:T(8,128)(2,1)}) %all-gather.17.cloned.1.call-update) | async-done | bytes 9437200 | tf_op jit(solution)/shard_map/all_gather | solution.py:204
  295.2 80.3 %all-gather.19.cloned.1.call-done = bf16[4608,1024]{1,0:T(8,128)(2,1)} async-done(((bf16[576,1024]{1,0:T(8,128)(2,1)}), bf16[4608,1024]{1,0:T(8,128)(2,1)}) %all-gather.19.cloned.1.call-update) | async-done | bytes 9437200 | tf_op jit(solution)/shard_map/all_gather | solution.py:205
  375.5 18.5 %multiply_convert_fusion = (bf16[512,4608]{1,0:T(8,128)(2,1)}, bf16[512,4608]{1,0:T(8,128)(2,1)}, bf16[512,4608]{1,0:T(8,128)(2,1)}) fusion(f32[512,4608]{1,0:T(8,128)} %fusion.93, f32[512,4608]{1,0:T(8,128)} %fusion.94, bf16[512,1024]{1,0:T(8,128)(2,1)} %param.29, bf16[4608,1024]{1,0:T(8,128)(2,1)} %all-gather.19.cloned.1.call-done), kind=kOutput, calls=%fused_computation.69 | convolution fusion | flops 4869586944 | bytes 43515904 | tf_op jit(solution)/shard_map/dot_general | solution.py:74
  438.7 199.1 %while.29 = (s32[]{:T(128)}, f32[2048,2,64]{0,2,1:T(8,128)}, f32[2048,2,64]{0,2,1:T(8,128)}, bf16[4,512,2,2,64]{1,4,3,2,0:T(8,128)(2,1)}, s32[4]{0:T(128)S(1)}, ...) while((s32[]{:T(128)}, f32[2048,2,64]{0,2,1:T(8,128)}, ...), condition=%wide.region_13.14_spmd.clone, body=%wide.region_11.13_spmd.clone.sunk | while | flops 2751987712 | bytes 254768080 | solution.py:268
  446.4 11.6 fusion.160
  457.9 10.9 fusion.161
  495.9 11.5 fusion.160
  507.4 10.9 fusion.161
  545.6 11.5 fusion.160
  557.1 10.9 fusion.161
  595.3 11.5 fusion.160
  606.9 10.9 fusion.161
  643.6 11.2 all-to-all-done.4
  672.6 16.0 %all_to_all.90 = bf16[4,512,256]{1,2,0:T(8,128)(2,1)S(1)} all-to-all(bf16[4,512,256]{1,2,0:T(8,128)(2,1)S(1)} %copy.108), channel_id=1, replica_groups=mesh['dp'=8,'seq'=4] {'seq'}, dimensions={0} | all-to-all | bytes 2097152 | tf_op jit(solution)/shard_map/all_to_all | solution.py:281
  745.7 14.4 %all-reduce.7 = (bf16[1024]{0:T(1024)(128)(2,1)S(1)}, bf16[64]{0:T(256)(128)(2,1)S(1)}, bf16[64]{0:T(256)(128)(2,1)S(1)}, bf16[1024]{0:T(1024)(128)(2,1)S(1)}) all-reduce(bf16[1024]{0:T(1024)(128)(2,1)S(1)} %get-tuple-element.224, bf16[64]{0:T(256)(128)(2,1)S(1)} %reduce_sum.160, ...), channel_id=2, replica_groups=mesh['dp'=8,'seq'=4] {'dp'}, use_global_device_ids=true, to_apply=%region_18.19.clone | all-reduce | flops 2176 | bytes 8704
  763.9 77.2 %reduce-scatter.13.cloned.1.call-done = bf16[1024,576]{0,1:T(8,128)(2,1)} async-done(((bf16[1024,4608]{0,1:T(8,128)(2,1)}), bf16[1024,576]{0,1:T(8,128)(2,1)}) %reduce-scatter.13.cloned.1.call-update) | async-done | bytes 1179664 | tf_op jit(solution)/shard_map/reduce_scatter | solution.py:220
  841.0 99.9 %reduce-scatter.15.cloned.1.call-done = bf16[1024,576]{0,1:T(8,128)(2,1)} async-done(((bf16[1024,4608]{0,1:T(8,128)(2,1)}), bf16[1024,576]{0,1:T(8,128)(2,1)}) %reduce-scatter.15.cloned.1.call-update) | async-done | bytes 1179664 | tf_op jit(solution)/shard_map/reduce_scatter | solution.py:223
  941.0 100.1 %reduce-scatter.17.cloned.1.call-done = bf16[576,1024]{1,0:T(8,128)(2,1)} async-done(((bf16[4608,1024]{1,0:T(8,128)(2,1)}), bf16[576,1024]{1,0:T(8,128)(2,1)}) %reduce-scatter.17.cloned.1.call-update) | async-done | bytes 1179664 | tf_op jit(solution)/shard_map/reduce_scatter | solution.py:226
  1041.0 288.0 %all-reduce.10 = (f32[128]{0:T(128)}, f32[128,1024]{1,0:T(8,128)}, f32[128,1024]{1,0:T(8,128)}, f32[8]{0:T(128)}, f32[8]{0:T(128)}, /*index=5*/f32[128,1024]{1,0...) all-reduce(f32[128]{0:T(128)S(1)} %dynamic-slice_convert_fusion.4, ...), channel_id=1, replica_groups=mesh['dp'=8,'seq'=4] {'seq'}, use_global_device_ids=true, to_apply=%region_19.20 | all-reduce | flops 2162960 | bytes 12978304 | tf_op jit(solution)/shard_map/psum | solution.py:354
  (456 shorter events, 385.1 us)
Async XLA Ops:
  7.2 18.8 %copy-start.56 = (bf16[8]{0:T(256)(128)(2,1)S(1)}, bf16[8]{0:T(256)(128)(2,1)}, u32[]{:S(2)}) copy-start(bf16[8]{0:T(256)(128)(2,1)} %param.22) | copy-start | bytes 52
  7.2 19.0 %copy-start.57 = (bf16[8]{0:T(256)(128)(2,1)S(1)}, bf16[8]{0:T(256)(128)(2,1)}, u32[]{:S(2)}) copy-start(bf16[8]{0:T(256)(128)(2,1)} %param.23) | copy-start | bytes 52
  7.2 34.1 %copy-start.58 = (s32[1,16]{1,0:T(1,128)S(1)}, s32[1,16]{1,0:T(1,128)}, u32[]{:S(2)}) copy-start(s32[1,16]{1,0:T(1,128)} %param.31) | copy-start | bytes 196
  7.2 47.4 %all-gather.9.cloned.1.call-start = ((), (), s32[]{:S(2)}) async-start(), calls=%async_computation.12 | async-start | bytes 2359296 | tf_op jit(solution)/shard_map/all_gather | solution.py:118
  8.0 64.1 %all-gather.11.cloned.1.call-start = ((), (), s32[]{:S(2)}) async-start(), calls=%async_computation.13 | async-start | bytes 2359296 | tf_op jit(solution)/shard_map/all_gather | solution.py:119
  8.7 173.8 %all-gather.13.cloned.1.call-start = ((), (), s32[]{:S(2)}) async-start(), calls=%async_computation.14 | async-start | bytes 2359296 | tf_op jit(solution)/shard_map/all_gather | solution.py:122
  9.5 184.6 %all-gather.15.cloned.1.call-start = ((), (), s32[]{:S(2)}) async-start(), calls=%async_computation.15 | async-start | bytes 10616832 | tf_op jit(solution)/shard_map/all_gather | solution.py:203
  10.0 274.7 %all-gather.17.cloned.1.call-start = ((), (), s32[]{:S(2)}) async-start(), calls=%async_computation.16 | async-start | bytes 10616832 | tf_op jit(solution)/shard_map/all_gather | solution.py:204
  24.7 47.3 %copy-start.40 = (f32[8,1,128]{2,1,0:T(1,128)}, f32[8,1,128]{2,1,0:T(1,128)S(1)}, u32[]{:S(2)}) copy-start(f32[8,1,128]{2,1,0:T(1,128)S(1)} %convert_element_type.218) | copy-start | bytes 12292
  40.8 20.4 %copy-start.46 = (f32[64]{0:T(128)}, f32[64]{0:T(128)S(1)}, u32[]{:S(2)}) copy-start(f32[64]{0:T(128)S(1)} %convert_element_type.174) | copy-start | bytes 772
  40.8 34.5 %copy-start.44 = (f32[64]{0:T(128)}, f32[64]{0:T(128)S(1)}, u32[]{:S(2)}) copy-start(f32[64]{0:T(128)S(1)} %convert_element_type.177) | copy-start | bytes 772
  54.6 21.8 %copy-start.21 = (f32[512,32]{0,1:T(8,128)}, f32[512,32]{0,1:T(8,128)S(1)}, u32[]{:S(2)}) copy-start(f32[512,32]{0,1:T(8,128)S(1)} %get-tuple-element.315) | copy-start | bytes 196612
  63.6 17.1 %all-to-all-start = ((bf16[512,4,256]{0,2,1:T(8,128)(2,1)}), bf16[512,4,256]{0,2,1:T(8,128)(2,1)S(1)}, u32[]{:S(2)}, u32[]{:S(2)}) async-start(bf16[512,4,256]{0,2,1:T(8,128)(2,1)} %bitcast.11), calls=%async_computation | async-start | bytes 2097152 | tf_op jit(solution)/shard_map/all_to_all | solution.py:147
  80.7 19.5 %all-to-all-start.1 = ((bf16[512,4,256]{0,2,1:T(8,128)(2,1)}), bf16[512,4,256]{0,2,1:T(8,128)(2,1)S(1)}, u32[]{:S(2)}, u32[]{:S(2)}) async-start(bf16[512,4,256]{0,2,1:T(8,128)(2,1)} %bitcast.17), calls=%async_computation.1 | async-start | bytes 2097152 | tf_op jit(solution)/shard_map/all_to_all | solution.py:154
  84.2 291.3 %all-gather.19.cloned.1.call-start = ((), (), s32[]{:S(2)}) async-start(), calls=%async_computation.17 | async-start | bytes 10616832 | tf_op jit(solution)/shard_map/all_gather | solution.py:205
  168.6 17.5 %all-to-all-start.2 = ((bf16[4,512,256]{1,2,0:T(8,128)(2,1)}), bf16[4,512,256]{1,2,0:T(8,128)(2,1)}, u32[]{:S(2)}, u32[]{:S(2)}) async-start(bf16[4,512,256]{1,2,0:T(8,128)(2,1)} %bitcast.312), calls=%async_computation.2 | async-start | bytes 2097152 | tf_op jit(solution)/shard_map/all_to_all | solution.py:193
  413.6 18.6 %all-to-all-start.3 = ((bf16[512,4,256]{2,0,1:T(8,128)(2,1)}), bf16[512,4,256]{2,0,1:T(8,128)(2,1)}, u32[]{:S(2)}, u32[]{:S(2)}) async-start(bf16[512,4,256]{2,0,1:T(8,128)(2,1)} %bitcast.310), calls=%async_computation.3 | async-start | bytes 2097152 | tf_op jit(solution)/shard_map/all_to_all | solution.py:236
  417.9 346.0 %reduce-scatter.11.cloned.1.call-start = ((), (), s32[]{:S(2)}) async-start(), calls=%async_computation.20 | async-start | bytes 2359296 | tf_op jit(solution)/shard_map/reduce_scatter | solution.py:336
  637.8 17.1 %all-to-all-start.4 = ((bf16[4,512,256]{1,2,0:T(8,128)(2,1)}), bf16[4,512,256]{1,2,0:T(8,128)(2,1)S(1)}, u32[]{:S(2)}, u32[]{:S(2)}) async-start(bf16[4,512,256]{1,2,0:T(8,128)(2,1)} %bitcast.311), calls=%async_computation.4 | async-start | bytes 2097152 | tf_op jit(solution)/shard_map/all_to_all | solution.py:280
  641.4 122.4 %reduce-scatter.7.cloned.1.call-start = ((), (), s32[]{:S(2)}) async-start(), calls=%async_computation.18 | async-start | bytes 2359296 | tf_op jit(solution)/shard_map/reduce_scatter | solution.py:324
  669.8 94.1 %reduce-scatter.9.cloned.1.call-start = ((), (), s32[]{:S(2)}) async-start(), calls=%async_computation.19 | async-start | bytes 2359296 | tf_op jit(solution)/shard_map/reduce_scatter | solution.py:327
  695.0 146.0 %reduce-scatter.13.cloned.1.call-start = ((), (), s32[]{:S(2)}) async-start(), calls=%async_computation.21 | async-start | bytes 10616832 | tf_op jit(solution)/shard_map/reduce_scatter | solution.py:220
  706.3 234.7 %reduce-scatter.15.cloned.1.call-start = ((), (), s32[]{:S(2)}) async-start(), calls=%async_computation.22 | async-start | bytes 10616832 | tf_op jit(solution)/shard_map/reduce_scatter | solution.py:223
  716.5 324.5 %reduce-scatter.17.cloned.1.call-start = ((), (), s32[]{:S(2)}) async-start(), calls=%async_computation.23 | async-start | bytes 10616832 | tf_op jit(solution)/shard_map/reduce_scatter | solution.py:226
  (108 other events, 602.5 us)
Sparse Core Ops, SparseCore 0:
  9.7 32.0 all-gather.8
  43.4 28.6 all-gather.10
  73.7 28.5 all-gather.12
  103.8 90.2 all-gather.14
  195.6 89.1 all-gather.16
  286.3 89.1 all-gather.18
  422.6 34.6 reduce-scatter.10
  669.9 33.2 reduce-scatter.6
  705.5 34.6 reduce-scatter.8
  742.3 98.6 reduce-scatter.12
  843.3 97.5 reduce-scatter.14
  943.1 97.8 reduce-scatter.16
where the time goes:
time: 1350 us; the launch traced here: 1340 us
  waiting for transfers between devices  476 us (35%)
  blocking collectives  356 us (26%)
  matrix products  293 us (22%)
  other arithmetic  94.1 us (7%)
  local copies, waits for them, and re-layouts  73.3 us (5%)
  starting transfers between devices  20.2 us (1%)
  between operations  17.5 us (1%)
    psum x1, blocking collectives, shards(): lax.psum((owned_attn_gain, owned_query_w, owned_keyval_w, owned_query_gai...  288 us
    reduce_scatter x1, waiting for transfers between devices, shards(): lax.psum_scatter(grad_down_part.astype(jnp.bfloat16), 'dp', scatter_dimen...  100 us
    reduce_scatter x1, waiting for transfers between devices, shards(): lax.psum_scatter(grad_up_part.astype(jnp.bfloat16), 'dp', scatter_dimensi...  99.9 us
    all_gather x1, waiting for transfers between devices, shards(): lax.all_gather(w_down, 'dp', axis=0, tiled=True)  80.3 us
    all_gather x1, waiting for transfers between devices, shards(): lax.all_gather(w_up, 'dp', axis=1, tiled=True)  80.3 us
    reduce_scatter x1, waiting for transfers between devices, shards(): lax.psum_scatter(grad_gate_part.astype(jnp.bfloat16), 'dp', scatter_dimen...  77.2 us
    dot_general x4, matrix products, backward_block(): jnp.einsum('rkad,jkd->karj', grad_rows, value_rows, preferred_element_typ...  46.1 us
    convert_element_type x4, other arithmetic, backward_block(): grad_scores = (weights_full * (grad_weights - row_dot)).astype(jnp.bfloat16)  43.6 us
  transfers between devices with their start and end apart: 17, of which 11 were waited for; matrix products, arithmetic and copies ran while one was open for 31% of the time, Pallas kernels for 0%

commit v1 on v0

v1 whole, which is shorter than its diff:
```python
import functools
import math

import jax
import jax.numpy as jnp
from jax import lax
from jax.experimental import pallas as pl
from jax.experimental.pallas import tpu as pltpu
from jax.sharding import PartitionSpec as P

KEY_VALUE_HEADS = 8
HEAD = 64
PAIR = 2 * HEAD
BLOCK = 128
SPAN = 256
EPS = 1e-05
THETA = 1000000.0
MOST_DOCS = 8
F32 = jnp.float32
BF16 = jnp.bfloat16
VMEM = pltpu.VMEM
LIMIT = 66000000


def nn(a, b):
    return lax.dot_general(a, b, (((1,), (0,)), ((), ())), preferred_element_type=F32)


def nt(a, b):
    return lax.dot_general(a, b, (((1,), (1,)), ((), ())), preferred_element_type=F32)


def tn(a, b):
    return lax.dot_general(a, b, (((0,), (0,)), ((), ())), preferred_element_type=F32)


def split_dot(a, b):
    high = a.astype(BF16)
    low = (a - high.astype(F32)).astype(BF16)
    return nn(high, b) + nn(low, b)


def lanes(shape):
    return lax.broadcasted_iota(jnp.int32, shape, len(shape) - 1)


def head_mean(wide):
    row = lax.broadcasted_iota(jnp.int32, (wide, wide), 0) // HEAD
    col = lax.broadcasted_iota(jnp.int32, (wide, wide), 1) // HEAD
    return jnp.where(row == col, 1.0 / HEAD, 0.0).astype(BF16)


def partner(u):
    wide, half = u.shape[-1], HEAD // 2
    front = lanes(u.shape) % HEAD < half
    return jnp.where(front, pltpu.roll(u, wide - half, 1), pltpu.roll(u, half, 1))


def swap_heads(u):
    return pltpu.roll(u, HEAD, 1)


def tile_lanes(u, times):
    return u if times == 1 else jnp.concatenate([u] * times, axis=1)


def attend_kernel(groups, inv, first, q_raw, kv_raw, cos, sin, starts, gain_q, gain_kv,
                  o_ref, qs, kvs, linv, ov):
    blocks = inv.shape[0]
    wide = q_raw.shape[1]
    mean = head_mean(wide)
    low_half = lanes((BLOCK, PAIR)) < HEAD
    is_key = lanes((BLOCK, wide)) % PAIR < HEAD

    def prepare(p, _):
        rows = pl.ds(pl.multiple_of(inv[p] * BLOCK, BLOCK), BLOCK)
        place = pl.ds(pl.multiple_of(p * BLOCK, BLOCK), BLOCK)
        c = tile_lanes(cos[place, :], groups)
        s = tile_lanes(sin[place, :], groups)

        def turned(raw, gain):
            u = raw * lax.rsqrt(split_dot(raw * raw, mean) + EPS) * gain
            return u * c + partner(u) * s

        q = turned(q_raw[rows, :], gain_q[...]) * (HEAD ** -0.5)
        kv = kv_raw[rows, :]
        kv = jnp.where(is_key, turned(kv, gain_kv[...]), kv)
        for g in range(groups):
            pair = q[:, g * PAIR:(g + 1) * PAIR]
            qs[g, pl.ds(pl.multiple_of(p * SPAN, SPAN), BLOCK), :] = jnp.where(low_half, pair, 0.0).astype(BF16)
            qs[g, pl.ds(pl.multiple_of(p * SPAN + BLOCK, BLOCK), BLOCK), :] = jnp.where(
                low_half, swap_heads(pair), 0.0).astype(BF16)
            one = kv[:, g * PAIR:(g + 1) * PAIR]
            kvs[g, place, :] = one.astype(BF16)
            ov[g, place, :] = jnp.where(low_half, 1.0, one).astype(BF16)
        return 0

    lax.fori_loop(0, blocks, prepare, 0)
    for g in range(groups):
        kvs[g, blocks * BLOCK:, :] = jnp.zeros((BLOCK, PAIR), BF16)
        ov[g, blocks * BLOCK:, :] = jnp.zeros((BLOCK, PAIR), BF16)

    def one_block(p, _):
        base = p * BLOCK
        row = base + lax.broadcasted_iota(jnp.int32, (BLOCK, SPAN), 0)
        start = tile_lanes(starts[pl.ds(pl.multiple_of(base, BLOCK), BLOCK), :], SPAN // BLOCK)
        begin = first[p]

        def step(i, totals):
            at = pl.multiple_of((begin + 2 * i) * BLOCK, BLOCK)
            col = at + lanes((BLOCK, SPAN))
            allowed = (col >= start) & (col <= row)
            keys = pl.ds(at, SPAN)
            result = []
            for g in range(groups):
                score = nt(qs[g, pl.ds(pl.multiple_of(p * SPAN, SPAN), SPAN), :], kvs[g, keys, :])
                e = jnp.exp(score)
                e = jnp.concatenate([jnp.where(allowed, e[:BLOCK], 0.0), jnp.where(allowed, e[BLOCK:], 0.0)], axis=0)
                result.append(totals[g] + nn(e.astype(BF16), ov[g, keys, :]))
            return tuple(result)

        totals = lax.fori_loop(
            0, (p - begin) // 2 + 1, step, tuple(jnp.zeros((SPAN, PAIR), F32) for _ in range(groups)))
        rows = pl.ds(pl.multiple_of(inv[p] * BLOCK, BLOCK), BLOCK)
        for g in range(groups):
            total = totals[g]
            linv[g, p, :, :] = 1.0 / jnp.transpose(total)[0:8, :]
            one, two = total[:BLOCK], total[BLOCK:]
            o = jnp.where(low_half, swap_heads(one) / one, two / swap_heads(two))
            o_ref[rows, g * PAIR:(g + 1) * PAIR] = o.astype(BF16)
        return 0

    lax.fori_loop(0, blocks, one_block, 0)


def attend(inv, first, q_raw, kv_raw, cos, sin, starts, gain_q, gain_kv):
    rows, wide = q_raw.shape
    groups = wide // PAIR
    blocks = rows // BLOCK
    whole = pl.BlockSpec(memory_space=VMEM)
    return pl.pallas_call(
        functools.partial(attend_kernel, groups),
        out_shape=(
            jax.ShapeDtypeStruct((rows, wide), BF16),
            jax.ShapeDtypeStruct((groups, rows * 2, PAIR), BF16),
            jax.ShapeDtypeStruct((groups, rows + BLOCK, PAIR), BF16),
            jax.ShapeDtypeStruct((groups, blocks, 8, SPAN), F32),
        ),
        in_specs=[pl.BlockSpec(memory_space=pltpu.SMEM)] * 2 + [whole] * 7,
        out_specs=(whole,) * 4,
        scratch_shapes=[VMEM((groups, rows + BLOCK, PAIR), BF16)],
        compiler_params=pltpu.CompilerParams(vmem_limit_bytes=LIMIT),
        name="attend",
    )(inv, first, q_raw, kv_raw, cos, sin, starts, gain_q, gain_kv)


def attend_back_kernel(groups, inv, first, q_raw, kv_raw, cos, sin, starts, gain_q, gain_kv, o_ref, do_ref,
                       qs, kvs, linv, dq_ref, dkv_ref, gains_ref, kt, dkv, dq):
    blocks = inv.shape[0]
    wide = q_raw.shape[1]
    mean = head_mean(wide)
    low_half = lanes((BLOCK, PAIR)) < HEAD
    is_key = lanes((BLOCK, wide)) % PAIR < HEAD
    pick = (lax.broadcasted_iota(jnp.int32, (16, PAIR), 1) // HEAD
            == lax.broadcasted_iota(jnp.int32, (16, PAIR), 0) // 8).astype(BF16)

    dkv[...] = jnp.zeros_like(dkv)

    def turn_keys(p, _):
        place = pl.ds(pl.multiple_of(p * BLOCK, BLOCK), BLOCK)
        for g in range(groups):
            kt[g, :, place] = jnp.transpose(kvs[g, place, :].astype(F32))[:HEAD].astype(BF16)
        return 0

    lax.fori_loop(0, blocks, turn_keys, 0)
    for g in range(groups):
        kt[g, :, blocks * BLOCK:] = jnp.zeros((HEAD, BLOCK), BF16)

    def one_block(p, _):
        base = p * BLOCK
        rows = pl.ds(pl.multiple_of(inv[p] * BLOCK, BLOCK), BLOCK)
        queries = pl.ds(pl.multiple_of(p * SPAN, SPAN), SPAN)
        place_q = base + lanes((SPAN, SPAN)) % BLOCK
        start = jnp.broadcast_to(tile_lanes(starts[p, 0:1, :], 2), (SPAN, SPAN))
        begin = first[p]
        grads, dots = [], []
        for g in range(groups):
            pair = do_ref[rows, g * PAIR:(g + 1) * PAIR].astype(F32)
            grads.append(jnp.concatenate(
                [jnp.where(low_half, 0.0, swap_heads(pair)), jnp.where(low_half, 0.0, pair)], axis=0).astype(BF16))
            prod = pair * o_ref[rows, g * PAIR:(g + 1) * PAIR].astype(F32)
            high = prod.astype(BF16)
            low = (prod - high.astype(F32)).astype(BF16)
            d = nt(pick, high) + nt(pick, low)
            dots.append(jnp.concatenate([d[0:1], d[8:9]], axis=1))

        def step(i, totals):
            at = pl.multiple_of((begin + 2 * i) * BLOCK, BLOCK)
            keys = pl.ds(at, SPAN)
            place_k = at + lax.broadcasted_iota(jnp.int32, (SPAN, SPAN), 0)
            allowed = (place_k >= start) & (place_k <= place_q)
            result = []
            for g in range(groups):
                q = qs[g, queries, :]
                kv = kvs[g, keys, :]
                p_t = jnp.where(allowed, jnp.exp(nt(kv, q)) * linv[g, p, 0:1, :], 0.0)
                ds_t = (p_t * (nt(kv, grads[g]) - dots[g])).astype(BF16)
                dkv[g, keys, :] += nn(ds_t, q) + nn(p_t.astype(BF16), grads[g])
                result.append(totals[g] + nn(kt[g, :, keys], ds_t))
            return tuple(result)

        totals = lax.fori_loop(
            0, (p - begin) // 2 + 1, step, tuple(jnp.zeros((HEAD, SPAN), F32) for _ in range(groups)))
        for g in range(groups):
            total = totals[g]
            stacked = jnp.concatenate([total[:, :BLOCK], total[:, BLOCK:]], axis=0)
            dq[pl.ds(pl.multiple_of(base, BLOCK), BLOCK), g * PAIR:(g + 1) * PAIR] = (
                jnp.transpose(stacked) * (HEAD ** -0.5))
        return 0

    lax.fori_loop(0, blocks, one_block, 0)

    def finish(p, sums):
        rows = pl.ds(pl.multiple_of(inv[p] * BLOCK, BLOCK), BLOCK)
        place = pl.ds(pl.multiple_of(p * BLOCK, BLOCK), BLOCK)
        c = tile_lanes(cos[place, :], groups)
        s = tile_lanes(sin[place, :], groups)

        def back(raw, gain, grad):
            u = grad.astype(BF16).astype(F32)
            u = u * c - partner(u) * s
            factor = lax.rsqrt(split_dot(raw * raw, mean) + EPS)
            n = raw * factor
            term = u * n
            return factor * (u * gain - n * split_dot(term * gain, mean)), term

        dq_raw, q_term = back(q_raw[rows, :], gain_q[...], dq[place, :])
        dq_ref[rows, :] = dq_raw.astype(BF16)
        grad = jnp.concatenate([dkv[g, place, :] for g in range(groups)], axis=1)
        dk_raw, k_term = back(kv_raw[rows, :], gain_kv[...], grad)
        dkv_ref[rows, :] = jnp.where(is_key, dk_raw, grad).astype(BF16)

        def folded(term):
            return jnp.sum(term.reshape(BLOCK // 8, 8, wide), axis=0)

        return sums[0] + folded(q_term), sums[1] + folded(k_term)

    zero = jnp.zeros((8, wide), F32)
    sums = lax.fori_loop(0, blocks, finish, (zero, zero))
    gains_ref[0:8, :] = sums[0]
    gains_ref[8:16, :] = sums[1]


def attend_back(inv, first, q_raw, kv_raw, cos, sin, starts, gain_q, gain_kv, o, do, qs, kvs, linv):
    rows, wide = q_raw.shape
    groups = wide // PAIR
    whole = pl.BlockSpec(memory_space=VMEM)
    return pl.pallas_call(
        functools.partial(attend_back_kernel, groups),
        out_shape=(
            jax.ShapeDtypeStruct((rows, wide), BF16),
            jax.ShapeDtypeStruct((rows, wide), BF16),
            jax.ShapeDtypeStruct((16, wide), F32),
        ),
        in_specs=[pl.BlockSpec(memory_space=pltpu.SMEM)] * 2 + [whole] * 12,
        out_specs=(whole,) * 3,
        scratch_shapes=[
            VMEM((groups, HEAD, rows + BLOCK), BF16),
            VMEM((groups, rows + BLOCK, PAIR), F32),
            VMEM((rows, wide), F32),
        ],
        compiler_params=pltpu.CompilerParams(vmem_limit_bytes=LIMIT),
        name="attend_back",
    )(inv, first, q_raw, kv_raw, cos, sin, starts, gain_q, gain_kv, o, do, qs, kvs, linv)


def ffn_kernel(tile, x_ref, o_ref, gy_ref, w_out, gain, w_hbm, y_ref, db_ref, grad_hbm,
               w, total, b_s, y_s, db_s, out_s, sems):
    step = pl.program_id(0)
    pieces, _, part, width = w_hbm.shape
    hidden = pieces * part

    def copies(source, target):
        for k in range(3):
            for d in range(pieces):
                yield source, target, k, d

    def load(k, d):
        return pltpu.make_async_copy(w_hbm.at[d, k], w.at[k, pl.ds(d * part, part), :], sems.at[k, d])

    def store(k, d):
        return pltpu.make_async_copy(out_s.at[k, pl.ds(d * part, part), :], grad_hbm.at[d, k], sems.at[k, d])

    @pl.when(step == 0)
    def _():
        for k in range(3):
            for d in range(pieces):
                load(k, d).start()
        total[...] = jnp.zeros_like(total)
        for k in range(3):
            for d in range(pieces):
                load(k, d).wait()

    x1 = x_ref[...].astype(F32) + nn(o_ref[...], w_out[...])
    scale = lax.rsqrt(jnp.mean(x1 * x1, axis=-1, keepdims=True) + EPS)
    b_s[...] = (x1 * scale * gain[...]).astype(BF16)
    y_s[...] = jnp.zeros_like(y_s)
    db_s[...] = jnp.zeros_like(db_s)

    def hidden_tile(i, _):
        at = pl.ds(pl.multiple_of(i * tile, tile), tile)
        b, gy = b_s[...], gy_ref[...]
        gate = nt(b, w[0, at, :])
        up = nt(b, w[1, at, :])
        d_act = nt(gy, w[2, at, :])
        sig = jax.nn.sigmoid(gate)
        silu = gate * sig
        act = (silu * up).astype(BF16)
        d_gate = (d_act * up * sig * (1.0 + gate * (1.0 - sig))).astype(BF16)
        d_up = (d_act * silu).astype(BF16)
        total[0, at, :] += tn(d_gate, b)
        total[1, at, :] += tn(d_up, b)
        total[2, at, :] += tn(act, gy)
        y_s[...] += nn(act, w[2, at, :])
        db_s[...] += nn(d_gate, w[0, at, :]) + nn(d_up, w[1, at, :])
        return 0

    lax.fori_loop(0, hidden // tile, hidden_tile, 0)
    y_ref[...] = y_s[...].astype(BF16)
    db_ref[...] = db_s[...].astype(BF16)

    @pl.when(step == pl.num_programs(0) - 1)
    def _():
        for k in range(3):
            out_s[k] = total[k].astype(BF16)
            for d in range(pieces):
                store(k, d).start()
        for k in range(3):
            for d in range(pieces):
                store(k, d).wait()


def ffn(x, o, gy, w_out, gain, w, chunk):
    rows, width = x.shape
    pieces, _, part, _ = w.shape
    hidden = pieces * part
    tile = next(t for t in (384, 288, 256, 192, 128, 64, hidden) if hidden % t == 0)
    row_spec = pl.BlockSpec((chunk, width), lambda i: (i, 0))
    return pl.pallas_call(
        functools.partial(ffn_kernel, tile),
        grid=(rows // chunk,),
        out_shape=(
            jax.ShapeDtypeStruct((rows, width), BF16),
            jax.ShapeDtypeStruct((rows, width), BF16),
            jax.ShapeDtypeStruct((pieces, 3, part, width), BF16),
        ),
        in_specs=[row_spec] * 3 + [
            pl.BlockSpec((width, width), lambda i: (0, 0), pipeline_mode=pl.Buffered(1)),
            pl.BlockSpec((1, width), lambda i: (0, 0)),
            pl.BlockSpec(memory_space=pl.ANY),
        ],
        out_specs=(row_spec, row_spec, pl.BlockSpec(memory_space=pl.ANY)),
        scratch_shapes=[
            VMEM((3, hidden, width), BF16),
            VMEM((3, hidden, width), F32),
            VMEM((chunk, width), BF16),
            VMEM((chunk, width), F32),
            VMEM((chunk, width), F32),
            VMEM((3, hidden, width), BF16),
            pltpu.SemaphoreType.DMA((3, pieces)),
        ],
        compiler_params=pltpu.CompilerParams(vmem_limit_bytes=LIMIT),
        name="ffn",
    )(x, o, gy, w_out, gain, w)


def norm_factor(u):
    return lax.rsqrt(jnp.mean(u * u, axis=-1, keepdims=True) + EPS)


def norm_back(u, gain, upstream):
    factor = norm_factor(u)
    unit = u * factor
    weighted = upstream * gain
    back = factor * (weighted - unit * jnp.mean(weighted * unit, axis=-1, keepdims=True))
    return back, jnp.sum(upstream * unit, axis=0)


def place_tables(segment_row, order_row):
    length = segment_row.shape[0]
    docs = jnp.arange(1, MOST_DOCS, dtype=jnp.int32)
    begins = jnp.sum(segment_row[None, :] < docs[:, None], axis=1, dtype=jnp.int32)
    starts = jnp.max(jnp.where(segment_row[None, :] >= docs[:, None], begins[:, None], 0), axis=0)
    blocks = order_row.shape[0]
    ids = jnp.arange(blocks, dtype=jnp.int32)
    inv = jnp.sum(jnp.where(order_row[None, :] == ids[:, None], ids[None, :], 0), axis=1, dtype=jnp.int32)
    first = starts.reshape(blocks, BLOCK)[:, 0] // BLOCK
    lane = jnp.arange(PAIR, dtype=jnp.int32)
    frequency = jnp.exp((lane % (HEAD // 2)).astype(F32) * (-2.0 * math.log(THETA) / HEAD))
    offset = (jnp.arange(length, dtype=jnp.int32) - starts).astype(F32)
    turned = offset[:, None] * frequency[None, :]
    sign = jnp.where(lane % HEAD < HEAD // 2, -1.0, 1.0)
    return inv, first, starts, jnp.cos(turned), jnp.sin(turned) * sign[None, :]


def shards(tokens_in, norm_attn, w_query, w_keyval, gain_query, gain_key, w_out, norm_ffn,
           w_gate, w_up, w_down, cotangent, segments, blocks):
    seq, dp = lax.axis_size("seq"), lax.axis_size("dp")
    me = lax.axis_index("seq")
    rows, width = tokens_in.shape
    total_rows = rows * seq
    mine = KEY_VALUE_HEADS // seq * PAIR
    depth = w_query.shape[0]
    part = w_down.shape[0] // seq

    def my_columns(u):
        return lax.dynamic_slice_in_dim(u, me * mine, mine, 1)

    gain_row = jnp.concatenate([norm_attn, norm_ffn, gain_query, gain_key])
    sizes = (norm_attn.shape[0], norm_ffn.shape[0], gain_query.shape[0], gain_key.shape[0])
    gain_rows = jnp.pad(gain_row[None, :], ((0, 15), (0, 2 * mine - gain_row.shape[0])))
    packed = jnp.concatenate([jnp.concatenate([my_columns(w_query), my_columns(w_keyval)], 1), gain_rows], 0)
    packed = lax.all_gather(packed, "dp", axis=0)
    w_qkv = packed[:, :depth].reshape(width, 2 * mine)
    gains = packed[:, depth].astype(F32)
    g_attn, g_ffn, g_query, g_key = (
        gains[:, sum(sizes[:i]):sum(sizes[:i + 1])].reshape(-1) for i in range(4))
    out_w = lax.all_gather(w_out, "dp", axis=0, tiled=True)

    def my_rows(u):
        return lax.dynamic_slice_in_dim(u, me * part, part, 0)

    ffn_w = jnp.stack([my_rows(w_gate.T), my_rows(w_up.T), my_rows(w_down)])
    ffn_w = lax.all_gather(ffn_w, "dp", axis=0)
    pieces = dp if part % 16 == 0 else 1
    if pieces == 1:
        ffn_w = jnp.moveaxis(ffn_w, 0, 1).reshape(1, 3, dp * part, width)

    inv, first, starts, cos, sin = place_tables(segments[0], blocks[0])
    starts_down = jnp.broadcast_to(starts[:, None], (total_rows, BLOCK))
    starts_across = jnp.broadcast_to(starts.reshape(-1, 1, BLOCK), (total_rows // BLOCK, 8, BLOCK))
    gain_q = jnp.tile(g_query, mine // HEAD)[None, :]
    gain_kv = jnp.tile(jnp.concatenate([g_key, jnp.ones_like(g_key)]), mine // PAIR)[None, :]

    x_all = lax.all_gather(tokens_in, "seq", axis=0, tiled=True)
    gy_all = lax.all_gather(cotangent, "seq", axis=0, tiled=True)
    hidden = x_all.astype(F32)
    a_all = (hidden * norm_factor(hidden) * g_attn).astype(BF16)
    qkv = nn(a_all, w_qkv)
    q_raw, kv_raw = qkv[:, :mine], qkv[:, mine:]
    o, qs, kvs, linv = attend(inv, first, q_raw, kv_raw, cos, sin, starts_down, gain_q, gain_kv)

    o_all = lax.all_gather(o, "seq", axis=1, tiled=True)
    y_part, db_part, ffn_grads = ffn(x_all, o_all, gy_all, out_w, g_ffn[None, :], ffn_w, min(rows, 512))
    d_b = lax.psum_scatter(db_part, "seq", scatter_dimension=0, tiled=True).astype(F32)
    y = lax.psum_scatter(y_part, "seq", scatter_dimension=0, tiled=True).astype(F32)

    if pieces == 1:
        ffn_grads = jnp.moveaxis(ffn_grads.reshape(3, dp, part, width), 1, 0)
    ffn_grads = lax.psum_scatter(ffn_grads, "dp", scatter_dimension=0, tiled=True)[0]
    ffn_grads = lax.all_gather(ffn_grads, "seq", axis=1, tiled=True).astype(F32)

    x_own = tokens_in.astype(F32)
    o_own = lax.dynamic_slice_in_dim(o_all, me * rows, rows, 0)
    x1 = x_own + nn(o_own, out_w)
    output = (x1 + y).astype(BF16)
    d_x1, d_g_ffn = norm_back(x1, g_ffn, d_b)
    d_x1 = d_x1 + cotangent.astype(F32)
    d_y = d_x1.astype(BF16)
    grad_out = tn(o_own, d_y)
    d_o = nt(d_y, out_w).astype(BF16)
    d_o = lax.all_to_all(d_o, "seq", split_axis=1, concat_axis=0, tiled=True)

    dq_raw, dkv_raw, gain_sums = attend_back(
        inv, first, q_raw, kv_raw, cos, sin, starts_across, gain_q, gain_kv, o, d_o, qs, kvs, linv)
    d_qkv = jnp.concatenate([dq_raw, dkv_raw], 1)
    da_part = nt(d_qkv, w_qkv).astype(BF16)
    grad_qkv = tn(a_all, d_qkv)
    d_a = lax.psum_scatter(da_part, "seq", scatter_dimension=0, tiled=True).astype(F32)
    back, d_g_attn = norm_back(x_own, g_attn, d_a)
    grad_tokens = d_x1 + back
    q_sums, k_sums = jnp.sum(gain_sums[:8], 0), jnp.sum(gain_sums[8:], 0)
    d_g_query = jnp.sum(q_sums.reshape(-1, HEAD), 0)
    d_g_key = jnp.sum(k_sums.reshape(-1, PAIR)[:, :HEAD], 0)

    small = jnp.concatenate(
        [u.reshape(dp, -1) for u in (d_g_attn, d_g_ffn, d_g_query, d_g_key)], 1)
    small = jnp.pad(small, ((0, 0), (0, width - small.shape[1])))[:, None, :]
    small = jnp.pad(small, ((0, 0), (0, 15), (0, 0)))
    bundle = jnp.concatenate(
        [grad_qkv.reshape(dp, -1, width), grad_out.reshape(dp, -1, width), small], 1).astype(BF16)
    bundle = lax.psum_scatter(bundle, "dp", scatter_dimension=0, tiled=True)[0]
    bundle = lax.all_gather(bundle, "seq", axis=0).astype(F32)
    n_qkv = depth * 2 * mine // width
    g_qkv = bundle[:, :n_qkv].reshape(seq, depth, 2, mine)
    grad_wq = jnp.moveaxis(g_qkv[:, :, 0], 0, 1).reshape(depth, width)
    grad_wkv = jnp.moveaxis(g_qkv[:, :, 1], 0, 1).reshape(depth, width)
    rest = jnp.sum(bundle[:, n_qkv:], 0)
    grad_wout = rest[:depth]
    tail = rest[depth]
    grads = [tail[sum(sizes[:i]):sum(sizes[:i + 1])] for i in range(4)]
    return (output, grad_tokens, grads[0], grad_wq, grad_wkv, grads[2], grads[3], grad_wout, grads[1],
            ffn_grads[0].T, ffn_grads[1].T, ffn_grads[2])


def solution(mesh):
    rows, cols, row2 = P("dp", None), P(None, "dp"), P(("dp", "seq"), None)
    vec = P("dp")
    return jax.shard_map(
        shards,
        mesh=mesh,
        in_specs=(row2, vec, rows, rows, vec, vec, rows, vec, cols, cols, rows, row2, rows, rows),
        out_specs=(row2, row2, vec, rows, rows, vec, vec, rows, vec, cols, cols, rows),
        check_vma=False,
    )
```

time: 1350 us -> 832 us (0.62)
  blocking collectives: 356 us -> 17.6 us
  matrix products: 293 us -> 21.6 us
  Pallas kernels: 0 us -> 159 us
  waiting for transfers between devices: 476 us -> 559 us
  other arithmetic: 94.1 us -> 31.8 us
  local copies, waits for them, and re-layouts: 73.3 us -> 27.5 us
  starting transfers between devices: 20.2 us -> 0.96 us
    psum x1 -> x0, blocking collectives: 288 us -> none  [shards(): lax.psum((owned_attn_gain, owned_query_w, owned_keyval_w, owned_query_gai...]
    dot_general x46 -> x6, matrix products: 293 us -> 21.6 us  [the longest x2 10.2 us: tn(): lax.dot_general(a, b, (((0,), (0,)), ((), ())), preferred_element_type=F32)]
    pallas_call x0 -> x3, Pallas kernels: none -> 159 us  [the longest x1 77.3 us: ffn(): pl.pallas_call(functools.partial(ffn_kernel, tile), grid=(rows // chunk,)...]
    all_gather x6 -> x8, waiting for transfers between devices: 167 us -> 300 us  [the longest x1 73.4 us: shards(): ffn_w = lax.all_gather(ffn_w, 'dp', axis=0)]
    convert_element_type x17 -> x4, other arithmetic: 45.9 us -> 4.68 us  [the longest x1 2.81 us: shards(): ffn_grads = lax.all_gather(ffn_grads, 'seq', axis=1, tiled=True).astype(F32)]
    unnamed x2 -> x0, blocking collectives: 28.7 us -> none
    all_to_all x5 -> x0, waiting for transfers between devices: 27.6 us -> none  [the longest x1 11.2 us: shards(): lax.all_to_all(grad_query_heads, 'seq', split_axis=0, concat_axis=1, tile...]
    gather x2 -> x0, local copies, waits for them, and re-layouts: 23.6 us -> none  [layout(): return (placed_tokens, segment_row[placed_tokens], offsets[placed_tokens])]
  transfers between devices with their start and end apart: 17 -> 13, of which waited for: 11 -> 12; matrix products, arithmetic and copies ran while one was open for 31% -> 7% of each run, Pallas kernels for 0% -> 5%
where the time goes in v1:
time: 832 us; the launch traced here: 831 us
  waiting for transfers between devices  559 us (67%)
  Pallas kernels  159 us (19%)
  other arithmetic  31.8 us (4%)
  local copies, waits for them, and re-layouts  27.5 us (3%)
  matrix products  21.6 us (3%)
  blocking collectives  17.6 us (2%)
  between operations  14.2 us (2%)
    pallas_call x1, Pallas kernels, ffn(): pl.pallas_call(functools.partial(ffn_kernel, tile), grid=(rows // chunk,)...  77.3 us
    reduce_scatter x1, waiting for transfers between devices, shards(): lax.psum_scatter(ffn_grads, 'dp', scatter_dimension=0, tiled=True)[0]  74 us
    all_gather x1, waiting for transfers between devices, shards(): ffn_w = lax.all_gather(ffn_w, 'dp', axis=0)  73.4 us
    reduce_scatter x1, waiting for transfers between devices, shards(): lax.psum_scatter(y_part, 'seq', scatter_dimension=0, tiled=True).astype(F32)  54 us
    all_gather x1, waiting for transfers between devices, shards(): o_all = lax.all_gather(o, 'seq', axis=1, tiled=True)  52.9 us
    all_gather x1, waiting for transfers between devices, shards(): x_all = lax.all_gather(tokens_in, 'seq', axis=0, tiled=True)  50.6 us
    reduce_scatter x1, waiting for transfers between devices, shards(): lax.psum_scatter(db_part, 'seq', scatter_dimension=0, tiled=True)  48.3 us
    all_gather x1, waiting for transfers between devices, shards(): ffn_grads = lax.all_gather(ffn_grads, 'seq', axis=1, tiled=True).astype(F32)  44.6 us
  transfers between devices with their start and end apart: 13, of which 12 were waited for; matrix products, arithmetic and copies ran while one was open for 7% of the time, Pallas kernels for 5%

profile of v1, /device:TPU:0, one launch (start us, length us, event | category | flops | bytes accessed | tf_op | source)
XLA Modules:
  0.0 831.2 jit_solution(11687667871660174979)
XLA Ops:
  16.5 5.6 fusion.23
  22.1 13.5 %all-gather.22.cloned.1.call-done = bf16[1152,512]{1,0:T(8,128)(2,1)} async-done(((bf16[144,512]{1,0:T(8,128)(2,1)}), bf16[1152,512]{1,0:T(8,128)(2,1)}) %all-gather.22.cloned.1.call-update) | async-done | bytes 1179664 | tf_op jit(solution)/shard_map/all_gather | solution.py:423
  39.4 50.6 %all-gather.12.cloned.1.call-done.x_ref = bf16[2048,1024]{1,0:T(8,128)(2,1)} async-done(((bf16[512,1024]{1,0:T(8,128)(2,1)}), bf16[2048,1024]{1,0:T(8,128)(2,1)}) %all-gather.12.cloned.1.call-update) | async-done | bytes 4194320 | tf_op jit(solution)/shard_map/all_gather | solution.py:445
  90.0 3.2 fusion
  100.0 37.4 %attend.1 = (bf16[2048,256]{1,0:T(8,128)(2,1)}, bf16[2,4096,128]{2,1,0:T(8,128)(2,1)}, bf16[2,2176,128]{2,1,0:T(8,128)(2,1)}, f32[2,16,8,256]{3,2,1,0:T(8,128)}) custom-call(s32[16]{0:T(128)} %select_reduce_fusion.1.inv, s32[16]{0:T(128)} %and_select_fusion.2.first, f32[2048,256]{1,0:T(8,128)} %get-tuple-element.42.q_raw, ...), custom_call_target="tpu_custom_call" | custom-call | tf_op jit(solution)/shard_map/attend/pallas_call | solution.py:141
  137.8 37.0 %all-gather.18.cloned.1.call-done.gy_ref = bf16[2048,1024]{1,0:T(8,128)(2,1)} async-done(((bf16[512,1024]{1,0:T(8,128)(2,1)}), bf16[2048,1024]{1,0:T(8,128)(2,1)}) %all-gather.18.cloned.1.call-update) | async-done | bytes 4194320 | tf_op jit(solution)/shard_map/all_gather | solution.py:446
  174.7 73.4 %all-gather.24.cloned.1.call-done = bf16[24,144,1024]{2,1,0:T(8,128)(2,1)} async-done(((bf16[3,144,1024]{2,1,0:T(8,128)(2,1)}), bf16[24,144,1024]{2,1,0:T(8,128)(2,1)}) %all-gather.24.cloned.1.call-update) | async-done | bytes 7077904 | tf_op jit(solution)/shard_map/all_gather | solution.py:434
  248.1 52.9 %all-gather.14.cloned.1.call-done.o_ref = bf16[2048,1024]{1,0:T(8,128)(2,1)} async-done(((bf16[2048,256]{1,0:T(8,128)(2,1)}), bf16[2048,1024]{1,0:T(8,128)(2,1)}) %all-gather.14.cloned.1.call-update) | async-done | bytes 4194320 | tf_op jit(solution)/shard_map/all_gather | solution.py:453
  300.9 77.3 %ffn.1 = (bf16[2048,1024]{1,0:T(8,128)(2,1)}, bf16[2048,1024]{1,0:T(8,128)(2,1)}, bf16[8,3,144,1024]{3,2,1,0:T(8,128)(2,1)}) custom-call(bf16[2048,1024]{1,0:T(8,128)(2,1)} %all-gather.12.cloned.1.call-done.x_ref, bf16[2048,1024]{1,0:T(8,128)(2,1)} %all-gather.14.cloned.1.call-done.o_ref, bf16[2048,1024]{1,0:T(8,128)(2,1)} %all-gather.18.cloned.1.call-done.gy_ref, ...), custom_call_target="tpu_custom_call" | custom-call | tf_op jit(solution)/shard_map/ffn/pallas_call | solution.py:349
  379.5 3.3 multiply_reduce_fusion
  382.8 48.3 %reduce-scatter.8.cloned.1.call-done = bf16[512,1024]{1,0:T(8,128)(2,1)} async-done(((bf16[2048,1024]{1,0:T(8,128)(2,1)}), bf16[512,1024]{1,0:T(8,128)(2,1)}) %reduce-scatter.8.cloned.1.call-update) | async-done | bytes 1048592 | tf_op jit(solution)/shard_map/reduce_scatter | solution.py:455
  433.1 54.0 %reduce-scatter.6.cloned.1.call-done = bf16[512,1024]{1,0:T(8,128)(2,1)} async-done(((bf16[2048,1024]{1,0:T(8,128)(2,1)}), bf16[512,1024]{1,0:T(8,128)(2,1)}) %reduce-scatter.6.cloned.1.call-update) | async-done | bytes 1048592 | tf_op jit(solution)/shard_map/reduce_scatter | solution.py:456
  487.1 3.4 fusion.15
  491.9 17.6 %all_to_all.19 = bf16[512,4,256]{2,0,1:T(8,128)(2,1)} all-to-all(bf16[512,4,256]{2,0,1:T(8,128)(2,1)S(1)} %bitcast.83), channel_id=1, replica_groups=mesh['dp'=8,'seq'=4] {'seq'}, dimensions={1} | all-to-all | bytes 2097152 | tf_op jit(solution)/shard_map/all_to_all | solution.py:472
  510.1 44.0 %attend_back.1 = (bf16[2048,256]{1,0:T(8,128)(2,1)}, bf16[2048,256]{1,0:T(8,128)(2,1)}, f32[16,256]{1,0:T(8,128)}) custom-call(s32[16]{0:T(128)} %select_reduce_fusion.1.inv, s32[16]{0:T(128)} %and_select_fusion.2.first, f32[2048,256]{1,0:T(8,128)} %get-tuple-element.42.q_raw, f32[2048,256]{1,0:T(8,128)} %get-tuple-element.41.kv_raw, ...), custom_call_target="tpu_custom_call" | custom-call | tf_op jit(solution)/shard_map/attend_back/pallas_call | solution.py:258
  557.0 4.5 convolution_convert_fusion
  563.5 3.8 convolution_convert_fusion.1
  567.6 6.4 convolution_convert_fusion.3
  576.2 36.0 %reduce-scatter.10.cloned.1.call-done = bf16[512,1024]{1,0:T(8,128)(2,1)} async-done(((bf16[2048,1024]{1,0:T(8,128)(2,1)}), bf16[512,1024]{1,0:T(8,128)(2,1)}) %reduce-scatter.10.cloned.1.call-update) | async-done | bytes 1048592 | tf_op jit(solution)/shard_map/reduce_scatter | solution.py:479
  614.5 3.2 fusion.4
  617.7 74.0 %reduce-scatter.14.cloned.1.call-done = bf16[1,3,144,1024]{3,2,1,0:T(8,128)(2,1)} async-done(((bf16[8,3,144,1024]{3,2,1,0:T(8,128)(2,1)}), bf16[1,3,144,1024]{3,2,1,0:T(8,128)(2,1)}) %reduce-scatter.14.cloned.1.call-update) | async-done | bytes 884752 | tf_op jit(solution)/shard_map/reduce_scatter | solution.py:460
  692.1 43.0 %reduce-scatter.12.cloned.1.call-done = bf16[1,208,1024]{2,1,0:T(8,128)(2,1)} async-done(((bf16[8,208,1024]{2,1,0:T(8,128)(2,1)}), bf16[1,208,1024]{2,1,0:T(8,128)(2,1)}) %reduce-scatter.12.cloned.1.call-update) | async-done | bytes 426000 | tf_op jit(solution)/shard_map/reduce_scatter | solution.py:492
  738.3 44.6 %all-gather.26.cloned.1.call-done = bf16[1,3,576,1024]{3,2,1,0:T(8,128)(2,1)} async-done(((bf16[1,3,144,1024]{3,2,1,0:T(8,128)(2,1)}), bf16[1,3,576,1024]{3,2,1,0:T(8,128)(2,1)}) %all-gather.26.cloned.1.call-update) | async-done | bytes 3538960 | tf_op jit(solution)/shard_map/all_gather | solution.py:461
  788.9 28.1 %all-gather.20.cloned.1.call-done = bf16[4,208,1024]{2,1,0:T(8,128)(2,1)} async-done(((bf16[1,208,1024]{2,1,0:T(8,128)(2,1)}), bf16[4,208,1024]{2,1,0:T(8,128)(2,1)}) %all-gather.20.cloned.1.call-update) | async-done | bytes 1703952 | tf_op jit(solution)/shard_map/all_gather | solution.py:493
  (125 shorter events, 51.9 us)
Async XLA Ops:
  7.2 28.4 %all-gather.22.cloned.1.call-start = ((), (), s32[]{:S(2)}) async-start(), calls=%async_computation.16 | async-start | bytes 1327104 | tf_op jit(solution)/shard_map/all_gather | solution.py:423
  9.6 80.4 %all-gather.12.cloned.1.call-start = ((), (), s32[]{:S(2)}) async-start(), calls=%async_computation.6 | async-start | bytes 5242880 | tf_op jit(solution)/shard_map/all_gather | solution.py:445
  10.4 127.4 %all-gather.16.cloned.1.call-start = ((), (), s32[]{:S(2)}) async-start(), calls=%async_computation.8 | async-start | bytes 2359296 | tf_op jit(solution)/shard_map/all_gather | solution.py:428
  11.1 163.6 %all-gather.18.cloned.1.call-start = ((), (), s32[]{:S(2)}) async-start(), calls=%async_computation.9 | async-start | bytes 5242880 | tf_op jit(solution)/shard_map/all_gather | solution.py:446
  11.7 236.4 %all-gather.24.cloned.1.call-start = ((), (), s32[]{:S(2)}) async-start(), calls=%async_computation.17 | async-start | bytes 7962624 | tf_op jit(solution)/shard_map/all_gather | solution.py:434
  11.7 3.2 copy-start.15
  11.7 3.9 copy-start.13
  14.9 286.1 %all-gather.14.cloned.1.call-start = ((), (), s32[]{:S(2)}) async-start(), calls=%async_computation.7 | async-start | bytes 5242880 | tf_op jit(solution)/shard_map/all_gather | solution.py:453
  37.8 55.5 %copy-start.9 = (bf16[8,128,512]{2,1,0:T(8,128)(2,1)}, bf16[8,128,512]{2,1,0:T(8,128)(2,1)S(1)}, u32[]{:S(2)}) copy-start(bf16[8,128,512]{2,1,0:T(8,128)(2,1)S(1)} %slice.123) | copy-start | bytes 3145732
  90.0 3.4 copy-start.2
  137.5 293.6 %reduce-scatter.8.cloned.1.call-start = ((), (), s32[]{:S(2)}) async-start(), calls=%async_computation.11 | async-start | bytes 5242880 | tf_op jit(solution)/shard_map/reduce_scatter | solution.py:455
  378.2 108.8 %reduce-scatter.6.cloned.1.call-start = ((), (), s32[]{:S(2)}) async-start(), calls=%async_computation.10 | async-start | bytes 5242880 | tf_op jit(solution)/shard_map/reduce_scatter | solution.py:456
  379.0 233.2 %reduce-scatter.10.cloned.1.call-start = ((), (), s32[]{:S(2)}) async-start(), calls=%async_computation.12 | async-start | bytes 5242880 | tf_op jit(solution)/shard_map/reduce_scatter | solution.py:479
  382.8 104.3 %copy-start.6 = (bf16[512,1024]{1,0:T(8,128)(2,1)S(1)}, bf16[512,1024]{1,0:T(8,128)(2,1)}, u32[]{:S(2)}) copy-start(bf16[512,1024]{1,0:T(8,128)(2,1)} %param.25) | copy-start | bytes 3145732
  487.1 3.4 copy-start.8
  554.1 2.9 copy-start.10
  561.5 130.3 %reduce-scatter.14.cloned.1.call-start = ((), (), s32[]{:S(2)}) async-start(), calls=%async_computation.15 | async-start | bytes 7962624 | tf_op jit(solution)/shard_map/reduce_scatter | solution.py:460
  561.6 1.9 copy-start.4
  562.1 173.1 %reduce-scatter.12.cloned.1.call-start = ((), (), s32[]{:S(2)}) async-start(), calls=%async_computation.13 | async-start | bytes 3833856 | tf_op jit(solution)/shard_map/reduce_scatter | solution.py:492
  563.5 3.9 copy-start.14
  612.2 2.2 copy-start.7
  617.7 165.3 %all-gather.26.cloned.1.call-start = ((), (), s32[]{:S(2)}) async-start(), calls=%async_computation.18 | async-start | bytes 4423680 | tf_op jit(solution)/shard_map/all_gather | solution.py:461
  691.8 125.2 %all-gather.20.cloned.1.call-start = ((), (), s32[]{:S(2)}) async-start(), calls=%async_computation.14 | async-start | bytes 2129920 | tf_op jit(solution)/shard_map/all_gather | solution.py:493
  818.9 2.2 copy-start.5
  (5 other events, 6.6 us)
Sparse Core Ops, SparseCore 0:
  10.2 25.3 all-gather.21
  37.5 52.5 all-gather.11
  91.6 29.1 all-gather.15
  122.5 52.1 all-gather.17
  176.8 71.2 all-gather.23
  249.8 51.1 all-gather.13
  378.4 52.7 reduce-scatter.7
  434.4 52.6 reduce-scatter.5
  561.6 50.5 reduce-scatter.9
  614.5 77.2 reduce-scatter.13
  694.2 40.9 reduce-scatter.11
  737.0 45.8 all-gather.25
  784.9 32.0 all-gather.19

commit v2 on v1

--- a/solution.py
+++ b/solution.py
@@ -82,9 +82,9 @@
             u = raw * lax.rsqrt(split_dot(raw * raw, mean) + EPS) * gain
             return u * c + partner(u) * s
 
-        q = turned(q_raw[rows, :], gain_q[...]) * (HEAD ** -0.5)
+        q = turned(q_raw[rows, :], gain_q[0:1, :]) * (HEAD ** -0.5)
         kv = kv_raw[rows, :]
-        kv = jnp.where(is_key, turned(kv, gain_kv[...]), kv)
+        kv = jnp.where(is_key, turned(kv, gain_kv[0:1, :]), kv)
         for g in range(groups):
             pair = q[:, g * PAIR:(g + 1) * PAIR]
             qs[g, pl.ds(pl.multiple_of(p * SPAN, SPAN), BLOCK), :] = jnp.where(low_half, pair, 0.0).astype(BF16)
@@ -234,10 +234,10 @@
             term = u * n
             return factor * (u * gain - n * split_dot(term * gain, mean)), term
 
-        dq_raw, q_term = back(q_raw[rows, :], gain_q[...], dq[place, :])
+        dq_raw, q_term = back(q_raw[rows, :], gain_q[0:1, :], dq[place, :])
         dq_ref[rows, :] = dq_raw.astype(BF16)
         grad = jnp.concatenate([dkv[g, place, :] for g in range(groups)], axis=1)
-        dk_raw, k_term = back(kv_raw[rows, :], gain_kv[...], grad)
+        dk_raw, k_term = back(kv_raw[rows, :], gain_kv[0:1, :], grad)
         dkv_ref[rows, :] = jnp.where(is_key, dk_raw, grad).astype(BF16)
 
         def folded(term):
@@ -274,116 +274,672 @@
     )(inv, first, q_raw, kv_raw, cos, sin, starts, gain_q, gain_kv, o, do, qs, kvs, linv)
 
 
-def ffn_kernel(tile, x_ref, o_ref, gy_ref, w_out, gain, w_hbm, y_ref, db_ref, grad_hbm,
-               w, total, b_s, y_s, db_s, out_s, sems):
-    step = pl.program_id(0)
-    pieces, _, part, width = w_hbm.shape
+def other(index, bits, count):
+    flipped, weight = 0, 1
+    while weight < count:
+        one, two = (index // weight) % 2, (bits // weight) % 2
+        flipped = flipped + weight * (one + two - 2 * one * two)
+        weight *= 2
+    return flipped
+
+
+def greet(seq, me, dp=0, here=0):
+    barrier = pltpu.get_barrier_semaphore()
+    peers = [{"seq": other(me, j, seq)} for j in range(1, seq)]
+    if dp:
+        peers += [{"dp": other(here, 1, dp)}] + [{"dp": other(here, 2 * t, dp)} for t in range(1, dp // 2)]
+    for peer in peers:
+        pl.semaphore_signal(barrier, inc=1, device_id=peer, device_id_type=pl.DeviceIdType.MESH)
+    pl.semaphore_wait(barrier, len(peers))
+
+
+def send(source, target, sems, at, peer, axis="seq"):
+    return pltpu.make_async_remote_copy(
+        src_ref=source, dst_ref=target, send_sem=sems[0].at[at], recv_sem=sems[1].at[at],
+        device_id={axis: peer}, device_id_type=pl.DeviceIdType.MESH)
+
+
+def flips(seq):
+    bits = [1 << i for i in range(seq.bit_length() - 1)]
+    return bits, bits[::-1]
+
+
+class Gather:
+    def __init__(self, me, seq, own, slots, sems):
+        self.me, self.seq, self.own, self.slots, self.sems = me, seq, own, slots, sems
+        self.half = own.shape[0] // 2
+        self.orders = flips(seq)
+        self.arrived = set()
+        self.source = {}
+        self.items = []
+        for step in range(len(self.orders[0])):
+            for part in range(2):
+                bits = self.orders[part]
+                held = [0]
+                for bit in bits[:step]:
+                    held += [k + bit for k in held]
+                for k in held:
+                    self.items.append((part, step, k))
+                    self.source[part, k + bits[step]] = (part, step, k)
+
+    def copy(self, part, step, k):
+        bit = self.orders[part][step]
+        rows = pl.ds(part * self.half, self.half)
+        source = self.own.at[rows, :] if k == 0 else self.slots.at[k, rows, :]
+        return send(source, self.slots.at[k + bit, rows, :], self.sems, (part, step, k), other(self.me, bit, self.seq))
+
+    def begin(self):
+        for item in self.items:
+            if item[2] == 0:
+                self.copy(*item).start()
+
+    def wait(self, part, k):
+        if (part, k) not in self.arrived:
+            self.arrived.add((part, k))
+            self.copy(*self.source[part, k]).wait_recv()
+
+    def forward(self):
+        for item in self.items:
+            if item[2] != 0:
+                self.wait(item[0], item[2])
+                self.copy(*item).start()
+
+    def finish(self, k):
+        self.wait(0, k)
+        self.wait(1, k)
+
+    def drain(self):
+        for item in self.items:
+            self.copy(*item).wait_send()
+
+    @staticmethod
+    def semaphores(seq):
+        return pltpu.SemaphoreType.DMA((2, max(seq.bit_length() - 1, 1), seq))
+
+
+class Spread:
+    def __init__(self, here, dp, own, slots, sems):
+        self.here, self.dp, self.own, self.slots = here, dp, own, slots
+        self.far, self.near = sems[:2], sems[2:]
+
+    def to_far(self, t):
+        return send(self.own, self.slots.at[self.here], self.far, t, other(self.here, 2 * t, self.dp), "dp")
+
+    def to_near(self, t):
+        owner = other(self.here, 2 * t, self.dp)
+        source = self.own if t == 0 else self.slots.at[owner]
+        return send(source, self.slots.at[owner], self.near, t, other(self.here, 1, self.dp), "dp")
+
+    def begin(self):
+        for t in range(1, self.dp // 2):
+            self.to_far(t).start()
+        self.to_near(0).start()
+
+    def forward(self):
+        for t in range(1, self.dp // 2):
+            self.to_far(t).wait_recv()
+            self.to_near(t).start()
+
+    def finish(self):
+        for t in range(self.dp // 2):
+            self.to_near(t).wait_recv()
+
+    def drain(self):
+        for t in range(1, self.dp // 2):
+            self.to_far(t).wait_send()
+        for t in range(self.dp // 2):
+            self.to_near(t).wait_send()
+
+    @staticmethod
+    def semaphores(dp):
+        return [pltpu.SemaphoreType.DMA((dp // 2,))] * 4
+
+
+def selected(piece, offset, size, owner, wide, period):
+    group = offset // PAIR
+    lane = lax.broadcasted_iota(jnp.int32, (PAIR, wide), 0) - offset % PAIR
+    place = lax.broadcasted_iota(jnp.int32, (PAIR, wide), 1) % period
+    hot = (place == lane + owner * size) & (lane >= 0) & (lane < size)
+    return nn(piece[:, group * PAIR:(group + 1) * PAIR], hot.astype(BF16))
+
+
+def project_kernel(seq, dp, sizes, x_ref, pack_ref, x_all, a_all, q_raw, kv_raw, w_ref, g_attn, g_ffn, g_q, g_kv,
+                   packs, x_send, x_recv, far_out, far_in, near_out, near_in, own_sem):
+    me, here = lax.axis_index("seq"), lax.axis_index("dp")
+    rows, width = x_ref.shape
+    depth = pack_ref.shape[0] - 16
+    mine = q_raw.shape[1]
+    gather = Gather(me, seq, x_ref, x_all, (x_send, x_recv))
+    pack = Spread(here, dp, pack_ref, packs, (far_out, far_in, near_out, near_in))
+    greet(seq, me, dp, here)
+    pack.begin()
+    gather.begin()
+    copies = [pltpu.make_async_copy(x_ref, x_all.at[0], own_sem.at[0]),
+              pltpu.make_async_copy(pack_ref, packs.at[here], own_sem.at[1])]
+    for copy in copies:
+        copy.start()
+    pack.forward()
+    gather.forward()
+    pack.finish()
+    copies[1].wait()
+    totals = [jnp.zeros((16, width), F32)] * 2 + [jnp.zeros((16, mine), F32)] * 2
+    for d in range(dp):
+        w_ref[d * depth:(d + 1) * depth, :] = packs[d, :depth, :]
+        piece = packs[d, depth:, :]
+        for i, period in enumerate((width, width, HEAD, PAIR)):
+            totals[i] = totals[i] + selected(piece, sum(sizes[:i]), sizes[i], d, totals[i].shape[1], period)
+    gain = totals[0][0:1]
+    g_attn[...] = totals[0][:8]
+    g_ffn[...] = totals[1][:8]
+    g_q[...] = totals[2][:8]
+    g_kv[...] = jnp.where(lanes((8, mine)) % PAIR < HEAD, totals[3][:8], 1.0)
+    for k in [0] + list(range(1, seq)):
+        if k:
+            gather.finish(k)
+        x = (x_ref[...] if k == 0 else x_all[k]).astype(F32)
+        a = (x * lax.rsqrt(jnp.mean(x * x, axis=-1, keepdims=True) + EPS) * gain).astype(BF16)
+        a_all[k] = a
+        qkv = nn(a, w_ref[...])
+        at = pl.ds(pl.multiple_of(other(me, k, seq) * rows, rows), rows)
+        q_raw[at, :] = qkv[:, :mine]
+        kv_raw[at, :] = qkv[:, mine:]
+    copies[0].wait()
+    gather.drain()
+    pack.drain()
+
+
+def project(x, packed, seq, dp, sizes):
+    rows, width = x.shape
+    wide = packed.shape[1]
+    mine = wide // 2
+    whole = pl.BlockSpec(memory_space=VMEM)
+    shape = jax.ShapeDtypeStruct
+    dma = pltpu.SemaphoreType.DMA
+    return pl.pallas_call(
+        functools.partial(project_kernel, seq, dp, sizes),
+        out_shape=(
+            shape((seq, rows, width), BF16), shape((seq, rows, width), BF16),
+            shape((seq * rows, mine), F32), shape((seq * rows, mine), F32),
+            shape((width, wide), BF16),
+            shape((8, width), F32), shape((8, width), F32), shape((8, mine), F32), shape((8, mine), F32)),
+        in_specs=[whole] * 2,
+        out_specs=(whole,) * 9,
+        scratch_shapes=[VMEM((dp,) + packed.shape, BF16), Gather.semaphores(seq), Gather.semaphores(seq)]
+        + Spread.semaphores(dp) + [dma((2,))],
+        compiler_params=pltpu.CompilerParams(vmem_limit_bytes=LIMIT, collective_id=0, has_side_effects=True),
+        name="project",
+    )(x, packed)
+
+
+def ffn_kernel(seq, tile, *refs):
+    refs = list(refs)
+    o_ref, x_hbm, gain, w_hbm = refs[:4]
+    gy_hbm = refs[4:4 + seq]
+    rest = refs[4 + seq:]
+    grad_hbm, dx_ref, dy_ref, xy_ref, w_out, o_own = rest[:6]
+    y_hbm = [None] + rest[6:5 + seq]
+    (w, total, o_buf, x_s, gy_s, b_s, y_s, db_s, x1_s, y_out, db_send, db_recv,
+     extra, w_sems, o_send, o_recv, db_out, db_in, in_sems, y_sem, extra_sem) = rest[5 + seq:]
+    me = lax.axis_index("seq")
+    pieces, _, width = w_hbm.shape
+    depth = width // pieces
+    part = (w_hbm.shape[1] - depth) // 3
     hidden = pieces * part
-
-    def copies(source, target):
+    rows = dx_ref.shape[0]
+    cols = o_ref.shape[1]
+
+    def load_w(k, d):
+        source = w_hbm.at[d, pl.ds(k * part, depth if k == 3 else part), :]
+        target = w_out.at[pl.ds(d * depth, depth), :] if k == 3 else w.at[k, pl.ds(d * part, part), :]
+        return pltpu.make_async_copy(source, target, w_sems.at[k, d])
+
+    def store_w(k, d):
+        return pltpu.make_async_copy(
+            w.at[k, pl.ds(d * part, part), :], grad_hbm.at[d, pl.ds(k * part, part), :], w_sems.at[k, d])
+
+    def store_extra(d):
+        return pltpu.make_async_copy(extra, grad_hbm.at[d, pl.ds(3 * part, 16), :], extra_sem.at[d])
+
+    def chunk_of(k):
+        return pl.ds(pl.multiple_of(other(me, k, seq) * rows, rows), rows)
+
+    def load_x(k, slot):
+        return pltpu.make_async_copy(x_hbm.at[k], x_s.at[slot], in_sems.at[0, slot])
+
+    def load_gy(k, slot):
+        return pltpu.make_async_copy(gy_hbm[k], gy_s.at[slot], in_sems.at[1, slot])
+
+    def start_inputs(k, slot):
+        load_x(k, slot).start()
+        for one in range(seq):
+            @pl.when(k == one)
+            def _():
+                load_gy(one, slot).start()
+
+    def store_y(k):
+        return pltpu.make_async_copy(y_out, y_hbm[k], y_sem)
+
+    def send_o(k, j):
+        peer = other(me, j, seq)
+        at = pl.ds(pl.multiple_of(other(peer, k, seq) * rows, rows), rows)
+        return send(o_ref.at[at, :], o_buf.at[k, j - 1], (o_send, o_recv), (k, j - 1), peer)
+
+    def send_db(k):
+        return send(db_send.at[k - 1], db_recv.at[k - 1], (db_out, db_in), k - 1, other(me, k, seq))
+
+    def out_rows(j):
+        return pl.ds(pl.multiple_of(other(me, j, seq) * cols, cols), cols)
+
+    for k in (3, 0, 1, 2):
+        for d in range(pieces):
+            load_w(k, d).start()
+    start_inputs(seq - 1, 0)
+    greet(seq, me)
+    for k in reversed(range(seq)):
+        for j in reversed(range(1, seq)):
+            send_o(k, j).start()
+    total[...] = jnp.zeros_like(total)
+    for k in range(4):
+        for d in range(pieces):
+            load_w(k, d).wait()
+
+    def one_chunk(i, _):
+        k = seq - 1 - i
+        slot = i % 2
+        load_x(0, slot).wait()
+        load_gy(0, slot).wait()
+
+        @pl.when(k > 0)
+        def _():
+            start_inputs(k - 1, 1 - slot)
+
+        for j in range(1, seq):
+            send_o(k, j).wait_recv()
+        x1 = x_s[slot].astype(F32) + nn(o_ref[chunk_of(k), :], w_out[out_rows(0), :])
+        for j in range(1, seq):
+            x1 = x1 + nn(o_buf[k, j - 1], w_out[out_rows(j), :])
+        x1_s[...] = x1
+        scale = lax.rsqrt(jnp.mean(x1 * x1, axis=-1, keepdims=True) + EPS)
+        b_s[...] = (x1 * scale * gain[0:1, :]).astype(BF16)
+        y_s[...] = jnp.zeros_like(y_s)
+        db_s[...] = jnp.zeros_like(db_s)
+
+        def hidden_tile(t, _):
+            at = pl.ds(pl.multiple_of(t * tile, tile), tile)
+            b, gy = b_s[...], gy_s[slot]
+            gate = nt(b, w[0, at, :])
+            up = nt(b, w[1, at, :])
+            d_act = nt(gy, w[2, at, :])
+            sig = jax.nn.sigmoid(gate)
+            silu = gate * sig
+            act = (silu * up).astype(BF16)
+            d_gate = (d_act * up * sig * (1.0 + gate * (1.0 - sig))).astype(BF16)
+            d_up = (d_act * silu).astype(BF16)
+            total[0, at, :] += tn(d_gate, b)
+            total[1, at, :] += tn(d_up, b)
+            total[2, at, :] += tn(act, gy)
+            y_s[...] += nn(act, w[2, at, :])
+            db_s[...] += nn(d_gate, w[0, at, :]) + nn(d_up, w[1, at, :])
+            return 0
+
+        lax.fori_loop(0, hidden // tile, hidden_tile, 0)
+
+        @pl.when(k > 0)
+        def _():
+            db_send[k - 1] = db_s[...].astype(BF16)
+            send_db(k).start()
+
+            @pl.when(i > 0)
+            def _():
+                store_y(1).wait()
+
+            y_out[...] = y_s[...].astype(BF16)
+            for one in range(1, seq):
+                @pl.when(k == one)
+                def _():
+                    store_y(one).start()
+
+        return 0
+
+    lax.fori_loop(0, seq, one_chunk, 0)
+    for k in range(3):
+        w[k] = total[k].astype(BF16)
+        for d in range(pieces):
+            store_w(k, d).start()
+    xy_ref[...] = x1_s[...] + y_s[...]
+    o_own[0] = o_ref[chunk_of(0), :]
+    for j in range(1, seq):
+        o_own[j] = o_buf[0, j - 1]
+    db = db_s[...]
+    for k in reversed(range(1, seq)):
+        send_db(k).wait_recv()
+        db = db + db_recv[k - 1].astype(F32)
+    x1 = x1_s[...]
+    factor = lax.rsqrt(jnp.mean(x1 * x1, axis=-1, keepdims=True) + EPS)
+    unit = x1 * factor
+    term = db * unit
+    weighted = db * gain[0:1, :]
+    back = factor * (weighted - unit * jnp.mean(term * gain[0:1, :], axis=-1, keepdims=True))
+    dx = gy_s[(seq - 1) % 2].astype(F32) + back
+    dx_ref[...] = dx
+    dy_ref[...] = dx.astype(BF16)
+    extra[...] = jnp.broadcast_to(jnp.sum(term, axis=0, keepdims=True), (16, width)).astype(BF16)
+    for d in range(pieces):
+        store_extra(d).start()
+    for k in range(1, seq):
+        send_db(k).wait_send()
+    store_y(1).wait()
+    for k in range(seq):
+        for j in range(1, seq):
+            send_o(k, j).wait_send()
+    for d in range(pieces):
+        store_extra(d).wait()
         for k in range(3):
-            for d in range(pieces):
-                yield source, target, k, d
-
-    def load(k, d):
-        return pltpu.make_async_copy(w_hbm.at[d, k], w.at[k, pl.ds(d * part, part), :], sems.at[k, d])
-
-    def store(k, d):
-        return pltpu.make_async_copy(out_s.at[k, pl.ds(d * part, part), :], grad_hbm.at[d, k], sems.at[k, d])
-
-    @pl.when(step == 0)
-    def _():
-        for k in range(3):
-            for d in range(pieces):
-                load(k, d).start()
-        total[...] = jnp.zeros_like(total)
-        for k in range(3):
-            for d in range(pieces):
-                load(k, d).wait()
-
-    x1 = x_ref[...].astype(F32) + nn(o_ref[...], w_out[...])
-    scale = lax.rsqrt(jnp.mean(x1 * x1, axis=-1, keepdims=True) + EPS)
-    b_s[...] = (x1 * scale * gain[...]).astype(BF16)
-    y_s[...] = jnp.zeros_like(y_s)
-    db_s[...] = jnp.zeros_like(db_s)
-
-    def hidden_tile(i, _):
-        at = pl.ds(pl.multiple_of(i * tile, tile), tile)
-        b, gy = b_s[...], gy_ref[...]
-        gate = nt(b, w[0, at, :])
-        up = nt(b, w[1, at, :])
-        d_act = nt(gy, w[2, at, :])
-        sig = jax.nn.sigmoid(gate)
-        silu = gate * sig
-        act = (silu * up).astype(BF16)
-        d_gate = (d_act * up * sig * (1.0 + gate * (1.0 - sig))).astype(BF16)
-        d_up = (d_act * silu).astype(BF16)
-        total[0, at, :] += tn(d_gate, b)
-        total[1, at, :] += tn(d_up, b)
-        total[2, at, :] += tn(act, gy)
-        y_s[...] += nn(act, w[2, at, :])
-        db_s[...] += nn(d_gate, w[0, at, :]) + nn(d_up, w[1, at, :])
-        return 0
-
-    lax.fori_loop(0, hidden // tile, hidden_tile, 0)
-    y_ref[...] = y_s[...].astype(BF16)
-    db_ref[...] = db_s[...].astype(BF16)
-
-    @pl.when(step == pl.num_programs(0) - 1)
-    def _():
-        for k in range(3):
-            out_s[k] = total[k].astype(BF16)
-            for d in range(pieces):
-                store(k, d).start()
-        for k in range(3):
-            for d in range(pieces):
-                store(k, d).wait()
-
-
-def ffn(x, o, gy, w_out, gain, w, chunk):
-    rows, width = x.shape
-    pieces, _, part, _ = w.shape
+            store_w(k, d).wait()
+
+
+def ffn(o, x, gy, gain, w):
+    seq = len(gy)
+    all_rows, cols = o.shape
+    rows, width = gy[0].shape
+    pieces = w.shape[0]
+    part = (w.shape[1] - width // pieces) // 3
     hidden = pieces * part
     tile = next(t for t in (384, 288, 256, 192, 128, 64, hidden) if hidden % t == 0)
-    row_spec = pl.BlockSpec((chunk, width), lambda i: (i, 0))
+    whole, far = pl.BlockSpec(memory_space=VMEM), pl.BlockSpec(memory_space=pl.ANY)
+    wide, narrow = jax.ShapeDtypeStruct((rows, width), F32), jax.ShapeDtypeStruct((rows, width), BF16)
+    dma = pltpu.SemaphoreType.DMA
     return pl.pallas_call(
-        functools.partial(ffn_kernel, tile),
-        grid=(rows // chunk,),
-        out_shape=(
-            jax.ShapeDtypeStruct((rows, width), BF16),
-            jax.ShapeDtypeStruct((rows, width), BF16),
-            jax.ShapeDtypeStruct((pieces, 3, part, width), BF16),
-        ),
-        in_specs=[row_spec] * 3 + [
-            pl.BlockSpec((width, width), lambda i: (0, 0), pipeline_mode=pl.Buffered(1)),
-            pl.BlockSpec((1, width), lambda i: (0, 0)),
-            pl.BlockSpec(memory_space=pl.ANY),
-        ],
-        out_specs=(row_spec, row_spec, pl.BlockSpec(memory_space=pl.ANY)),
+        functools.partial(ffn_kernel, seq, tile),
+        out_shape=(jax.ShapeDtypeStruct((pieces, 3 * part + 16, width), BF16), wide, narrow, wide,
+                   jax.ShapeDtypeStruct((width, width), BF16),
+                   jax.ShapeDtypeStruct((seq, rows, cols), BF16)) + (narrow,) * (seq - 1),
+        in_specs=[whole, far, whole, far] + [far] * seq,
+        out_specs=(far,) + (whole,) * 5 + (far,) * (seq - 1),
         scratch_shapes=[
             VMEM((3, hidden, width), BF16),
             VMEM((3, hidden, width), F32),
-            VMEM((chunk, width), BF16),
-            VMEM((chunk, width), F32),
-            VMEM((chunk, width), F32),
-            VMEM((3, hidden, width), BF16),
-            pltpu.SemaphoreType.DMA((3, pieces)),
+            VMEM((seq, seq - 1, rows, cols), BF16),
+            VMEM((2, rows, width), BF16),
+            VMEM((2, rows, width), BF16),
+            VMEM((rows, width), BF16),
+            VMEM((rows, width), F32),
+            VMEM((rows, width), F32),
+            VMEM((rows, width), F32),
+            VMEM((rows, width), BF16),
+            VMEM((seq - 1, rows, width), BF16),
+            VMEM((seq - 1, rows, width), BF16),
+            VMEM((16, width), BF16),
+            dma((4, pieces)), dma((seq, seq - 1)), dma((seq, seq - 1)), dma((seq - 1,)), dma((seq - 1,)),
+            dma((2, 2)), dma(()), dma((pieces,)),
         ],
-        compiler_params=pltpu.CompilerParams(vmem_limit_bytes=LIMIT),
+        compiler_params=pltpu.CompilerParams(vmem_limit_bytes=LIMIT, collective_id=1, has_side_effects=True),
         name="ffn",
-    )(x, o, gy, w_out, gain, w)
-
-
-def norm_factor(u):
-    return lax.rsqrt(jnp.mean(u * u, axis=-1, keepdims=True) + EPS)
-
-
-def norm_back(u, gain, upstream):
-    factor = norm_factor(u)
-    unit = u * factor
-    weighted = upstream * gain
-    back = factor * (weighted - unit * jnp.mean(weighted * unit, axis=-1, keepdims=True))
-    return back, jnp.sum(upstream * unit, axis=0)
+    )(o, x, gain, w, *gy)
+
+
+def out_back_kernel(seq, dy_ref, w_out, o_own, do_ref, grad_ref, held, send_sem, recv_sem):
+    me = lax.axis_index("seq")
+    rows, cols = held.shape[1:]
+    mine = pl.ds(pl.multiple_of(me * rows, rows), rows)
+
+    def out_rows(j):
+        return pl.ds(pl.multiple_of(other(me, j, seq) * cols, cols), cols)
+
+    def send_do(j):
+        return send(held.at[j - 1], do_ref.at[mine, :], (send_sem, recv_sem), j - 1, other(me, j, seq))
+
+    greet(seq, me)
+    dy = dy_ref[...]
+    for j in reversed(range(1, seq)):
+        held[j - 1] = nt(dy, w_out[out_rows(j), :]).astype(BF16)
+        send_do(j).start()
+    do_ref[mine, :] = nt(dy, w_out[out_rows(0), :]).astype(BF16)
+    for j in range(seq):
+        grad_ref[out_rows(j), :] = tn(o_own[j], dy).astype(BF16)
+    for j in range(1, seq):
+        send_do(j).wait_send()
+        send_do(j).wait_recv()
+
+
+def out_back(dy, w_out, o_own):
+    seq, rows, cols = o_own.shape
+    width = dy.shape[1]
+    whole = pl.BlockSpec(memory_space=VMEM)
+    dma = pltpu.SemaphoreType.DMA
+    return pl.pallas_call(
+        functools.partial(out_back_kernel, seq),
+        out_shape=(jax.ShapeDtypeStruct((seq * rows, cols), BF16), jax.ShapeDtypeStruct((width, width), BF16)),
+        in_specs=[whole] * 3,
+        out_specs=(whole,) * 2,
+        scratch_shapes=[VMEM((seq - 1, rows, cols), BF16), dma((seq - 1,)), dma((seq - 1,))],
+        compiler_params=pltpu.CompilerParams(vmem_limit_bytes=LIMIT, collective_id=2, has_side_effects=True),
+        name="out_back",
+    )(dy, w_out, o_own)
+
+
+class Reduce:
+    def __init__(self, here, dp, pieces, near, out, far, sems):
+        self.here, self.dp, self.pieces, self.near, self.out, self.far = here, dp, pieces, near, out, far
+        self.sems = sems
+
+    def to_near(self, t):
+        mate = other(self.here, 1, self.dp)
+        return send(self.pieces.at[other(mate, 2 * t, self.dp)], self.near.at[t], self.sems[2:], t, mate, "dp")
+
+    def to_far(self, t):
+        return send(self.out.at[t - 1], self.far.at[t - 1], self.sems[:2], t, other(self.here, 2 * t, self.dp), "dp")
+
+    def begin(self):
+        for t in reversed(range(self.dp // 2)):
+            self.to_near(t).start()
+
+    def pair(self, t):
+        return self.pieces[other(self.here, 2 * t, self.dp)].astype(F32) + self.near[t].astype(F32)
+
+    def middle(self):
+        for t in reversed(range(1, self.dp // 2)):
+            self.to_near(t).wait_recv()
+            self.out[t - 1] = self.pair(t).astype(BF16)
+            self.to_far(t).start()
+
+    def finish(self):
+        self.to_near(0).wait_recv()
+        total = self.pair(0)
+        for t in range(1, self.dp // 2):
+            self.to_far(t).wait_recv()
+            total = total + self.far[t - 1].astype(F32)
+        return total
+
+    def drain(self):
+        for t in range(self.dp // 2):
+            self.to_near(t).wait_send()
+        for t in range(1, self.dp // 2):
+            self.to_far(t).wait_send()
+
+    @staticmethod
+    def scratch(dp, rows, wide):
+        return [VMEM((dp // 2, rows, wide), BF16)] + [VMEM((dp // 2 - 1, rows, wide), BF16)] * 2
+
+    @staticmethod
+    def semaphores(dp):
+        return [pltpu.SemaphoreType.DMA((dp // 2,))] * 4
+
+
+def project_back_kernel(seq, dp, *refs):
+    refs = list(refs)
+    dq, dkv, gains, a_all, w, grad_out, x_ref, dx_ref, g_attn, xy_ref = refs[:10]
+    y_parts = refs[10:9 + seq]
+    (grad_x, out_ref, gwq_ref, gwkv_ref, gwo_ref, gain_out, acc, da, arrived, pieces, results, sums, sum_in,
+     q_near, q_out, q_far, o_near, o_out, o_far, rs_out, rs_in, q1, q2, q3, q4, o1, o2, o3, o4,
+     all_out, all_in) = refs[9 + seq:]
+    me, here = lax.axis_index("seq"), lax.axis_index("dp")
+    rows, width = x_ref.shape
+    mine = dq.shape[1]
+    depth = grad_out.shape[1]
+    half = rows // 2
+    orders = flips(seq)
+    red_q = Reduce(here, dp, pieces, q_near, q_out, q_far, (q1, q2, q3, q4))
+    red_o = Reduce(here, dp, grad_out, o_near, o_out, o_far, (o1, o2, o3, o4))
+
+    def chunk(k):
+        return pl.ds(pl.multiple_of(other(me, k, seq) * rows, rows), rows)
+
+    def pass_on(part, step, k):
+        return send(acc.at[k, pl.ds(part * half, half), :], arrived.at[part, k - 1], (rs_out, rs_in),
+                    (part, step, k), other(me, orders[part][step], seq))
+
+    def sent_at(part, step):
+        before = sum(orders[part][:step])
+        return [k for k in range(1, seq) if k & orders[part][step] and not k & before]
+
+    def to_all(j):
+        peer = other(me, j, seq)
+        return [send(results.at[me], results.at[me], (all_out, all_in), (0, j - 1), peer),
+                send(sums, sum_in.at[j - 1], (all_out, all_in), (1, j - 1), peer)]
+
+    def partial_da(k):
+        return nt(dq[chunk(k), :], w[:, :mine]) + nt(dkv[chunk(k), :], w[:, mine:])
+
+    greet(seq, me, dp, here)
+    red_o.begin()
+    for k in reversed(range(1, seq)):
+        acc[k] = partial_da(k).astype(BF16)
+        for part in range(2):
+            if k in sent_at(part, 0):
+                pass_on(part, 0, k).start()
+    da[...] = partial_da(0)
+    red_o.middle()
+    for d in range(2):
+        grads = dq if d == 0 else dkv
+        total = tn(a_all[0], grads[chunk(0), :])
+        for k in range(1, seq):
+            total = total + tn(a_all[k], grads[chunk(k), :])
+        pieces[:, :depth, d * mine:(d + 1) * mine] = total.astype(BF16).reshape(dp, depth, mine)
+        sum8 = jnp.sum(gains[8 * d:8 * d + 8, :], axis=0, keepdims=True)
+        pieces[:, depth:, d * mine:(d + 1) * mine] = jnp.broadcast_to(sum8[None], (dp, 16, mine)).astype(BF16)
+    red_q.begin()
+    out = xy_ref[...]
+    for y in y_parts:
+        out = out + y[...].astype(F32)
+    out_ref[...] = out.astype(BF16)
+    red_q.middle()
+    for step in range(len(orders[0])):
+        for part in range(2):
+            at = pl.ds(part * half, half)
+            for k in sent_at(part, step):
+                pass_on(part, step, k).wait_recv()
+                target = k - orders[part][step]
+                if target == 0:
+                    da[at, :] += arrived[part, k - 1].astype(F32)
+                else:
+                    acc[target, at, :] = (acc[target, at, :].astype(F32) + arrived[part, k - 1].astype(F32)).astype(BF16)
+            if step + 1 < len(orders[0]):
+                for k in sent_at(part, step + 1):
+                    pass_on(part, step + 1, k).start()
+        if step == 0:
+            sum_o = red_o.finish()
+            sums[...] = sum_o.astype(BF16)
+            results[me] = red_q.finish().astype(BF16)
+            for j in reversed(range(1, seq)):
+                for copy in to_all(j):
+                    copy.start()
+    x = x_ref[...].astype(F32)
+    factor = lax.rsqrt(jnp.mean(x * x, axis=-1, keepdims=True) + EPS)
+    unit = x * factor
+    weighted = da[...] * g_attn[0:1, :]
+    grad_x[...] = dx_ref[...] + factor * (weighted - unit * jnp.mean(weighted * unit, axis=-1, keepdims=True))
+    gwo = sums[...].astype(F32)
+    for j in range(1, seq):
+        for copy in to_all(j):
+            copy.wait_recv()
+        gwo = gwo + sum_in[j - 1].astype(F32)
+    gwo_ref[...] = gwo
+    gain_total = jnp.zeros((16, 2 * mine), F32)
+    for j in range(seq):
+        gwq_ref[:, j * mine:(j + 1) * mine] = results[j, :depth, :mine].astype(F32)
+        gwkv_ref[:, j * mine:(j + 1) * mine] = results[j, :depth, mine:].astype(F32)
+        gain_total = gain_total + results[j, depth:, :].astype(F32)
+    gain_out[...] = gain_total
+    for j in range(1, seq):
+        for copy in to_all(j):
+            copy.wait_send()
+    for part in range(2):
+        for step in range(len(orders[0])):
+            for k in sent_at(part, step):
+                pass_on(part, step, k).wait_send()
+    red_q.drain()
+    red_o.drain()
+
+
+def project_back(dq, dkv, gains, a_all, w_qkv, grad_out, x, dx, g_attn, xy, y_parts):
+    seq, rows, width = a_all.shape
+    dp, depth, _ = grad_out.shape
+    mine = dq.shape[1]
+    whole = pl.BlockSpec(memory_space=VMEM)
+    shape = jax.ShapeDtypeStruct
+    dma = pltpu.SemaphoreType.DMA
+    steps = seq.bit_length() - 1
+    return pl.pallas_call(
+        functools.partial(project_back_kernel, seq, dp),
+        out_shape=(shape((rows, width), F32), shape((rows, width), BF16), shape((depth, seq * mine), F32),
+                   shape((depth, seq * mine), F32), shape((depth, width), F32), shape((16, 2 * mine), F32)),
+        in_specs=[whole] * (9 + seq),
+        out_specs=(whole,) * 6,
+        scratch_shapes=[
+            VMEM((seq, rows, width), BF16),
+            VMEM((rows, width), F32),
+            VMEM((2, seq - 1, rows // 2, width), BF16),
+            VMEM((dp, depth + 16, 2 * mine), BF16),
+            VMEM((seq, depth + 16, 2 * mine), BF16),
+            VMEM((depth, width), BF16),
+            VMEM((seq - 1, depth, width), BF16),
+            *Reduce.scratch(dp, depth + 16, 2 * mine), *Reduce.scratch(dp, depth, width),
+            dma((2, steps, seq)), dma((2, steps, seq)),
+            *Reduce.semaphores(dp), *Reduce.semaphores(dp), dma((2, seq - 1)), dma((2, seq - 1)),
+        ],
+        compiler_params=pltpu.CompilerParams(vmem_limit_bytes=LIMIT, collective_id=3, has_side_effects=True),
+        name="project_back",
+    )(dq, dkv, gains, a_all, w_qkv, grad_out, x, dx, g_attn, xy, *y_parts)
+
+
+def share_kernel(seq, own, grads_ref, extra_ref, slots, send_sem, recv_sem):
+    me = lax.axis_index("seq")
+    gather = Gather(me, seq, own, slots, (send_sem, recv_sem))
+    part = grads_ref.shape[2]
+    greet(seq, me)
+    gather.begin()
+    extra = own[3 * part:, :].astype(F32)
+    for k in range(3):
+        grads_ref[k, me] = own[k * part:(k + 1) * part, :].astype(F32)
+    gather.forward()
+    for j in range(1, seq):
+        gather.finish(j)
+        for k in range(3):
+            grads_ref[k, other(me, j, seq)] = slots[j, k * part:(k + 1) * part, :].astype(F32)
+        extra = extra + slots[j, 3 * part:, :].astype(F32)
+    extra_ref[...] = extra
+    gather.drain()
+
+
+def share(own, seq, part):
+    rows, width = own.shape
+    spare = rows - 3 * part
+    whole = pl.BlockSpec(memory_space=VMEM)
+    shape = jax.ShapeDtypeStruct
+    return pl.pallas_call(
+        functools.partial(share_kernel, seq),
+        out_shape=(shape((3, seq, part, width), F32), shape((spare, width), F32)),
+        in_specs=[whole],
+        out_specs=(whole,) * 2,
+        scratch_shapes=[VMEM((seq, rows, width), BF16), Gather.semaphores(seq), Gather.semaphores(seq)],
+        compiler_params=pltpu.CompilerParams(vmem_limit_bytes=LIMIT, collective_id=4, has_side_effects=True),
+        name="share",
+    )(own)
+
+
+def exchanged(u, bits, seq):
+    return lax.ppermute(u, "seq", [(i, i ^ bits) for i in range(seq)])
 
 
 def place_tables(segment_row, order_row):
@@ -420,86 +976,55 @@
     sizes = (norm_attn.shape[0], norm_ffn.shape[0], gain_query.shape[0], gain_key.shape[0])
     gain_rows = jnp.pad(gain_row[None, :], ((0, 15), (0, 2 * mine - gain_row.shape[0])))
     packed = jnp.concatenate([jnp.concatenate([my_columns(w_query), my_columns(w_keyval)], 1), gain_rows], 0)
-    packed = lax.all_gather(packed, "dp", axis=0)
-    w_qkv = packed[:, :depth].reshape(width, 2 * mine)
-    gains = packed[:, depth].astype(F32)
-    g_attn, g_ffn, g_query, g_key = (
-        gains[:, sum(sizes[:i]):sum(sizes[:i + 1])].reshape(-1) for i in range(4))
-    out_w = lax.all_gather(w_out, "dp", axis=0, tiled=True)
-
     def my_rows(u):
         return lax.dynamic_slice_in_dim(u, me * part, part, 0)
 
-    ffn_w = jnp.stack([my_rows(w_gate.T), my_rows(w_up.T), my_rows(w_down)])
+    ffn_w = jnp.concatenate([my_rows(w_gate.T), my_rows(w_up.T), my_rows(w_down), w_out])
     ffn_w = lax.all_gather(ffn_w, "dp", axis=0)
-    pieces = dp if part % 16 == 0 else 1
-    if pieces == 1:
-        ffn_w = jnp.moveaxis(ffn_w, 0, 1).reshape(1, 3, dp * part, width)
+    in_pieces = part % 16 == 0
+    if not in_pieces:
+        body = jnp.moveaxis(ffn_w[:, :3 * part].reshape(dp, 3, part, width), 0, 1)
+        ffn_w = jnp.concatenate([body.reshape(-1, width), ffn_w[:, 3 * part:].reshape(-1, width)])[None]
 
     inv, first, starts, cos, sin = place_tables(segments[0], blocks[0])
     starts_down = jnp.broadcast_to(starts[:, None], (total_rows, BLOCK))
     starts_across = jnp.broadcast_to(starts.reshape(-1, 1, BLOCK), (total_rows // BLOCK, 8, BLOCK))
-    gain_q = jnp.tile(g_query, mine // HEAD)[None, :]
-    gain_kv = jnp.tile(jnp.concatenate([g_key, jnp.ones_like(g_key)]), mine // PAIR)[None, :]
-
-    x_all = lax.all_gather(tokens_in, "seq", axis=0, tiled=True)
-    gy_all = lax.all_gather(cotangent, "seq", axis=0, tiled=True)
-    hidden = x_all.astype(F32)
-    a_all = (hidden * norm_factor(hidden) * g_attn).astype(BF16)
-    qkv = nn(a_all, w_qkv)
-    q_raw, kv_raw = qkv[:, :mine], qkv[:, mine:]
+    x_all, a_all, q_raw, kv_raw, w_qkv, g_attn, g_ffn, gain_q, gain_kv = project(
+        tokens_in, packed, seq, dp, sizes)
+    gy, q_raw = lax.optimization_barrier((cotangent, q_raw))
+    gy_all = [gy] + [exchanged(gy, k, seq) for k in range(1, seq)]
     o, qs, kvs, linv = attend(inv, first, q_raw, kv_raw, cos, sin, starts_down, gain_q, gain_kv)
 
-    o_all = lax.all_gather(o, "seq", axis=1, tiled=True)
-    y_part, db_part, ffn_grads = ffn(x_all, o_all, gy_all, out_w, g_ffn[None, :], ffn_w, min(rows, 512))
-    d_b = lax.psum_scatter(db_part, "seq", scatter_dimension=0, tiled=True).astype(F32)
-    y = lax.psum_scatter(y_part, "seq", scatter_dimension=0, tiled=True).astype(F32)
-
-    if pieces == 1:
-        ffn_grads = jnp.moveaxis(ffn_grads.reshape(3, dp, part, width), 1, 0)
+    ffn_grads, d_x1, d_y, x1_y, out_w, o_own, *y_parts = ffn(o, x_all, gy_all, g_ffn, ffn_w)
+    if not in_pieces:
+        extra = jnp.broadcast_to(ffn_grads[0, None, -16:], (dp, 16, width))
+        body = jnp.moveaxis(ffn_grads[0, :-16].reshape(3, dp, part, width), 1, 0)
+        ffn_grads = jnp.concatenate([body.reshape(dp, 3 * part, width), extra], 1)
+        ffn_grads = jnp.pad(ffn_grads, ((0, 0), (0, -ffn_grads.shape[1] % 32), (0, 0)))
     ffn_grads = lax.psum_scatter(ffn_grads, "dp", scatter_dimension=0, tiled=True)[0]
-    ffn_grads = lax.all_gather(ffn_grads, "seq", axis=1, tiled=True).astype(F32)
-
-    x_own = tokens_in.astype(F32)
-    o_own = lax.dynamic_slice_in_dim(o_all, me * rows, rows, 0)
-    x1 = x_own + nn(o_own, out_w)
-    output = (x1 + y).astype(BF16)
-    d_x1, d_g_ffn = norm_back(x1, g_ffn, d_b)
-    d_x1 = d_x1 + cotangent.astype(F32)
-    d_y = d_x1.astype(BF16)
-    grad_out = tn(o_own, d_y)
-    d_o = nt(d_y, out_w).astype(BF16)
-    d_o = lax.all_to_all(d_o, "seq", split_axis=1, concat_axis=0, tiled=True)
-
+
+    d_o, grad_out = out_back(d_y, out_w, o_own)
+    d_o, y_parts = lax.optimization_barrier((d_o, y_parts))
+    y_parts = [exchanged(y_parts[k - 1], k, seq) for k in range(1, seq)]
     dq_raw, dkv_raw, gain_sums = attend_back(
         inv, first, q_raw, kv_raw, cos, sin, starts_across, gain_q, gain_kv, o, d_o, qs, kvs, linv)
-    d_qkv = jnp.concatenate([dq_raw, dkv_raw], 1)
-    da_part = nt(d_qkv, w_qkv).astype(BF16)
-    grad_qkv = tn(a_all, d_qkv)
-    d_a = lax.psum_scatter(da_part, "seq", scatter_dimension=0, tiled=True).astype(F32)
-    back, d_g_attn = norm_back(x_own, g_attn, d_a)
-    grad_tokens = d_x1 + back
-    q_sums, k_sums = jnp.sum(gain_sums[:8], 0), jnp.sum(gain_sums[8:], 0)
-    d_g_query = jnp.sum(q_sums.reshape(-1, HEAD), 0)
-    d_g_key = jnp.sum(k_sums.reshape(-1, PAIR)[:, :HEAD], 0)
-
-    small = jnp.concatenate(
-        [u.reshape(dp, -1) for u in (d_g_attn, d_g_ffn, d_g_query, d_g_key)], 1)
-    small = jnp.pad(small, ((0, 0), (0, width - small.shape[1])))[:, None, :]
-    small = jnp.pad(small, ((0, 0), (0, 15), (0, 0)))
-    bundle = jnp.concatenate(
-        [grad_qkv.reshape(dp, -1, width), grad_out.reshape(dp, -1, width), small], 1).astype(BF16)
-    bundle = lax.psum_scatter(bundle, "dp", scatter_dimension=0, tiled=True)[0]
-    bundle = lax.all_gather(bundle, "seq", axis=0).astype(F32)
-    n_qkv = depth * 2 * mine // width
-    g_qkv = bundle[:, :n_qkv].reshape(seq, depth, 2, mine)
-    grad_wq = jnp.moveaxis(g_qkv[:, :, 0], 0, 1).reshape(depth, width)
-    grad_wkv = jnp.moveaxis(g_qkv[:, :, 1], 0, 1).reshape(depth, width)
-    rest = jnp.sum(bundle[:, n_qkv:], 0)
-    grad_wout = rest[:depth]
-    tail = rest[depth]
-    grads = [tail[sum(sizes[:i]):sum(sizes[:i + 1])] for i in range(4)]
-    return (output, grad_tokens, grads[0], grad_wq, grad_wkv, grads[2], grads[3], grad_wout, grads[1],
+    grad_tokens, output, grad_wq, grad_wkv, grad_wout, gain_sums = project_back(
+        dq_raw, dkv_raw, gain_sums, a_all, w_qkv, grad_out.reshape(dp, depth, width), tokens_in, d_x1, g_attn,
+        x1_y, y_parts)
+    ffn_grads, extra = share(ffn_grads, seq, part)
+    ffn_grads = ffn_grads.reshape(3, seq * part, width)
+
+    here = lax.axis_index("dp")
+
+    def owned(vector, size):
+        return lax.dynamic_slice_in_dim(vector, here * size, size)
+
+    d_g_ffn = owned(extra[0], sizes[1])
+    d_g_query = owned(jnp.sum(gain_sums[0, :mine].reshape(-1, HEAD), 0), sizes[2])
+    d_g_key = owned(jnp.sum(gain_sums[0, mine:].reshape(-1, PAIR)[:, :HEAD], 0), sizes[3])
+    d_g_attn = jnp.sum(grad_wq * w_query.astype(F32) + grad_wkv * w_keyval.astype(F32), axis=1)
+    d_g_attn = d_g_attn / norm_attn.astype(F32)
+    return (output, grad_tokens, d_g_attn, grad_wq, grad_wkv, d_g_query, d_g_key, grad_wout, d_g_ffn,
             ffn_grads[0].T, ffn_grads[1].T, ffn_grads[2])
 
 

time: 832 us -> 409 us (0.49)
  waiting for transfers between devices: 559 us -> 4.84 us
  Pallas kernels: 159 us -> 350 us
  matrix products: 21.6 us -> 0 us
  other arithmetic: 31.8 us -> 11.8 us
  blocking collectives: 17.6 us -> 0 us
  local copies, waits for them, and re-layouts: 27.5 us -> 18.8 us
    all_gather x7 -> x0, waiting for transfers between devices: 227 us -> none  [the longest x1 52.9 us: shards(): o_all = lax.all_gather(o, 'seq', axis=1, tiled=True)]
    pallas_call x1 -> x5, Pallas kernels: 77.3 us -> 274 us  [the longest x1 101 us: ffn(): pl.pallas_call(functools.partial(ffn_kernel, seq, tile), out_shape=(jax.S...]
    reduce_scatter x4 -> x0, waiting for transfers between devices: 181 us -> none  [the longest x1 54 us: shards(): lax.psum_scatter(y_part, 'seq', scatter_dimension=0, tiled=True).astype(F32)]
    reduce_scatter x1, waiting for transfers between devices: 74 us -> 0.01 us  [shards(): lax.psum_scatter(ffn_grads, 'dp', scatter_dimension=0, tiled=True)[0]]
    all_gather x1, waiting for transfers between devices: 73.4 us -> 0.2 us  [shards(): ffn_w = lax.all_gather(ffn_w, 'dp', axis=0)]
    dot_general x6 -> x0, matrix products: 21.6 us -> none  [the longest x2 10.2 us: tn(): lax.dot_general(a, b, (((0,), (0,)), ((), ())), preferred_element_type=F32)]
    all_to_all x1 -> x0, blocking collectives: 17.6 us -> none  [shards(): d_o = lax.all_to_all(d_o, 'seq', split_axis=1, concat_axis=0, tiled=True)]
  transfers between devices with their start and end apart: 13 -> 8, of which waited for: 12 -> 3; matrix products, arithmetic and copies ran while one was open for 7% -> 3% of each run, Pallas kernels for 5% -> 52%
where the time goes in v2:
time: 409 us; the launch traced here: 407 us
  Pallas kernels  350 us (86%)
  local copies, waits for them, and re-layouts  18.8 us (5%)
  between operations  14.3 us (3%)
  other arithmetic  11.8 us (3%)
  starting transfers between devices  7.19 us (2%)
  waiting for transfers between devices  4.84 us (1%)
    pallas_call x1, Pallas kernels, ffn(): pl.pallas_call(functools.partial(ffn_kernel, seq, tile), out_shape=(jax.S...  101 us
    pallas_call x1, Pallas kernels, project_back(): pl.pallas_call(functools.partial(project_back_kernel, seq, dp), out_shape...  68.7 us
    pallas_call x1, Pallas kernels, project(): pl.pallas_call(functools.partial(project_kernel, seq, dp, sizes), out_sha...  48.2 us
    pallas_call x1, Pallas kernels, attend_back(): pl.pallas_call(functools.partial(attend_back_kernel, groups), out_shape=(...  41.1 us
    pallas_call x1, Pallas kernels, share(): pl.pallas_call(functools.partial(share_kernel, seq), out_shape=(shape((3,...  36.7 us
    pallas_call x1, Pallas kernels, attend(): pl.pallas_call(functools.partial(attend_kernel, groups), out_shape=(jax.S...  34.9 us
    pallas_call x1, Pallas kernels, out_back(): pl.pallas_call(functools.partial(out_back_kernel, seq), out_shape=(jax.Sh...  19.3 us
  transfers between devices with their start and end apart: 8, of which 3 were waited for; matrix products, arithmetic and copies ran while one was open for 3% of the time, Pallas kernels for 52%

profile of v2, /device:TPU:0, one launch (start us, length us, event | category | flops | bytes accessed | tf_op | source)
XLA Modules:
  0.0 406.5 jit_solution(11162964009787252257)
XLA Ops:
  7.2 1.0 constant_dynamic-slice_fusion.1
  8.3 1.2 dynamic-slice_bitcast_fusion
  9.5 2.0 pad_maximum_fusion
  12.4 48.2 %project.1 = (bf16[4,512,1024]{2,1,0:T(8,128)(2,1)}, bf16[4,512,1024]{2,1,0:T(8,128)(2,1)}, f32[2048,256]{1,0:T(8,128)}, f32[2048,256]{1,0:T(8,128)}, bf16[1024,...) custom-call(bf16[512,1024]{1,0:T(8,128)(2,1)} %refs_6_.1, ...), custom_call_target="tpu_custom_call" | custom-call | tf_op jit(solution)/shard_map/project/pallas_call | solution.py:458
  60.6 1.6 collective-permute-start
  62.7 1.5 collective-permute-start.2
  65.7 5.5 %fusion = (f32[2048,128]{1,0:T(8,128)}, f32[2048,128]{1,0:T(8,128)}) fusion(f32[128]{0:T(128)S(1)} %get-tuple-element.101, f32[128]{0:T(128)S(1)} %get-tuple-element.102, f32[2048]{0:T(1024)S(1)} %subtract_convert_fusion), kind=kLoop, calls=%fused_computation.3 | loop fusion | flops 524288 | bytes 2106368 | tf_op jit(solution)/shard_map/mul | solution.py:959
  71.3 1.3 broadcast_in_dim.62.starts
  72.6 34.9 %attend.1 = (bf16[2048,256]{1,0:T(8,128)(2,1)}, bf16[2,4096,128]{2,1,0:T(8,128)(2,1)}, bf16[2,2176,128]{2,1,0:T(8,128)(2,1)}, f32[2,16,8,256]{3,2,1,0:T(8,128)}) custom-call(s32[16]{0:T(128)} %select_reduce_fusion.1.inv, s32[16]{0:T(128)} %and_select_fusion.2.first, f32[2048,256]{1,0:T(8,128)} %get-tuple-element.54.q_raw, ...), custom_call_target="tpu_custom_call" | custom-call | tf_op jit(solution)/shard_map/attend/pallas_call | solution.py:141
  107.5 1.3 collective-permute-done.1.refs_6_
  109.0 100.9 %ffn.1 = (bf16[8,448,1024]{2,1,0:T(8,128)(2,1)}, f32[512,1024]{1,0:T(8,128)}, bf16[512,1024]{1,0:T(8,128)(2,1)}, f32[512,1024]{1,0:T(8,128)}, bf16[1024,1024]{1,...) custom-call(bf16[2048,256]{1,0:T(8,128)(2,1)} %get-tuple-element.58., ...), custom_call_target="tpu_custom_call" | custom-call | tf_op jit(solution)/shard_map/ffn/pallas_call | solution.py:652
  209.9 19.3 %out_back.1 = (bf16[2048,256]{1,0:T(8,128)(2,1)}, bf16[1024,1024]{1,0:T(8,128)(2,1)}) custom-call(bf16[512,1024]{1,0:T(8,128)(2,1)} %get-tuple-element.62.dy_ref, bf16[1024,1024]{1,0:T(8,128)(2,1)} %get-tuple-element.63.w_out, bf16[4,512,256]{2,1,0:T(8,128)(2,1)} %get-tuple-element.64.o_own), custom_call_target="tpu_custom_call" | custom-call | tf_op jit(solution)/shard_map/out_back/pallas_call | solution.py:710
  229.2 0.9 collective-permute-start.3
  230.1 1.2 collective-permute-start.4
  231.3 1.4 collective-permute-start.5
  233.4 41.1 %attend_back.1 = (bf16[2048,256]{1,0:T(8,128)(2,1)}, bf16[2048,256]{1,0:T(8,128)(2,1)}, f32[16,256]{1,0:T(8,128)}) custom-call(s32[16]{0:T(128)} %select_reduce_fusion.1.inv, s32[16]{0:T(128)} %and_select_fusion.2.first, f32[2048,256]{1,0:T(8,128)} %get-tuple-element.54.q_raw, f32[2048,256]{1,0:T(8,128)} %get-tuple-element.55.kv_raw, ...), custom_call_target="tpu_custom_call" | custom-call | tf_op jit(solution)/shard_map/attend_back/pallas_call | solution.py:258
  274.4 3.3 collective-permute-done.4.refs_11_
  277.7 68.7 %project_back.1 = (f32[512,1024]{1,0:T(8,128)}, bf16[512,1024]{1,0:T(8,128)(2,1)}, f32[128,1024]{1,0:T(8,128)}, f32[128,1024]{1,0:T(8,128)}, f32[128,1024]{1,0:T(8,128)}, /*index=5*/f32[16,512]{1,0:T(8,128)}) custom-call(bf16[2048,256]{1,0:T(8,128)(2,1)} %get-tuple-element.73.refs_0_, bf16[2048,256]{1,0:T(8,128)(2,1)} %get-tuple-element.74.refs_1_, ...), custom_call_target="tpu_custom_call" | custom-call | tf_op jit(solution)/shard_map/project_back/pallas_call | solution.py:883
  348.5 1.4 add_reduce_fusion
  350.4 36.7 %share.1 = (f32[3,4,144,1024]{3,2,1,0:T(8,128)}, f32[16,1024]{1,0:T(8,128)}) custom-call(bf16[448,1024]{1,0:T(8,128)(2,1)} %bitcast.25), custom_call_target="tpu_custom_call" | custom-call | tf_op jit(solution)/shard_map/share/pallas_call | solution.py:930
  387.1 6.4 %fusion.7 = (f32[1,4,144,1024]{3,2,1,0:T(8,128)}, f32[1,4,144,1024]{3,2,1,0:T(8,128)}, f32[1,4,144,1024]{3,2,1,0:T(8,128)}) fusion(f32[3,4,144,1024]{3,2,1,0:T(8,128)} %get-tuple-element.93), kind=kLoop, calls=%fused_computation.36 | loop fusion | bytes 14155776 | tf_op jit(solution)/shard_map/slice | solution.py:1028
  393.5 0.9 slice.31
  395.0 1.0 copy.32
  395.9 1.3 copy.33
  (61 shorter events, 9.4 us)
Async XLA Ops:
  7.2 101.8 %all-gather.3.cloned.1.call-start = ((), (), s32[]{:S(2)}) async-start(), calls=%async_computation.2 | async-start | bytes 10321920 | tf_op jit(solution)/shard_map/all_gather | solution.py:983
  8.2 3.4 copy-start.8
  8.2 3.4 copy-start.9
  8.2 3.4 copy-start.10
  8.3 3.4 copy-start.11
  8.3 3.5 copy-start.5
  8.3 3.4 copy-start.6
  9.4 54.7 %copy-start.12 = (s32[1,16]{1,0:T(1,128)S(1)}, s32[1,16]{1,0:T(1,128)}, u32[]{:S(2)}) copy-start(s32[1,16]{1,0:T(1,128)} %param.27) | copy-start | bytes 196
  9.5 55.3 %copy-start.7 = (s32[1,2048]{1,0:T(1,128)S(1)}, s32[1,2048]{1,0:T(1,128)}, u32[]{:S(2)}) copy-start(s32[1,2048]{1,0:T(1,128)} %param.26) | copy-start | bytes 24580
  11.5 338.9 %reduce-scatter.2.cloned.1.call-start = ((), (), s32[]{:S(2)}) async-start(), calls=%async_computation.1 | async-start | bytes 8257536 | tf_op jit(solution)/shard_map/reduce_scatter | solution.py:1004
  60.6 46.9 %collective-permute-start = (bf16[512,1024]{1,0:T(8,128)(2,1)}, bf16[512,1024]{1,0:T(8,128)(2,1)}, u32[]{:S(2)}, u32[]{:S(2)}) collective-permute-start(bf16[512,1024]{1,0:T(8,128)(2,1)} %refs_4_), channel_id=1, source_target_pairs={{0,1},{1,0},{2,3},{3,2},{4,5},{5,4},{6,7},{7,6},{8,9},{9,8},{10,11... | collective-permute-start | bytes 3145736 | tf_op jit(solution)/shard_map/ppermute | solution.py:942
  62.2 46.6 %collective-permute-start.1 = (bf16[512,1024]{1,0:T(8,128)(2,1)}, bf16[512,1024]{1,0:T(8,128)(2,1)}, u32[]{:S(2)}, u32[]{:S(2)}) collective-permute-start(bf16[512,1024]{1,0:T(8,128)(2,1)} %refs_4_), channel_id=1, source_target_pairs={{0,2},{1,3},{2,0},{3,1},{4,6},{5,7},{6,4},{7,5},{8,10},{9,11},{10,... | collective-permute-start | bytes 3145736 | tf_op jit(solution)/shard_map/ppermute | solution.py:942
  62.7 46.1 %collective-permute-start.2 = (bf16[512,1024]{1,0:T(8,128)(2,1)}, bf16[512,1024]{1,0:T(8,128)(2,1)}, u32[]{:S(2)}, u32[]{:S(2)}) collective-permute-start(bf16[512,1024]{1,0:T(8,128)(2,1)} %refs_4_), channel_id=1, source_target_pairs={{0,3},{1,2},{2,1},{3,0},{4,7},{5,6},{6,5},{7,4},{8,11},{9,10},{10,... | collective-permute-start | bytes 3145736 | tf_op jit(solution)/shard_map/ppermute | solution.py:942
  229.2 45.3 %collective-permute-start.3 = (bf16[512,1024]{1,0:T(8,128)(2,1)}, bf16[512,1024]{1,0:T(8,128)(2,1)}, u32[]{:S(2)}, u32[]{:S(2)}) collective-permute-start(bf16[512,1024]{1,0:T(8,128)(2,1)} %get-tuple-element.82), channel_id=1, source_target_pairs={{0,1},{1,0},{2,3},{3,2},{4,5},{5,4},{6,7},{7,6},{8,9},{9,8},{10,11... | collective-permute-start | bytes 3145736 | tf_op jit(solution)/shard_map/ppermute | solution.py:942
  230.1 47.6 %collective-permute-start.4 = (bf16[512,1024]{1,0:T(8,128)(2,1)}, bf16[512,1024]{1,0:T(8,128)(2,1)}, u32[]{:S(2)}, u32[]{:S(2)}) collective-permute-start(bf16[512,1024]{1,0:T(8,128)(2,1)} %get-tuple-element.83), channel_id=1, source_target_pairs={{0,2},{1,3},{2,0},{3,1},{4,6},{5,7},{6,4},{7,5},{8,10},{9,11},{10,... | collective-permute-start | bytes 3145736 | tf_op jit(solution)/shard_map/ppermute | solution.py:942
  231.3 46.4 %collective-permute-start.5 = (bf16[512,1024]{1,0:T(8,128)(2,1)}, bf16[512,1024]{1,0:T(8,128)(2,1)}, u32[]{:S(2)}, u32[]{:S(2)}) collective-permute-start(bf16[512,1024]{1,0:T(8,128)(2,1)} %get-tuple-element.84), channel_id=1, source_target_pairs={{0,3},{1,2},{2,1},{3,0},{4,7},{5,6},{6,5},{7,4},{8,11},{9,10},{10,... | collective-permute-start | bytes 3145736 | tf_op jit(solution)/shard_map/ppermute | solution.py:942
  387.1 7.9 %copy-start.3 = (bf16[512,1024]{1,0:T(8,128)(2,1)S(1)}, bf16[512,1024]{1,0:T(8,128)(2,1)}, u32[]{:S(2)}) copy-start(bf16[512,1024]{1,0:T(8,128)(2,1)} %get-tuple-element.119) | copy-start | bytes 3145732
  393.5 2.4 copy-start
  395.9 1.4 copy-start.2
  395.9 2.2 copy-start.1
  397.3 1.6 copy-start.4
Sparse Core Ops, SparseCore 0:
  11.7 97.2 all-gather.2
  210.0 78.5 reduce-scatter.1

commit v3 on v2

--- a/solution.py
+++ b/solution.py
@@ -103,7 +103,8 @@
     def one_block(p, _):
         base = p * BLOCK
         row = base + lax.broadcasted_iota(jnp.int32, (BLOCK, SPAN), 0)
-        start = tile_lanes(starts[pl.ds(pl.multiple_of(base, BLOCK), BLOCK), :], SPAN // BLOCK)
+        start = jnp.transpose(jnp.broadcast_to(starts[pl.ds(p, 1), :].astype(F32), (BLOCK, BLOCK)))
+        start = tile_lanes(start.astype(jnp.int32), SPAN // BLOCK)
         begin = first[p]
 
         def step(i, totals):
@@ -181,7 +182,7 @@
         rows = pl.ds(pl.multiple_of(inv[p] * BLOCK, BLOCK), BLOCK)
         queries = pl.ds(pl.multiple_of(p * SPAN, SPAN), SPAN)
         place_q = base + lanes((SPAN, SPAN)) % BLOCK
-        start = jnp.broadcast_to(tile_lanes(starts[p, 0:1, :], 2), (SPAN, SPAN))
+        start = jnp.broadcast_to(tile_lanes(starts[pl.ds(p, 1), :], 2), (SPAN, SPAN))
         begin = first[p]
         grads, dots = [], []
         for g in range(groups):
@@ -403,25 +404,69 @@
     return nn(piece[:, group * PAIR:(group + 1) * PAIR], hot.astype(BF16))
 
 
-def project_kernel(seq, dp, sizes, x_ref, pack_ref, x_all, a_all, q_raw, kv_raw, w_ref, g_attn, g_ffn, g_q, g_kv,
-                   packs, x_send, x_recv, far_out, far_in, near_out, near_in, own_sem):
+def project_kernel(seq, dp, sizes, x_ref, wq_hbm, wkv_hbm, gain_ref, seg_ref,
+                   x_hbm, a_hbm, q_hbm, kv_hbm, cos_hbm, sin_hbm, w_ref, g_attn, g_ffn, g_q, g_kv, starts_ref,
+                   x_all, a_s, q_s, kv_s, cos_s, sin_s, start_s, pack_s, packs,
+                   x_send, x_recv, far_out, far_in, near_out, near_in, in_sems, out_sems, table_sems):
     me, here = lax.axis_index("seq"), lax.axis_index("dp")
     rows, width = x_ref.shape
-    depth = pack_ref.shape[0] - 16
-    mine = q_raw.shape[1]
+    depth = wq_hbm.shape[0]
+    mine = q_s.shape[2]
     gather = Gather(me, seq, x_ref, x_all, (x_send, x_recv))
-    pack = Spread(here, dp, pack_ref, packs, (far_out, far_in, near_out, near_in))
+    pack = Spread(here, dp, pack_s, packs, (far_out, far_in, near_out, near_in))
+    columns = pl.ds(pl.multiple_of(me * mine, mine), mine)
+    loads = [pltpu.make_async_copy(wq_hbm.at[:, columns], pack_s.at[:depth, :mine], in_sems.at[0]),
+             pltpu.make_async_copy(wkv_hbm.at[:, columns], pack_s.at[:depth, mine:], in_sems.at[1]),
+             pltpu.make_async_copy(gain_ref, pack_s.at[depth:, :], in_sems.at[2])]
+    for load in loads:
+        load.start()
+
+    def chunk(k):
+        return pl.ds(pl.multiple_of(other(me, k, seq) * rows, rows), rows)
+
+    def stores(k):
+        return [pltpu.make_async_copy(x_ref if k == 0 else x_all.at[k], x_hbm.at[k], out_sems.at[0, k]),
+                pltpu.make_async_copy(a_s.at[k], a_hbm.at[k], out_sems.at[1, k]),
+                pltpu.make_async_copy(q_s.at[k], q_hbm.at[chunk(k), :], out_sems.at[2, k]),
+                pltpu.make_async_copy(kv_s.at[k], kv_hbm.at[chunk(k), :], out_sems.at[3, k])]
+
     greet(seq, me, dp, here)
+    gather.begin()
+    for load in loads:
+        load.wait()
     pack.begin()
-    gather.begin()
-    copies = [pltpu.make_async_copy(x_ref, x_all.at[0], own_sem.at[0]),
-              pltpu.make_async_copy(pack_ref, packs.at[here], own_sem.at[1])]
-    for copy in copies:
+    own = pltpu.make_async_copy(pack_s, packs.at[here], in_sems.at[3])
+    own.start()
+
+    seg = seg_ref[...]
+    starts = jnp.zeros(seg.shape, F32)
+    for doc in range(1, MOST_DOCS):
+        begin = jnp.sum(jnp.where(seg < doc, 1.0, 0.0))
+        starts = jnp.maximum(starts, jnp.where(seg >= doc, begin, 0.0))
+    start_s[...] = starts
+    starts_ref[...] = starts.astype(jnp.int32)
+    lane = lanes((1, PAIR))
+    frequency = jnp.exp((lane % (HEAD // 2)).astype(F32) * (-2.0 * math.log(THETA) / HEAD))
+    sign = jnp.where(lane % HEAD < HEAD // 2, -1.0, 1.0)
+
+    def table(p, _):
+        at = pl.ds(pl.multiple_of(p * BLOCK, BLOCK), BLOCK)
+        start = jnp.transpose(jnp.broadcast_to(start_s[pl.ds(p, 1), :], (BLOCK, BLOCK)))
+        place = (p * BLOCK + lax.broadcasted_iota(jnp.int32, (BLOCK, PAIR), 0)).astype(F32)
+        turned = (place - start) * frequency
+        cos_s[at, :] = jnp.cos(turned)
+        sin_s[at, :] = jnp.sin(turned) * sign
+        return 0
+
+    lax.fori_loop(0, seg.shape[0], table, 0)
+    tables = [pltpu.make_async_copy(cos_s, cos_hbm, table_sems.at[0]),
+              pltpu.make_async_copy(sin_s, sin_hbm, table_sems.at[1])]
+    for copy in tables:
         copy.start()
     pack.forward()
     gather.forward()
     pack.finish()
-    copies[1].wait()
+    own.wait()
     totals = [jnp.zeros((16, width), F32)] * 2 + [jnp.zeros((16, mine), F32)] * 2
     for d in range(dp):
         w_ref[d * depth:(d + 1) * depth, :] = packs[d, :depth, :]
@@ -433,60 +478,74 @@
     g_ffn[...] = totals[1][:8]
     g_q[...] = totals[2][:8]
     g_kv[...] = jnp.where(lanes((8, mine)) % PAIR < HEAD, totals[3][:8], 1.0)
-    for k in [0] + list(range(1, seq)):
+    for k in range(seq):
         if k:
             gather.finish(k)
         x = (x_ref[...] if k == 0 else x_all[k]).astype(F32)
         a = (x * lax.rsqrt(jnp.mean(x * x, axis=-1, keepdims=True) + EPS) * gain).astype(BF16)
-        a_all[k] = a
+        a_s[k] = a
         qkv = nn(a, w_ref[...])
-        at = pl.ds(pl.multiple_of(other(me, k, seq) * rows, rows), rows)
-        q_raw[at, :] = qkv[:, :mine]
-        kv_raw[at, :] = qkv[:, mine:]
-    copies[0].wait()
+        q_s[k] = qkv[:, :mine]
+        kv_s[k] = qkv[:, mine:]
+        for copy in stores(k):
+            copy.start()
     gather.drain()
     pack.drain()
-
-
-def project(x, packed, seq, dp, sizes):
+    for copy in tables:
+        copy.wait()
+    for k in range(seq):
+        for copy in stores(k):
+            copy.wait()
+
+
+def project(x, w_query, w_keyval, gain_rows, segments, seq, dp, sizes):
     rows, width = x.shape
-    wide = packed.shape[1]
+    wide = gain_rows.shape[1]
     mine = wide // 2
-    whole = pl.BlockSpec(memory_space=VMEM)
+    depth = w_query.shape[0]
+    whole, far = pl.BlockSpec(memory_space=VMEM), pl.BlockSpec(memory_space=pl.ANY)
     shape = jax.ShapeDtypeStruct
     dma = pltpu.SemaphoreType.DMA
+    total = seq * rows
     return pl.pallas_call(
         functools.partial(project_kernel, seq, dp, sizes),
         out_shape=(
             shape((seq, rows, width), BF16), shape((seq, rows, width), BF16),
-            shape((seq * rows, mine), F32), shape((seq * rows, mine), F32),
-            shape((width, wide), BF16),
-            shape((8, width), F32), shape((8, width), F32), shape((8, mine), F32), shape((8, mine), F32)),
-        in_specs=[whole] * 2,
-        out_specs=(whole,) * 9,
-        scratch_shapes=[VMEM((dp,) + packed.shape, BF16), Gather.semaphores(seq), Gather.semaphores(seq)]
-        + Spread.semaphores(dp) + [dma((2,))],
+            shape((total, mine), F32), shape((total, mine), F32),
+            shape((total, PAIR), F32), shape((total, PAIR), F32), shape((width, wide), BF16),
+            shape((8, width), F32), shape((8, width), F32), shape((8, mine), F32), shape((8, mine), F32),
+            shape(segments.shape, jnp.int32)),
+        in_specs=[whole, far, far, whole, whole],
+        out_specs=(far,) * 6 + (whole,) * 6,
+        scratch_shapes=[
+            VMEM((seq, rows, width), BF16), VMEM((seq, rows, width), BF16),
+            VMEM((seq, rows, mine), F32), VMEM((seq, rows, mine), F32),
+            VMEM((total, PAIR), F32), VMEM((total, PAIR), F32), VMEM(segments.shape, F32),
+            VMEM((depth + 16, wide), BF16), VMEM((dp, depth + 16, wide), BF16),
+            Gather.semaphores(seq), Gather.semaphores(seq)]
+        + Spread.semaphores(dp) + [dma((4,)), dma((4, seq)), dma((2,))],
         compiler_params=pltpu.CompilerParams(vmem_limit_bytes=LIMIT, collective_id=0, has_side_effects=True),
         name="project",
-    )(x, packed)
-
-
-def ffn_kernel(seq, tile, *refs):
+    )(x, w_query, w_keyval, gain_rows, segments)
+
+
+def ffn_kernel(seq, *refs):
     refs = list(refs)
     o_ref, x_hbm, gain, w_hbm = refs[:4]
     gy_hbm = refs[4:4 + seq]
     rest = refs[4 + seq:]
-    grad_hbm, dx_ref, dy_ref, xy_ref, w_out, o_own = rest[:6]
-    y_hbm = [None] + rest[6:5 + seq]
-    (w, total, o_buf, x_s, gy_s, b_s, y_s, db_s, x1_s, y_out, db_send, db_recv,
-     extra, w_sems, o_send, o_recv, db_out, db_in, in_sems, y_sem, extra_sem) = rest[5 + seq:]
+    grad_hbm, dx_ref, xy_ref, do_ref = rest[:4]
+    y_hbm = [None] + rest[4:3 + seq]
+    (w, w_out, total, o_buf, x_s, gy_s, x1_s, db_s, db_t, y_out, db_send, db_recv, held, extra,
+     w_sems, o_send, o_recv, db_out, db_in, do_out, do_in, in_sems, y_sem, extra_sem) = rest[3 + seq:]
     me = lax.axis_index("seq")
     pieces, _, width = w_hbm.shape
     depth = width // pieces
     part = (w_hbm.shape[1] - depth) // 3
-    hidden = pieces * part
     rows = dx_ref.shape[0]
+    half = rows // 2
     cols = o_ref.shape[1]
+    relay = seq == 4
 
     def load_w(k, d):
         source = w_hbm.at[d, pl.ds(k * part, depth if k == 3 else part), :]
@@ -494,38 +553,57 @@
         return pltpu.make_async_copy(source, target, w_sems.at[k, d])
 
     def store_w(k, d):
+        source = w_out.at[pl.ds(d * depth, depth), :] if k == 3 else w.at[k, pl.ds(d * part, part), :]
         return pltpu.make_async_copy(
-            w.at[k, pl.ds(d * part, part), :], grad_hbm.at[d, pl.ds(k * part, part), :], w_sems.at[k, d])
+            source, grad_hbm.at[d, pl.ds(k * part, depth if k == 3 else part), :], w_sems.at[k, d])
 
     def store_extra(d):
-        return pltpu.make_async_copy(extra, grad_hbm.at[d, pl.ds(3 * part, 16), :], extra_sem.at[d])
-
-    def chunk_of(k):
-        return pl.ds(pl.multiple_of(other(me, k, seq) * rows, rows), rows)
-
-    def load_x(k, slot):
-        return pltpu.make_async_copy(x_hbm.at[k], x_s.at[slot], in_sems.at[0, slot])
-
-    def load_gy(k, slot):
-        return pltpu.make_async_copy(gy_hbm[k], gy_s.at[slot], in_sems.at[1, slot])
-
-    def start_inputs(k, slot):
-        load_x(k, slot).start()
+        return pltpu.make_async_copy(extra, grad_hbm.at[d, pl.ds(3 * part + depth, 16), :], extra_sem.at[d])
+
+    def rows_of(device, h):
+        return pl.ds(pl.multiple_of(device * rows + h * half, half), half)
+
+    def half_at(h):
+        return pl.ds(pl.multiple_of(h * half, half), half)
+
+    def load_x(k, h):
+        return pltpu.make_async_copy(x_hbm.at[k, half_at(h), :], x_s.at[h], in_sems.at[0, h])
+
+    def load_gy(k, h):
+        return pltpu.make_async_copy(gy_hbm[k].at[half_at(h), :], gy_s.at[h], in_sems.at[1, h])
+
+    def start_inputs(k, h):
+        load_x(k, h).start()
         for one in range(seq):
             @pl.when(k == one)
             def _():
-                load_gy(one, slot).start()
-
-    def store_y(k):
-        return pltpu.make_async_copy(y_out, y_hbm[k], y_sem)
-
-    def send_o(k, j):
+                load_gy(one, h).start()
+
+    def store_y(k, h):
+        return pltpu.make_async_copy(y_out, y_hbm[k].at[half_at(h), :], y_sem)
+
+    def send_o(k, h, j):
         peer = other(me, j, seq)
-        at = pl.ds(pl.multiple_of(other(peer, k, seq) * rows, rows), rows)
-        return send(o_ref.at[at, :], o_buf.at[k, j - 1], (o_send, o_recv), (k, j - 1), peer)
-
-    def send_db(k):
-        return send(db_send.at[k - 1], db_recv.at[k - 1], (db_out, db_in), k - 1, other(me, k, seq))
+        return send(o_ref.at[rows_of(other(peer, k, seq), h), :], o_buf.at[k, h, j - 1],
+                    (o_send, o_recv), (k, h, j - 1), peer)
+
+    def pass_o(k, h, j, target, peer):
+        return send(o_buf.at[k, h, j - 1], o_buf.at[target, h, 2], (o_send, o_recv), (target, h, 2),
+                    other(me, peer, seq))
+
+    def starts_o(k):
+        for h in range(2):
+            for j in reversed(range(1, seq)):
+                if not relay or j < 3:
+                    send_o(k, h, j).start()
+                elif not isinstance(k, int):
+                    pass
+                elif k == 3:
+                    send_o(k, h, j).start()
+
+    def send_db(k, h, peer):
+        return send(db_send.at[k - 1, half_at(h), :], db_recv.at[k - 1, half_at(h), :], (db_out, db_in), (k - 1, h),
+                    other(me, peer, seq))
 
     def out_rows(j):
         return pl.ds(pl.multiple_of(other(me, j, seq) * cols, cols), cols)
@@ -535,84 +613,108 @@
             load_w(k, d).start()
     start_inputs(seq - 1, 0)
     greet(seq, me)
-    for k in reversed(range(seq)):
-        for j in reversed(range(1, seq)):
-            send_o(k, j).start()
+    starts_o(seq - 1)
+    if seq > 1:
+        starts_o(seq - 2)
     total[...] = jnp.zeros_like(total)
     for k in range(4):
         for d in range(pieces):
             load_w(k, d).wait()
 
-    def one_chunk(i, _):
-        k = seq - 1 - i
-        slot = i % 2
-        load_x(0, slot).wait()
-        load_gy(0, slot).wait()
+    def one_part(i, _):
+        k = seq - 1 - i // 2
+        h = i % 2
+        load_x(0, h).wait()
+        load_gy(0, h).wait()
+
+        @pl.when(i < 2 * seq - 1)
+        def _():
+            start_inputs(seq - 1 - (i + 1) // 2, 1 - h)
+
+        for j in range(1, seq):
+            send_o(k, h, j).wait_recv()
+        if relay:
+            @pl.when(k == 3)
+            def _():
+                pass_o(3, h, 2, 2, 1).start()
+                pass_o(3, h, 1, 1, 2).start()
+
+            @pl.when((k == 2) & (h == 0))
+            def _():
+                pass_o(2, 0, 1, 0, 2).start()
+
+            @pl.when((k == 1) & (h == 1))
+            def _():
+                pass_o(1, 1, 2, 0, 1).start()
+
+        x1 = x_s[h].astype(F32) + nn(o_ref[rows_of(other(me, k, seq), h), :], w_out[out_rows(0), :])
+        for j in range(1, seq):
+            x1 = x1 + nn(o_buf[k, h, j - 1], w_out[out_rows(j), :])
+        x1_s[half_at(h), :] = x1
+        scale = lax.rsqrt(jnp.mean(x1 * x1, axis=-1, keepdims=True) + EPS)
+        b = (x1 * scale * gain[0:1, :]).astype(BF16)
+        gy = gy_s[h]
+        gate = nt(b, w[0])
+        up = nt(b, w[1])
+        d_act = nt(gy, w[2])
+        sig = jax.nn.sigmoid(gate)
+        silu = gate * sig
+        act = (silu * up).astype(BF16)
+        d_gate = (d_act * up * sig * (1.0 + gate * (1.0 - sig))).astype(BF16)
+        d_up = (d_act * silu).astype(BF16)
+        total[0] += tn(d_gate, b)
+        total[1] += tn(d_up, b)
+        total[2] += tn(act, gy)
+        db_t[...] = nn(d_gate, w[0]) + nn(d_up, w[1])
+        y = nn(act, w[2])
+
+        @pl.when(k == 0)
+        def _():
+            xy_ref[half_at(h), :] = x1_s[half_at(h), :] + y
+            db_s[half_at(h), :] = db_t[...]
+
+        if relay:
+            for one, when, near in ((2, 0, 1), (1, 1, 2)):
+                @pl.when((k == one) & (h == when))
+                def _():
+                    send_db(3, when, near).wait_recv()
+                    db_t[...] += db_recv[2, when * half:(when + 1) * half, :].astype(F32)
 
         @pl.when(k > 0)
         def _():
-            start_inputs(k - 1, 1 - slot)
-
-        for j in range(1, seq):
-            send_o(k, j).wait_recv()
-        x1 = x_s[slot].astype(F32) + nn(o_ref[chunk_of(k), :], w_out[out_rows(0), :])
-        for j in range(1, seq):
-            x1 = x1 + nn(o_buf[k, j - 1], w_out[out_rows(j), :])
-        x1_s[...] = x1
-        scale = lax.rsqrt(jnp.mean(x1 * x1, axis=-1, keepdims=True) + EPS)
-        b_s[...] = (x1 * scale * gain[0:1, :]).astype(BF16)
-        y_s[...] = jnp.zeros_like(y_s)
-        db_s[...] = jnp.zeros_like(db_s)
-
-        def hidden_tile(t, _):
-            at = pl.ds(pl.multiple_of(t * tile, tile), tile)
-            b, gy = b_s[...], gy_s[slot]
-            gate = nt(b, w[0, at, :])
-            up = nt(b, w[1, at, :])
-            d_act = nt(gy, w[2, at, :])
-            sig = jax.nn.sigmoid(gate)
-            silu = gate * sig
-            act = (silu * up).astype(BF16)
-            d_gate = (d_act * up * sig * (1.0 + gate * (1.0 - sig))).astype(BF16)
-            d_up = (d_act * silu).astype(BF16)
-            total[0, at, :] += tn(d_gate, b)
-            total[1, at, :] += tn(d_up, b)
-            total[2, at, :] += tn(act, gy)
-            y_s[...] += nn(act, w[2, at, :])
-            db_s[...] += nn(d_gate, w[0, at, :]) + nn(d_up, w[1, at, :])
-            return 0
-
-        lax.fori_loop(0, hidden // tile, hidden_tile, 0)
-
-        @pl.when(k > 0)
-        def _():
-            db_send[k - 1] = db_s[...].astype(BF16)
-            send_db(k).start()
-
             @pl.when(i > 0)
             def _():
-                store_y(1).wait()
-
-            y_out[...] = y_s[...].astype(BF16)
+                store_y(1, 0).wait()
+
+            y_out[...] = y.astype(BF16)
+            db_send[k - 1, half_at(h), :] = db_t[...].astype(BF16)
             for one in range(1, seq):
                 @pl.when(k == one)
                 def _():
-                    store_y(one).start()
+                    store_y(one, h).start()
+                    if not relay or one < 3:
+                        send_db(one, h, one).start()
+            if relay:
+                @pl.when(i == 0)
+                def _():
+                    send_db(3, 0, 1).start()
+
+                @pl.when(i == 1)
+                def _():
+                    send_db(3, 1, 2).start()
+
+        for one in range(2, seq):
+            @pl.when((k == one) & (h == 1))
+            def _():
+                starts_o(one - 2)
 
         return 0
 
-    lax.fori_loop(0, seq, one_chunk, 0)
-    for k in range(3):
-        w[k] = total[k].astype(BF16)
-        for d in range(pieces):
-            store_w(k, d).start()
-    xy_ref[...] = x1_s[...] + y_s[...]
-    o_own[0] = o_ref[chunk_of(0), :]
-    for j in range(1, seq):
-        o_own[j] = o_buf[0, j - 1]
+    lax.fori_loop(0, 2 * seq, one_part, 0)
     db = db_s[...]
-    for k in reversed(range(1, seq)):
-        send_db(k).wait_recv()
+    for k in reversed(range(1, 3 if relay else seq)):
+        for h in range(2):
+            send_db(k, h, k).wait_recv()
         db = db + db_recv[k - 1].astype(F32)
     x1 = x1_s[...]
     factor = lax.rsqrt(jnp.mean(x1 * x1, axis=-1, keepdims=True) + EPS)
@@ -620,21 +722,45 @@
     term = db * unit
     weighted = db * gain[0:1, :]
     back = factor * (weighted - unit * jnp.mean(term * gain[0:1, :], axis=-1, keepdims=True))
-    dx = gy_s[(seq - 1) % 2].astype(F32) + back
+    dx = jnp.concatenate([gy_s[0], gy_s[1]], axis=0).astype(F32) + back
     dx_ref[...] = dx
-    dy_ref[...] = dx.astype(BF16)
+    dy = dx.astype(BF16)
+
+    def send_do(j):
+        mine = pl.ds(pl.multiple_of(me * rows, rows), rows)
+        return send(held.at[j - 1], do_ref.at[mine, :], (do_out, do_in), j - 1, other(me, j, seq))
+
+    for j in reversed(range(1, seq)):
+        held[j - 1] = nt(dy, w_out[out_rows(j), :]).astype(BF16)
+        send_do(j).start()
+    do_ref[pl.ds(pl.multiple_of(me * rows, rows), rows), :] = nt(dy, w_out[out_rows(0), :]).astype(BF16)
     extra[...] = jnp.broadcast_to(jnp.sum(term, axis=0, keepdims=True), (16, width)).astype(BF16)
+    for j in range(seq):
+        grad = 0.0
+        for h in range(2):
+            o = o_ref[rows_of(me, h), :] if j == 0 else o_buf[0, h, j - 1]
+            grad = grad + tn(o, dy[h * half:(h + 1) * half])
+        w_out[out_rows(j), :] = grad.astype(BF16)
     for d in range(pieces):
         store_extra(d).start()
+        store_w(3, d).start()
+    for k in range(3):
+        w[k] = total[k].astype(BF16)
+        for d in range(pieces):
+            store_w(k, d).start()
+    for j in range(1, seq):
+        send_do(j).wait_send()
+        send_do(j).wait_recv()
+        for k in range(seq):
+            for h in range(2):
+                send_o(k, h, j).wait_send()
     for k in range(1, seq):
-        send_db(k).wait_send()
-    store_y(1).wait()
-    for k in range(seq):
-        for j in range(1, seq):
-            send_o(k, j).wait_send()
+        for h in range(2):
+            send_db(k, h, k).wait_send()
+    store_y(1, 0).wait()
     for d in range(pieces):
         store_extra(d).wait()
-        for k in range(3):
+        for k in range(4):
             store_w(k, d).wait()
 
 
@@ -643,79 +769,41 @@
     all_rows, cols = o.shape
     rows, width = gy[0].shape
     pieces = w.shape[0]
-    part = (w.shape[1] - width // pieces) // 3
+    depth = width // pieces
+    part = (w.shape[1] - depth) // 3
     hidden = pieces * part
-    tile = next(t for t in (384, 288, 256, 192, 128, 64, hidden) if hidden % t == 0)
+    half = rows // 2
     whole, far = pl.BlockSpec(memory_space=VMEM), pl.BlockSpec(memory_space=pl.ANY)
-    wide, narrow = jax.ShapeDtypeStruct((rows, width), F32), jax.ShapeDtypeStruct((rows, width), BF16)
+    shape = jax.ShapeDtypeStruct
     dma = pltpu.SemaphoreType.DMA
     return pl.pallas_call(
-        functools.partial(ffn_kernel, seq, tile),
-        out_shape=(jax.ShapeDtypeStruct((pieces, 3 * part + 16, width), BF16), wide, narrow, wide,
-                   jax.ShapeDtypeStruct((width, width), BF16),
-                   jax.ShapeDtypeStruct((seq, rows, cols), BF16)) + (narrow,) * (seq - 1),
+        functools.partial(ffn_kernel, seq),
+        out_shape=(shape((pieces, 3 * part + depth + 16, width), BF16), shape((rows, width), F32),
+                   shape((rows, width), F32), shape((all_rows, cols), BF16))
+        + (shape((rows, width), BF16),) * (seq - 1),
         in_specs=[whole, far, whole, far] + [far] * seq,
-        out_specs=(far,) + (whole,) * 5 + (far,) * (seq - 1),
+        out_specs=(far,) + (whole,) * 3 + (far,) * (seq - 1),
         scratch_shapes=[
             VMEM((3, hidden, width), BF16),
+            VMEM((width, width), BF16),
             VMEM((3, hidden, width), F32),
-            VMEM((seq, seq - 1, rows, cols), BF16),
-            VMEM((2, rows, width), BF16),
-            VMEM((2, rows, width), BF16),
-            VMEM((rows, width), BF16),
+            VMEM((seq, 2, seq - 1, half, cols), BF16),
+            VMEM((2, half, width), BF16),
+            VMEM((2, half, width), BF16),
             VMEM((rows, width), F32),
             VMEM((rows, width), F32),
-            VMEM((rows, width), F32),
-            VMEM((rows, width), BF16),
+            VMEM((half, width), F32),
+            VMEM((half, width), BF16),
             VMEM((seq - 1, rows, width), BF16),
             VMEM((seq - 1, rows, width), BF16),
+            VMEM((seq - 1, rows, cols), BF16),
             VMEM((16, width), BF16),
-            dma((4, pieces)), dma((seq, seq - 1)), dma((seq, seq - 1)), dma((seq - 1,)), dma((seq - 1,)),
-            dma((2, 2)), dma(()), dma((pieces,)),
+            dma((4, pieces)), dma((seq, 2, seq - 1)), dma((seq, 2, seq - 1)), dma((seq - 1, 2)), dma((seq - 1, 2)),
+            dma((seq - 1,)), dma((seq - 1,)), dma((2, 2)), dma(()), dma((pieces,)),
         ],
         compiler_params=pltpu.CompilerParams(vmem_limit_bytes=LIMIT, collective_id=1, has_side_effects=True),
         name="ffn",
     )(o, x, gain, w, *gy)
-
-
-def out_back_kernel(seq, dy_ref, w_out, o_own, do_ref, grad_ref, held, send_sem, recv_sem):
-    me = lax.axis_index("seq")
-    rows, cols = held.shape[1:]
-    mine = pl.ds(pl.multiple_of(me * rows, rows), rows)
-
-    def out_rows(j):
-        return pl.ds(pl.multiple_of(other(me, j, seq) * cols, cols), cols)
-
-    def send_do(j):
-        return send(held.at[j - 1], do_ref.at[mine, :], (send_sem, recv_sem), j - 1, other(me, j, seq))
-
-    greet(seq, me)
-    dy = dy_ref[...]
-    for j in reversed(range(1, seq)):
-        held[j - 1] = nt(dy, w_out[out_rows(j), :]).astype(BF16)
-        send_do(j).start()
-    do_ref[mine, :] = nt(dy, w_out[out_rows(0), :]).astype(BF16)
-    for j in range(seq):
-        grad_ref[out_rows(j), :] = tn(o_own[j], dy).astype(BF16)
-    for j in range(1, seq):
-        send_do(j).wait_send()
-        send_do(j).wait_recv()
-
-
-def out_back(dy, w_out, o_own):
-    seq, rows, cols = o_own.shape
-    width = dy.shape[1]
-    whole = pl.BlockSpec(memory_space=VMEM)
-    dma = pltpu.SemaphoreType.DMA
-    return pl.pallas_call(
-        functools.partial(out_back_kernel, seq),
-        out_shape=(jax.ShapeDtypeStruct((seq * rows, cols), BF16), jax.ShapeDtypeStruct((width, width), BF16)),
-        in_specs=[whole] * 3,
-        out_specs=(whole,) * 2,
-        scratch_shapes=[VMEM((seq - 1, rows, cols), BF16), dma((seq - 1,)), dma((seq - 1,))],
-        compiler_params=pltpu.CompilerParams(vmem_limit_bytes=LIMIT, collective_id=2, has_side_effects=True),
-        name="out_back",
-    )(dy, w_out, o_own)
 
 
 class Reduce:
@@ -768,19 +856,23 @@
 
 def project_back_kernel(seq, dp, *refs):
     refs = list(refs)
-    dq, dkv, gains, a_all, w, grad_out, x_ref, dx_ref, g_attn, xy_ref = refs[:10]
-    y_parts = refs[10:9 + seq]
-    (grad_x, out_ref, gwq_ref, gwkv_ref, gwo_ref, gain_out, acc, da, arrived, pieces, results, sums, sum_in,
-     q_near, q_out, q_far, o_near, o_out, o_far, rs_out, rs_in, q1, q2, q3, q4, o1, o2, o3, o4,
-     all_out, all_in) = refs[9 + seq:]
+    dq, dkv, gains, w, g_attn, a_hbm, x_hbm, dx_hbm, xy_hbm = refs[:9]
+    y_hbm = refs[9:8 + seq]
+    (grad_x, out_ref, gwq_ref, gwkv_ref, gain_out, a_all, x_s, dx_s, xy_s, y_s, acc, da, arrived, pieces, results,
+     q_near, q_out, q_far, rs_out, rs_in, q1, q2, q3, q4, all_out, all_in, in_sems) = refs[8 + seq:]
     me, here = lax.axis_index("seq"), lax.axis_index("dp")
-    rows, width = x_ref.shape
+    rows, width = x_s.shape
     mine = dq.shape[1]
-    depth = grad_out.shape[1]
+    depth = width // dp
     half = rows // 2
     orders = flips(seq)
     red_q = Reduce(here, dp, pieces, q_near, q_out, q_far, (q1, q2, q3, q4))
-    red_o = Reduce(here, dp, grad_out, o_near, o_out, o_far, (o1, o2, o3, o4))
+    loads = [pltpu.make_async_copy(a_hbm, a_all, in_sems.at[0]), pltpu.make_async_copy(xy_hbm, xy_s, in_sems.at[1])]
+    loads += [pltpu.make_async_copy(y_hbm[k], y_s.at[k], in_sems.at[2 + k]) for k in range(seq - 1)]
+    loads += [pltpu.make_async_copy(x_hbm, x_s, in_sems.at[1 + seq]),
+              pltpu.make_async_copy(dx_hbm, dx_s, in_sems.at[2 + seq])]
+    for load in loads:
+        load.start()
 
     def chunk(k):
         return pl.ds(pl.multiple_of(other(me, k, seq) * rows, rows), rows)
@@ -794,22 +886,18 @@
         return [k for k in range(1, seq) if k & orders[part][step] and not k & before]
 
     def to_all(j):
-        peer = other(me, j, seq)
-        return [send(results.at[me], results.at[me], (all_out, all_in), (0, j - 1), peer),
-                send(sums, sum_in.at[j - 1], (all_out, all_in), (1, j - 1), peer)]
+        return send(results.at[me], results.at[me], (all_out, all_in), j - 1, other(me, j, seq))
 
     def partial_da(k):
         return nt(dq[chunk(k), :], w[:, :mine]) + nt(dkv[chunk(k), :], w[:, mine:])
 
     greet(seq, me, dp, here)
-    red_o.begin()
     for k in reversed(range(1, seq)):
         acc[k] = partial_da(k).astype(BF16)
         for part in range(2):
             if k in sent_at(part, 0):
                 pass_on(part, 0, k).start()
-    da[...] = partial_da(0)
-    red_o.middle()
+    loads[0].wait()
     for d in range(2):
         grads = dq if d == 0 else dkv
         total = tn(a_all[0], grads[chunk(0), :])
@@ -819,11 +907,14 @@
         sum8 = jnp.sum(gains[8 * d:8 * d + 8, :], axis=0, keepdims=True)
         pieces[:, depth:, d * mine:(d + 1) * mine] = jnp.broadcast_to(sum8[None], (dp, 16, mine)).astype(BF16)
     red_q.begin()
-    out = xy_ref[...]
-    for y in y_parts:
-        out = out + y[...].astype(F32)
+    da[...] = partial_da(0)
+    red_q.middle()
+    for load in loads[1:]:
+        load.wait()
+    out = xy_s[...]
+    for k in range(seq - 1):
+        out = out + y_s[k].astype(F32)
     out_ref[...] = out.astype(BF16)
-    red_q.middle()
     for step in range(len(orders[0])):
         for part in range(2):
             at = pl.ds(part * half, half)
@@ -838,23 +929,16 @@
                 for k in sent_at(part, step + 1):
                     pass_on(part, step + 1, k).start()
         if step == 0:
-            sum_o = red_o.finish()
-            sums[...] = sum_o.astype(BF16)
             results[me] = red_q.finish().astype(BF16)
             for j in reversed(range(1, seq)):
-                for copy in to_all(j):
-                    copy.start()
-    x = x_ref[...].astype(F32)
+                to_all(j).start()
+    x = x_s[...].astype(F32)
     factor = lax.rsqrt(jnp.mean(x * x, axis=-1, keepdims=True) + EPS)
     unit = x * factor
     weighted = da[...] * g_attn[0:1, :]
-    grad_x[...] = dx_ref[...] + factor * (weighted - unit * jnp.mean(weighted * unit, axis=-1, keepdims=True))
-    gwo = sums[...].astype(F32)
+    grad_x[...] = dx_s[...] + factor * (weighted - unit * jnp.mean(weighted * unit, axis=-1, keepdims=True))
     for j in range(1, seq):
-        for copy in to_all(j):
-            copy.wait_recv()
-        gwo = gwo + sum_in[j - 1].astype(F32)
-    gwo_ref[...] = gwo
+        to_all(j).wait_recv()
     gain_total = jnp.zeros((16, 2 * mine), F32)
     for j in range(seq):
         gwq_ref[:, j * mine:(j + 1) * mine] = results[j, :depth, :mine].astype(F32)
@@ -862,54 +946,57 @@
         gain_total = gain_total + results[j, depth:, :].astype(F32)
     gain_out[...] = gain_total
     for j in range(1, seq):
-        for copy in to_all(j):
-            copy.wait_send()
+        to_all(j).wait_send()
     for part in range(2):
         for step in range(len(orders[0])):
             for k in sent_at(part, step):
                 pass_on(part, step, k).wait_send()
     red_q.drain()
-    red_o.drain()
-
-
-def project_back(dq, dkv, gains, a_all, w_qkv, grad_out, x, dx, g_attn, xy, y_parts):
+
+
+def project_back(dq, dkv, gains, a_all, w_qkv, dp, x, dx, g_attn, xy, y_parts):
     seq, rows, width = a_all.shape
-    dp, depth, _ = grad_out.shape
+    depth = width // dp
     mine = dq.shape[1]
-    whole = pl.BlockSpec(memory_space=VMEM)
+    whole, far = pl.BlockSpec(memory_space=VMEM), pl.BlockSpec(memory_space=pl.ANY)
     shape = jax.ShapeDtypeStruct
     dma = pltpu.SemaphoreType.DMA
     steps = seq.bit_length() - 1
     return pl.pallas_call(
         functools.partial(project_back_kernel, seq, dp),
         out_shape=(shape((rows, width), F32), shape((rows, width), BF16), shape((depth, seq * mine), F32),
-                   shape((depth, seq * mine), F32), shape((depth, width), F32), shape((16, 2 * mine), F32)),
-        in_specs=[whole] * (9 + seq),
-        out_specs=(whole,) * 6,
+                   shape((depth, seq * mine), F32), shape((16, 2 * mine), F32)),
+        in_specs=[whole] * 5 + [far] * (3 + seq),
+        out_specs=(whole,) * 5,
         scratch_shapes=[
+            VMEM((seq, rows, width), BF16),
+            VMEM((rows, width), BF16),
+            VMEM((rows, width), F32),
+            VMEM((rows, width), F32),
+            VMEM((seq - 1, rows, width), BF16),
             VMEM((seq, rows, width), BF16),
             VMEM((rows, width), F32),
             VMEM((2, seq - 1, rows // 2, width), BF16),
             VMEM((dp, depth + 16, 2 * mine), BF16),
             VMEM((seq, depth + 16, 2 * mine), BF16),
-            VMEM((depth, width), BF16),
-            VMEM((seq - 1, depth, width), BF16),
-            *Reduce.scratch(dp, depth + 16, 2 * mine), *Reduce.scratch(dp, depth, width),
+            *Reduce.scratch(dp, depth + 16, 2 * mine),
             dma((2, steps, seq)), dma((2, steps, seq)),
-            *Reduce.semaphores(dp), *Reduce.semaphores(dp), dma((2, seq - 1)), dma((2, seq - 1)),
+            *Reduce.semaphores(dp), dma((seq - 1,)), dma((seq - 1,)), dma((3 + seq,)),
         ],
         compiler_params=pltpu.CompilerParams(vmem_limit_bytes=LIMIT, collective_id=3, has_side_effects=True),
         name="project_back",
-    )(dq, dkv, gains, a_all, w_qkv, grad_out, x, dx, g_attn, xy, *y_parts)
-
-
-def share_kernel(seq, own, grads_ref, extra_ref, slots, send_sem, recv_sem):
+    )(dq, dkv, gains, w_qkv, g_attn, a_all, x, dx, xy, *y_parts)
+
+
+def share_kernel(seq, own, grads_ref, out_ref, extra_ref, slots, send_sem, recv_sem):
     me = lax.axis_index("seq")
     gather = Gather(me, seq, own, slots, (send_sem, recv_sem))
     part = grads_ref.shape[2]
+    depth = out_ref.shape[0]
     greet(seq, me)
     gather.begin()
-    extra = own[3 * part:, :].astype(F32)
+    out_ref[...] = own[3 * part:3 * part + depth, :].astype(F32)
+    extra_ref[...] = own[3 * part + depth:, :].astype(F32)
     for k in range(3):
         grads_ref[k, me] = own[k * part:(k + 1) * part, :].astype(F32)
     gather.forward()
@@ -917,21 +1004,21 @@
         gather.finish(j)
         for k in range(3):
             grads_ref[k, other(me, j, seq)] = slots[j, k * part:(k + 1) * part, :].astype(F32)
-        extra = extra + slots[j, 3 * part:, :].astype(F32)
-    extra_ref[...] = extra
+        out_ref[...] += slots[j, 3 * part:3 * part + depth, :].astype(F32)
+        extra_ref[...] += slots[j, 3 * part + depth:, :].astype(F32)
     gather.drain()
 
 
-def share(own, seq, part):
+def share(own, seq, part, depth):
     rows, width = own.shape
-    spare = rows - 3 * part
     whole = pl.BlockSpec(memory_space=VMEM)
     shape = jax.ShapeDtypeStruct
     return pl.pallas_call(
         functools.partial(share_kernel, seq),
-        out_shape=(shape((3, seq, part, width), F32), shape((spare, width), F32)),
+        out_shape=(shape((3, seq, part, width), F32), shape((depth, width), F32),
+                   shape((rows - 3 * part - depth, width), F32)),
         in_specs=[whole],
-        out_specs=(whole,) * 2,
+        out_specs=(whole,) * 3,
         scratch_shapes=[VMEM((seq, rows, width), BF16), Gather.semaphores(seq), Gather.semaphores(seq)],
         compiler_params=pltpu.CompilerParams(vmem_limit_bytes=LIMIT, collective_id=4, has_side_effects=True),
         name="share",
@@ -942,21 +1029,11 @@
     return lax.ppermute(u, "seq", [(i, i ^ bits) for i in range(seq)])
 
 
-def place_tables(segment_row, order_row):
-    length = segment_row.shape[0]
-    docs = jnp.arange(1, MOST_DOCS, dtype=jnp.int32)
-    begins = jnp.sum(segment_row[None, :] < docs[:, None], axis=1, dtype=jnp.int32)
-    starts = jnp.max(jnp.where(segment_row[None, :] >= docs[:, None], begins[:, None], 0), axis=0)
+def packed_order(order_row, starts):
     blocks = order_row.shape[0]
     ids = jnp.arange(blocks, dtype=jnp.int32)
     inv = jnp.sum(jnp.where(order_row[None, :] == ids[:, None], ids[None, :], 0), axis=1, dtype=jnp.int32)
-    first = starts.reshape(blocks, BLOCK)[:, 0] // BLOCK
-    lane = jnp.arange(PAIR, dtype=jnp.int32)
-    frequency = jnp.exp((lane % (HEAD // 2)).astype(F32) * (-2.0 * math.log(THETA) / HEAD))
-    offset = (jnp.arange(length, dtype=jnp.int32) - starts).astype(F32)
-    turned = offset[:, None] * frequency[None, :]
-    sign = jnp.where(lane % HEAD < HEAD // 2, -1.0, 1.0)
-    return inv, first, starts, jnp.cos(turned), jnp.sin(turned) * sign[None, :]
+    return inv, starts[:, 0] // BLOCK
 
 
 def shards(tokens_in, norm_attn, w_query, w_keyval, gain_query, gain_key, w_out, norm_ffn,
@@ -969,13 +1046,9 @@
     depth = w_query.shape[0]
     part = w_down.shape[0] // seq
 
-    def my_columns(u):
-        return lax.dynamic_slice_in_dim(u, me * mine, mine, 1)
-
     gain_row = jnp.concatenate([norm_attn, norm_ffn, gain_query, gain_key])
     sizes = (norm_attn.shape[0], norm_ffn.shape[0], gain_query.shape[0], gain_key.shape[0])
     gain_rows = jnp.pad(gain_row[None, :], ((0, 15), (0, 2 * mine - gain_row.shape[0])))
-    packed = jnp.concatenate([jnp.concatenate([my_columns(w_query), my_columns(w_keyval)], 1), gain_rows], 0)
     def my_rows(u):
         return lax.dynamic_slice_in_dim(u, me * part, part, 0)
 
@@ -986,32 +1059,28 @@
         body = jnp.moveaxis(ffn_w[:, :3 * part].reshape(dp, 3, part, width), 0, 1)
         ffn_w = jnp.concatenate([body.reshape(-1, width), ffn_w[:, 3 * part:].reshape(-1, width)])[None]
 
-    inv, first, starts, cos, sin = place_tables(segments[0], blocks[0])
-    starts_down = jnp.broadcast_to(starts[:, None], (total_rows, BLOCK))
-    starts_across = jnp.broadcast_to(starts.reshape(-1, 1, BLOCK), (total_rows // BLOCK, 8, BLOCK))
-    x_all, a_all, q_raw, kv_raw, w_qkv, g_attn, g_ffn, gain_q, gain_kv = project(
-        tokens_in, packed, seq, dp, sizes)
+    (x_all, a_all, q_raw, kv_raw, cos, sin, w_qkv, g_attn, g_ffn, gain_q, gain_kv, starts) = project(
+        tokens_in, w_query, w_keyval, gain_rows, segments.reshape(-1, BLOCK), seq, dp, sizes)
+    inv, first = packed_order(blocks[0], starts)
     gy, q_raw = lax.optimization_barrier((cotangent, q_raw))
     gy_all = [gy] + [exchanged(gy, k, seq) for k in range(1, seq)]
-    o, qs, kvs, linv = attend(inv, first, q_raw, kv_raw, cos, sin, starts_down, gain_q, gain_kv)
-
-    ffn_grads, d_x1, d_y, x1_y, out_w, o_own, *y_parts = ffn(o, x_all, gy_all, g_ffn, ffn_w)
+    o, qs, kvs, linv = attend(inv, first, q_raw, kv_raw, cos, sin, starts, gain_q, gain_kv)
+
+    ffn_grads, d_x1, x1_y, d_o, *y_parts = ffn(o, x_all, gy_all, g_ffn, ffn_w)
     if not in_pieces:
+        body = jnp.moveaxis(ffn_grads[0, :3 * dp * part].reshape(3, dp, part, width), 1, 0)
+        out = ffn_grads[0, 3 * dp * part:-16].reshape(dp, depth, width)
         extra = jnp.broadcast_to(ffn_grads[0, None, -16:], (dp, 16, width))
-        body = jnp.moveaxis(ffn_grads[0, :-16].reshape(3, dp, part, width), 1, 0)
-        ffn_grads = jnp.concatenate([body.reshape(dp, 3 * part, width), extra], 1)
+        ffn_grads = jnp.concatenate([body.reshape(dp, 3 * part, width), out, extra], 1)
         ffn_grads = jnp.pad(ffn_grads, ((0, 0), (0, -ffn_grads.shape[1] % 32), (0, 0)))
     ffn_grads = lax.psum_scatter(ffn_grads, "dp", scatter_dimension=0, tiled=True)[0]
 
-    d_o, grad_out = out_back(d_y, out_w, o_own)
-    d_o, y_parts = lax.optimization_barrier((d_o, y_parts))
     y_parts = [exchanged(y_parts[k - 1], k, seq) for k in range(1, seq)]
     dq_raw, dkv_raw, gain_sums = attend_back(
-        inv, first, q_raw, kv_raw, cos, sin, starts_across, gain_q, gain_kv, o, d_o, qs, kvs, linv)
-    grad_tokens, output, grad_wq, grad_wkv, grad_wout, gain_sums = project_back(
-        dq_raw, dkv_raw, gain_sums, a_all, w_qkv, grad_out.reshape(dp, depth, width), tokens_in, d_x1, g_attn,
-        x1_y, y_parts)
-    ffn_grads, extra = share(ffn_grads, seq, part)
+        inv, first, q_raw, kv_raw, cos, sin, starts, gain_q, gain_kv, o, d_o, qs, kvs, linv)
+    grad_tokens, output, grad_wq, grad_wkv, gain_sums = project_back(
+        dq_raw, dkv_raw, gain_sums, a_all, w_qkv, dp, tokens_in, d_x1, g_attn, x1_y, y_parts)
+    ffn_grads, grad_wout, extra = share(ffn_grads, seq, part, depth)
     ffn_grads = ffn_grads.reshape(3, seq * part, width)
 
     here = lax.axis_index("dp")

time: 409 us -> 386 us (0.944)
  Pallas kernels: 350 us -> 319 us
  waiting for transfers between devices: 4.84 us -> 22.2 us
  other arithmetic: 11.8 us -> 5.28 us
    pallas_call x1, Pallas kernels: 68.7 us -> 47.9 us  [project_back(): pl.pallas_call(functools.partial(project_back_kernel, seq, dp), out_shape...]
    pallas_call x2 -> x1, Pallas kernels: 120 us -> 105 us  [ffn(): pl.pallas_call(functools.partial(ffn_kernel, seq), out_shape=(shape((piec...]
    reduce_scatter x1, waiting for transfers between devices: 0.01 us -> 8.17 us  [shards(): lax.psum_scatter(ffn_grads, 'dp', scatter_dimension=0, tiled=True)[0]]
    pallas_call x1, Pallas kernels: 36.7 us -> 43.9 us  [share(): pl.pallas_call(functools.partial(share_kernel, seq), out_shape=(shape((3,...]
    ppermute x6, waiting for transfers between devices: 4.6 us -> 11.1 us  [exchanged(): return lax.ppermute(u, 'seq', [(i, i ^ bits) for i in range(seq)])]
    mul x1 -> x0, other arithmetic: 5.53 us -> none  [place_tables(): jnp.sin(turned) * sign[None, :]]
  transfers between devices with their start and end apart: 8 -> 8, of which waited for: 3 -> 4; matrix products, arithmetic and copies ran while one was open for 3% -> 2% of each run, Pallas kernels for 52% -> 44%
where the time goes in v3:
time: 386 us
  Pallas kernels  319 us (83%)
  waiting for transfers between devices  22.2 us (6%)
  local copies, waits for them, and re-layouts  18.1 us (5%)
  between operations  14.2 us (4%)
  starting transfers between devices  7.19 us (2%)
  other arithmetic  5.28 us (1%)
    pallas_call x1, Pallas kernels, ffn(): pl.pallas_call(functools.partial(ffn_kernel, seq), out_shape=(shape((piec...  105 us
    pallas_call x1, Pallas kernels, project_back(): pl.pallas_call(functools.partial(project_back_kernel, seq, dp), out_shape...  47.9 us
    pallas_call x1, Pallas kernels, project(): pl.pallas_call(functools.partial(project_kernel, seq, dp, sizes), out_sha...  45.5 us
    pallas_call x1, Pallas kernels, share(): pl.pallas_call(functools.partial(share_kernel, seq), out_shape=(shape((3,...  43.9 us
    pallas_call x1, Pallas kernels, attend_back(): pl.pallas_call(functools.partial(attend_back_kernel, groups), out_shape=(...  40.9 us
    pallas_call x1, Pallas kernels, attend(): pl.pallas_call(functools.partial(attend_kernel, groups), out_shape=(jax.S...  35.3 us
    ppermute x6, waiting for transfers between devices, exchanged(): return lax.ppermute(u, 'seq', [(i, i ^ bits) for i in range(seq)])  11.1 us
    reduce_scatter x1, waiting for transfers between devices, shards(): lax.psum_scatter(ffn_grads, 'dp', scatter_dimension=0, tiled=True)[0]  8.17 us
  transfers between devices with their start and end apart: 8, of which 4 were waited for; matrix products, arithmetic and copies ran while one was open for 2% of the time, Pallas kernels for 44%

profile of v3, /device:TPU:0, one launch (start us, length us, event | category | flops | bytes accessed | tf_op | source)
XLA Modules:
  0.0 385.7 jit_solution(9419072425437081709)
XLA Ops:
  7.2 1.0 constant_dynamic-slice_fusion.1
  8.3 1.1 dynamic-slice_bitcast_fusion
  9.4 2.0 pad_maximum_fusion
  12.2 45.5 %project.1 = (bf16[4,512,1024]{2,1,0:T(8,128)(2,1)}, bf16[4,512,1024]{2,1,0:T(8,128)(2,1)}, f32[2048,256]{1,0:T(8,128)}, f32[2048,256]{1,0:T(8,128)}, f32[2048,1...) custom-call(bf16[512,1024]{1,0:T(8,128)(2,1)} %refs_6_.1, ...), custom_call_target="tpu_custom_call" | custom-call | tf_op jit(solution)/shard_map/project/pallas_call | solution.py:510
  57.8 1.6 collective-permute-start
  59.8 1.5 collective-permute-start.2
  61.9 0.8 slice_reduce_fusion
  63.3 35.3 %attend.1 = (bf16[2048,256]{1,0:T(8,128)(2,1)}, bf16[2,4096,128]{2,1,0:T(8,128)(2,1)}, bf16[2,2176,128]{2,1,0:T(8,128)(2,1)}, f32[2,16,8,256]{3,2,1,0:T(8,128)}) custom-call(s32[16]{0:T(128)} %select_reduce_fusion.inv, s32[16]{0:T(128)} %and_select_fusion.first, f32[2048,256]{1,0:T(8,128)} %get-tuple-element.50.q_raw, f32[2048,256]{1,0:T(8,128)} %get-tuple-element.51.kv_raw, ...), custom_call_target="tpu_custom_call" | custom-call | tf_op jit(solution)/shard_map/attend/pallas_call | solution.py:142
  98.6 7.3 %collective-permute-done.1.refs_6_ = bf16[512,1024]{1,0:T(8,128)(2,1)} collective-permute-done((bf16[512,1024]{1,0:T(8,128)(2,1)}, bf16[512,1024]{1,0:T(8,128)(2,1)}, u32[]{:S(2)}, u32[]{:S(2)}) %collective-permute-start.1) | collective-permute-done | bytes 1048608 | tf_op jit(solution)/shard_map/ppermute | solution.py:1029
  106.0 2.9 all-gather.3.cloned.1.call-done
  108.8 105.1 %ffn.1 = (bf16[8,576,1024]{2,1,0:T(8,128)(2,1)}, f32[512,1024]{1,0:T(8,128)}, f32[512,1024]{1,0:T(8,128)}, bf16[2048,256]{1,0:T(8,128)(2,1)}, bf16[512,1024]{1,0...) custom-call(bf16[2048,256]{1,0:T(8,128)(2,1)} %get-tuple-element.56.refs_0_.o_ref, ...), custom_call_target="tpu_custom_call" | custom-call | tf_op jit(solution)/shard_map/ffn/pallas_call | solution.py:779
  214.0 1.6 collective-permute-start.3
  216.3 1.3 collective-permute-start.5
  217.5 40.9 %attend_back.1 = (bf16[2048,256]{1,0:T(8,128)(2,1)}, bf16[2048,256]{1,0:T(8,128)(2,1)}, f32[16,256]{1,0:T(8,128)}) custom-call(s32[16]{0:T(128)} %select_reduce_fusion.inv, s32[16]{0:T(128)} %and_select_fusion.first, f32[2048,256]{1,0:T(8,128)} %get-tuple-element.50.q_raw, f32[2048,256]{1,0:T(8,128)} %get-tuple-element.51.kv_raw, ...), custom_call_target="tpu_custom_call" | custom-call | tf_op jit(solution)/shard_map/attend_back/pallas_call | solution.py:259
  258.5 3.7 collective-permute-done.4.refs_10_
  262.2 47.9 %project_back.1 = (f32[512,1024]{1,0:T(8,128)}, bf16[512,1024]{1,0:T(8,128)(2,1)}, f32[128,1024]{1,0:T(8,128)}, f32[128,1024]{1,0:T(8,128)}, f32[16,512]{1,0:T(8,128)}) custom-call(bf16[2048,256]{1,0:T(8,128)(2,1)} %get-tuple-element.64.refs_0_, bf16[2048,256]{1,0:T(8,128)(2,1)} %get-tuple-element.65.refs_1_, f32[16,256]{1,0:T(8,128)} %get-tuple-element.66.refs_2_, ...), custom_call_target="tpu_custom_call" | custom-call | tf_op jit(solution)/shard_map/project_back/pallas_call | solution.py:965
  312.1 1.5 add_reduce_fusion
  314.1 8.2 %reduce-scatter.2.cloned.1.call-done = bf16[1,576,1024]{2,1,0:T(8,128)(2,1)} async-done(((bf16[8,576,1024]{2,1,0:T(8,128)(2,1)}), bf16[1,576,1024]{2,1,0:T(8,128)(2,1)}) %reduce-scatter.2.cloned.1.call-update) | async-done | bytes 1179664 | tf_op jit(solution)/shard_map/reduce_scatter | solution.py:1076
  322.3 43.9 %share.1 = (f32[3,4,144,1024]{3,2,1,0:T(8,128)}, f32[128,1024]{1,0:T(8,128)}, f32[16,1024]{1,0:T(8,128)}) custom-call(bf16[576,1024]{1,0:T(8,128)(2,1)} %bitcast.22), custom_call_target="tpu_custom_call" | custom-call | tf_op jit(solution)/shard_map/share/pallas_call | solution.py:1016
  366.2 6.4 %fusion.1 = (f32[1,4,144,1024]{3,2,1,0:T(8,128)}, f32[1,4,144,1024]{3,2,1,0:T(8,128)}, f32[1,4,144,1024]{3,2,1,0:T(8,128)}) fusion(f32[3,4,144,1024]{3,2,1,0:T(8,128)} %get-tuple-element.83), kind=kLoop, calls=%fused_computation.18 | loop fusion | bytes 14155776 | tf_op jit(solution)/shard_map/slice | solution.py:1097
  372.7 0.9 slice.31
  374.1 1.0 copy.31
  375.1 1.3 copy.32
  377.2 0.8 copy.34
  (49 shorter events, 7.9 us)
Async XLA Ops:
  7.2 101.7 %all-gather.3.cloned.1.call-start = ((), (), s32[]{:S(2)}) async-start(), calls=%async_computation.2 | async-start | bytes 10321920 | tf_op jit(solution)/shard_map/all_gather | solution.py:1056
  8.2 3.3 copy-start.7
  8.2 3.3 copy-start.8
  8.2 3.3 copy-start.9
  8.3 3.3 copy-start.10
  9.4 51.9 %copy-start.11 = (s32[1,16]{1,0:T(1,128)S(1)}, s32[1,16]{1,0:T(1,128)}, u32[]{:S(2)}) copy-start(s32[1,16]{1,0:T(1,128)} %param.27) | copy-start | bytes 196
  11.4 310.8 %reduce-scatter.2.cloned.1.call-start = ((), (), s32[]{:S(2)}) async-start(), calls=%async_computation.1 | async-start | bytes 10616832 | tf_op jit(solution)/shard_map/reduce_scatter | solution.py:1076
  57.8 40.8 %collective-permute-start = (bf16[512,1024]{1,0:T(8,128)(2,1)}, bf16[512,1024]{1,0:T(8,128)(2,1)}, u32[]{:S(2)}, u32[]{:S(2)}) collective-permute-start(bf16[512,1024]{1,0:T(8,128)(2,1)} %refs_4_), channel_id=1, source_target_pairs={{0,1},{1,0},{2,3},{3,2},{4,5},{5,4},{6,7},{7,6},{8,9},{9,8},{10,11... | collective-permute-start | bytes 3145736 | tf_op jit(solution)/shard_map/ppermute | solution.py:1029
  59.3 46.6 %collective-permute-start.1 = (bf16[512,1024]{1,0:T(8,128)(2,1)}, bf16[512,1024]{1,0:T(8,128)(2,1)}, u32[]{:S(2)}, u32[]{:S(2)}) collective-permute-start(bf16[512,1024]{1,0:T(8,128)(2,1)} %refs_4_), channel_id=1, source_target_pairs={{0,2},{1,3},{2,0},{3,1},{4,6},{5,7},{6,4},{7,5},{8,10},{9,11},{10,... | collective-permute-start | bytes 3145736 | tf_op jit(solution)/shard_map/ppermute | solution.py:1029
  59.8 46.1 %collective-permute-start.2 = (bf16[512,1024]{1,0:T(8,128)(2,1)}, bf16[512,1024]{1,0:T(8,128)(2,1)}, u32[]{:S(2)}, u32[]{:S(2)}) collective-permute-start(bf16[512,1024]{1,0:T(8,128)(2,1)} %refs_4_), channel_id=1, source_target_pairs={{0,3},{1,2},{2,1},{3,0},{4,7},{5,6},{6,5},{7,4},{8,11},{9,10},{10,... | collective-permute-start | bytes 3145736 | tf_op jit(solution)/shard_map/ppermute | solution.py:1029
  214.0 44.5 %collective-permute-start.3 = (bf16[512,1024]{1,0:T(8,128)(2,1)}, bf16[512,1024]{1,0:T(8,128)(2,1)}, u32[]{:S(2)}, u32[]{:S(2)}) collective-permute-start(bf16[512,1024]{1,0:T(8,128)(2,1)} %get-tuple-element.72), channel_id=1, source_target_pairs={{0,1},{1,0},{2,3},{3,2},{4,5},{5,4},{6,7},{7,6},{8,9},{9,8},{10,11... | collective-permute-start | bytes 3145736 | tf_op jit(solution)/shard_map/ppermute | solution.py:1029
  215.6 46.6 %collective-permute-start.4 = (bf16[512,1024]{1,0:T(8,128)(2,1)}, bf16[512,1024]{1,0:T(8,128)(2,1)}, u32[]{:S(2)}, u32[]{:S(2)}) collective-permute-start(bf16[512,1024]{1,0:T(8,128)(2,1)} %get-tuple-element.73), channel_id=1, source_target_pairs={{0,2},{1,3},{2,0},{3,1},{4,6},{5,7},{6,4},{7,5},{8,10},{9,11},{10,... | collective-permute-start | bytes 3145736 | tf_op jit(solution)/shard_map/ppermute | solution.py:1029
  216.3 45.9 %collective-permute-start.5 = (bf16[512,1024]{1,0:T(8,128)(2,1)}, bf16[512,1024]{1,0:T(8,128)(2,1)}, u32[]{:S(2)}, u32[]{:S(2)}) collective-permute-start(bf16[512,1024]{1,0:T(8,128)(2,1)} %get-tuple-element.74), channel_id=1, source_target_pairs={{0,3},{1,2},{2,1},{3,0},{4,7},{5,6},{6,5},{7,4},{8,11},{9,10},{10,... | collective-permute-start | bytes 3145736 | tf_op jit(solution)/shard_map/ppermute | solution.py:1029
  262.2 50.0 %copy-start.4 = (bf16[128,1024]{1,0:T(8,128)(2,1)S(1)}, bf16[128,1024]{1,0:T(8,128)(2,1)}, u32[]{:S(2)}) copy-start(bf16[128,1024]{1,0:T(8,128)(2,1)} %wq_hbm.1) | copy-start | bytes 786436
  262.2 50.0 %copy-start.5 = (bf16[128,1024]{1,0:T(8,128)(2,1)S(1)}, bf16[128,1024]{1,0:T(8,128)(2,1)}, u32[]{:S(2)}) copy-start(bf16[128,1024]{1,0:T(8,128)(2,1)} %wkv_hbm.1) | copy-start | bytes 786436
  366.2 7.9 %copy-start.3 = (bf16[512,1024]{1,0:T(8,128)(2,1)S(1)}, bf16[512,1024]{1,0:T(8,128)(2,1)}, u32[]{:S(2)}) copy-start(bf16[512,1024]{1,0:T(8,128)(2,1)} %get-tuple-element.103) | copy-start | bytes 3145732
  372.7 2.4 copy-start
  375.1 1.4 copy-start.2
  375.1 2.2 copy-start.1
  376.4 1.6 copy-start.6
Sparse Core Ops, SparseCore 0:
  11.6 97.2 all-gather.2
  214.1 108.1 reduce-scatter.1
